TPU v7x, 128 devices: a whole 4x4x4 slice. The times are simulated.
128 devices in a mesh: subtree: 32 (over z, x, core), front: 4 (over y).
Axes of the slice: x: 4, y: 4, z: 4, core: 2. Of those that a mesh axis runs over, the one named last changes fastest.
Arguments:
- right_hand_sides: float32 [64, 851968], P(None, ('subtree', 'front')), may hold values from -6 to 6
- elimination_natural_index: int32 [851968], P(('subtree', 'front')), may hold values from 0 to 851967, as said below
- leaf_diagonal_inverse: bfloat16 [512, 512, 512], P(('subtree', 'front')), may hold values from -1 to 1.5
- leaf_update_block: bfloat16 [512, 512, 256], P(('subtree', 'front')), may hold values from -0.25 to 0.25
- leaf_parent_rows: int32 [512, 256], P(('subtree', 'front')), may hold values from 0 to 1023, as said below
- leaf_parent_node: int32 [512], P(('subtree', 'front')), may hold values from 0 to 255, as said below
- level1_diagonal_inverse: bfloat16 [256, 1024, 1024], P(('subtree', 'front')), may hold values from -1 to 1.5
- level1_update_block: bfloat16 [256, 1024, 512], P(('subtree', 'front')), may hold values from -0.1875 to 0.1875
- level1_parent_rows: int32 [256, 512], P(('subtree', 'front')), may hold values from 0 to 1535, as said below
- level1_parent_node: int32 [256], P(('subtree', 'front')), may hold values from 0 to 127, as said below
- level2_diagonal_inverse: bfloat16 [128, 1536, 1536], P('subtree', None, 'front'), may hold values from -1 to 1.5
- level2_update_block: bfloat16 [128, 1536, 768], P('subtree', 'front'), may hold values from -0.15625 to 0.15625
- level2_parent_rows: int32 [128, 768], P('subtree'), may hold values from 0 to 2047, as said below
- level2_parent_node: int32 [128], P('subtree'), may hold values from 0 to 63, as said below
- level3_diagonal_inverse: bfloat16 [64, 2048, 2048], P('subtree', None, 'front'), may hold values from -1 to 1.5
Outputs:
- solution: float32 [64, 851968], P(None, ('subtree', 'front'))
Inputs may be any that keep to these rules, and one draw needn't show every extreme that they name: `elimination_natural_index`: A permutation of the unknowns; each device's block of 6656 elimination positions takes exactly 6656 / 128 unknowns from each device's block of natural positions. `leaf_parent_node`: the leaf with number (s * 4 + f) * 4 + c has a parent (t * 4 + f) * 2 + q with t equal to s or s xor 1; every level-1 supernode has exactly two children, one from each of the two subtree indices s and s xor 1. `level1_parent_node`: the level-1 supernode on subtree index s has a parent t * 4 + q with t equal to s or s xor 2; every level-2 supernode has exactly two children, one from each of the two subtree indices s and s xor 2. `level2_parent_node`: the level-2 supernode s * 4 + c has a parent t * 2 + q with t equal to s or s xor 4; every level-3 supernode has exactly two children, one from each of the two subtree indices s and s xor 4. `leaf_parent_rows`: distinct within each row. `level1_parent_rows`: distinct within each row; position j lies in the share j // (512 / 4) of the parent's rows, the share f being rows f * 1536 / 4 to (f + 1) * 1536 / 4 - 1. `level2_parent_rows`: distinct within each row; position j lies in the share j // (768 / 4) of the parent's rows, the share f being rows f * 2048 / 4 to (f + 1) * 2048 / 4 - 1.
All inputs are finite; a program needn't handle non-finite values.
Results may differ from a plain program's by a relative error of at most 0.0043.
Values may be sent and summed in bfloat16 or wider, within the bound.
No kernel may reach another device: no remote copies, remote signals or barrier semaphores. Data moves between devices by JAX's collectives and lax.ppermute only.
A program may use at most 320 MiB of HBM per device.

v0:
```python
import jax
import jax.numpy as jnp
from jax import lax
from jax.experimental import pallas as pl
from jax.experimental.pallas import tpu as pltpu
from jax.sharding import Mesh, PartitionSpec as P

RHS = 64
LEAVES, LEAF, BORDER0 = 4, 512, 256
NODES1, SEP1, BORDER1 = 2, 1024, 512
NODES2, SEP2, BORDER2 = 4, 1536, 768
NODES3, SEP3 = 2, 2048
FRONT = 4
SHARE2, SHARE3 = SEP2 // FRONT, SEP3 // FRONT
PART1, PART2 = BORDER1 // FRONT, BORDER2 // FRONT
ROWS = 6656
DEVICES = 128
EACH = ROWS // DEVICES
HALF = EACH // 2
SLOT = 32
EDGE0 = LEAVES * LEAF
EDGE1 = EDGE0 + NODES1 * SEP1
EDGE2 = EDGE1 + NODES2 * SHARE2
META = 16

SUBTREE = ("z", "x1", "x0", "core")
ALL = SUBTREE + ("front",)

bf16, f32, i32 = jnp.bfloat16, jnp.float32, jnp.int32
VMEM = pl.BlockSpec(memory_space=pltpu.VMEM)
SMEM = pl.BlockSpec(memory_space=pltpu.SMEM)
HBM = pl.BlockSpec(memory_space=pl.ANY)


def params(mib):
    return pltpu.CompilerParams(vmem_limit_bytes=mib << 20)


def struct(shape, dtype):
    return jax.ShapeDtypeStruct(shape, dtype)


def mm(a, b):
    return jnp.dot(a, b, preferred_element_type=f32)


def mm_nt(a, b):
    return lax.dot_general(a, b, (((1,), (1,)), ((), ())), preferred_element_type=f32)


def place(targets, width):
    ids = lax.broadcasted_iota(i32, (width, targets.shape[1]), 0)
    return jnp.where(ids == targets, 1.0, 0.0).astype(bf16)


def digits(targets, flag):
    n = targets.shape[1]
    ids = lax.broadcasted_iota(i32, (META, n), 0)
    high = jnp.broadcast_to(targets >> 6, (META, n))
    low = jnp.broadcast_to(targets & 63, (META, n))
    rows = jnp.where(ids == 0, high, jnp.where(ids == 1, low, flag))
    return rows.astype(f32).astype(bf16)


def undigits(meta):
    m = meta.astype(f32).astype(i32)
    return m[0:1] * 64 + m[1:2], m[2:3]


def tall_kernel(wide_ref, tall_ref):
    wide = wide_ref[...]
    tall_ref[...] = jnp.concatenate([wide, wide], axis=0).T


def pick_kernel(asked_ref, tall_ref, out_ref, buf):
    low = lax.broadcasted_iota(i32, (1, 128), 1) < RHS

    def gather(d, carry):
        base = pl.multiple_of(d * SLOT, SLOT)
        buf[pl.ds(base + 24, 8), :] = jnp.zeros((8, 128), f32)
        for k in range(HALF):
            first = tall_ref[pl.ds(asked_ref[d, k], 1), :]
            second = tall_ref[pl.ds(asked_ref[d, k + HALF], 1), :]
            buf[pl.ds(base + k, 1), :] = jnp.where(low, first, second)
        return carry

    lax.fori_loop(0, DEVICES, gather, 0)

    def narrow(d, carry):
        base = pl.multiple_of(d * 8 * SLOT, 8 * SLOT)
        out_ref[pl.ds(base, 8 * SLOT), :] = buf[pl.ds(base, 8 * SLOT), :].astype(bf16)
        return carry

    lax.fori_loop(0, DEVICES // 8, narrow, 0)


def leaf_kernel(
    order_ref,
    parent_ref,
    where_ref,
    arrived_ref,
    rows_ref,
    inverse_hbm,
    update_hbm,
    out_hbm,
    send_ref,
    rhs1_ref,
    rhs2_ref,
    rhs3_ref,
    flat,
    turned,
    tall,
    inverse_ref,
    update_ref,
    sol_ref,
    kept_ref,
    kept_rows,
    sems,
):
    load_inverse = pltpu.make_async_copy(inverse_hbm, inverse_ref, sems.at[0])
    load_update = pltpu.make_async_copy(update_hbm, update_ref, sems.at[1])
    load_inverse.start()
    load_update.start()

    def widen(d, carry):
        base = pl.multiple_of(d * 8 * SLOT, 8 * SLOT)
        piece = arrived_ref[pl.ds(base, 8 * SLOT), :].astype(f32)
        flat[pl.ds(base, 8 * SLOT), :] = piece
        turned[pl.ds(base, 8 * SLOT), :] = pltpu.roll(piece, RHS, 1)
        return carry

    lax.fori_loop(0, DEVICES // 8, widen, 0)

    def scatter(d, carry):
        base = pl.multiple_of(d * SLOT, SLOT)
        for k in range(HALF):
            tall[pl.ds(order_ref[d, k], 1), :] = flat[pl.ds(base + k, 1), :]
            tall[pl.ds(order_ref[d, k + HALF], 1), :] = turned[pl.ds(base + k, 1), :]
        return carry

    lax.fori_loop(0, DEVICES, scatter, 0)
    core = where_ref[0]
    load_inverse.wait()
    load_update.wait()
    for n in range(LEAVES):
        lhs = tall[n * LEAF : (n + 1) * LEAF, :].T[:RHS].astype(bf16)
        sol = mm(lhs, inverse_ref[n])
        sol_ref[:, n * LEAF : (n + 1) * LEAF] = sol
        terms = mm(sol.astype(bf16), update_ref[n]).astype(bf16)
        node = parent_ref[n]
        slot = node & 1
        away = ((node >> 3) & 1) != core
        targets = rows_ref[n : n + 1, :]

        @pl.when(away)
        def _():
            send_ref[slot, 0:RHS, :] = terms
            send_ref[slot, RHS : RHS + META, :] = digits(targets, 0)

        @pl.when(jnp.logical_not(away))
        def _():
            kept_ref[slot] = terms
            kept_rows[slot] = jnp.broadcast_to(targets, (8, BORDER0))

    store = pltpu.make_async_copy(sol_ref, out_hbm.at[:, 0:EDGE0], sems.at[2])
    store.start()
    for q in range(NODES1):
        rhs = tall[EDGE0 + q * SEP1 : EDGE0 + (q + 1) * SEP1, :].T[:RHS]
        rhs1_ref[q] = rhs - mm_nt(kept_ref[q], place(kept_rows[q, 0:1, :], SEP1))
    rhs2_ref[...] = tall[EDGE1:EDGE2, :].T[:RHS]
    rhs3_ref[...] = tall[EDGE2:ROWS, :].T[:RHS]
    store.wait()


def level1_kernel(
    parent_ref,
    got_ref,
    rhs_ref,
    rows_ref,
    inverse_ref,
    update_ref,
    out_in,
    out_hbm,
    send_ref,
    sol_ref,
    sem,
):
    del out_in
    for n in range(NODES1):
        targets, _ = undigits(got_ref[n, RHS : RHS + META, :])
        rhs = rhs_ref[n] - mm_nt(got_ref[n, 0:RHS, :], place(targets, SEP1))
        sol = mm(rhs.astype(bf16), inverse_ref[n])
        sol_ref[:, n * SEP1 : (n + 1) * SEP1] = sol
        terms = mm(sol.astype(bf16), update_ref[n]).astype(bf16)
        node = parent_ref[n]
        slot = node & 3
        side = (node >> 3) & 1
        for f in range(FRONT):
            own = slice(f * PART1, (f + 1) * PART1)
            targets = rows_ref[n : n + 1, own] + (slot * SHARE2 - f * SHARE2)
            meta = digits(targets, side)
            for x in range(2):
                send_ref[x * FRONT + f, n, 0:RHS, :] = terms[:, own]
                send_ref[x * FRONT + f, n, RHS : RHS + META, :] = meta
    store = pltpu.make_async_copy(sol_ref, out_hbm.at[:, EDGE0:EDGE1], sem)
    store.start()
    store.wait()


def sum2_kernel(where_ref, got_ref, rhs_ref, out_ref):
    x0 = where_ref[1]
    total = rhs_ref[...]
    for e in range(2 * FRONT):
        lhs, targets = [], []
        for n in range(NODES1):
            lhs.append(got_ref[e, n, 0:RHS, :])
            target, side = undigits(got_ref[e, n, RHS : RHS + META, :])
            targets.append(jnp.where(side == x0, target, -1))
        total = total - mm_nt(
            jnp.concatenate(lhs, axis=1), place(jnp.concatenate(targets, axis=1), NODES2 * SHARE2)
        )
    out_ref[...] = total.astype(bf16)


def level2_kernel(
    parent_ref,
    rhs_ref,
    rows_ref,
    inverse_ref,
    update_ref,
    out_in,
    out_hbm,
    send_ref,
    sol_ref,
    terms_ref,
    terms_rows,
    sem,
):
    del out_in
    for c in range(NODES2):
        own = slice(c * SHARE2, (c + 1) * SHARE2)
        lhs = jnp.concatenate([rhs_ref[g, :, own] for g in range(FRONT)], axis=1)
        sol = mm(lhs, inverse_ref[c])
        sol_ref[:, own] = sol
        node = parent_ref[c]
        slot = ((node >> 3) & 1) * NODES3 + (node & 1)
        terms_ref[slot] = mm(sol.astype(bf16), update_ref[c])
        terms_rows[slot] = jnp.broadcast_to(rows_ref[c : c + 1, :], (8, BORDER2))
    store = pltpu.make_async_copy(sol_ref, out_hbm.at[:, EDGE1:EDGE2], sem)
    store.start()
    for x in range(2):
        for f in range(FRONT):
            ends, end_rows = [], []
            for q in range(NODES3):
                at = x * NODES3 + q
                terms = terms_ref[at, :, f * PART2 : (f + 1) * PART2]
                rows = terms_rows[at, 0:1, f * PART2 : (f + 1) * PART2] + (q - f) * SHARE3
                send_ref[x * FRONT + f, q, 0:RHS, :] = terms[:, :128].astype(bf16)
                send_ref[x * FRONT + f, q, RHS : RHS + META, :] = digits(rows[:, :128], 0)
                ends.append(terms[:, 128:])
                end_rows.append(rows[:, 128:])
            end = jnp.concatenate(ends, axis=1).astype(bf16)
            send_ref[x * FRONT + f, NODES3, 0:RHS, :] = end
            send_ref[x * FRONT + f, NODES3, RHS : RHS + META, :] = digits(
                jnp.concatenate(end_rows, axis=1), 0
            )
    store.wait()


def sum3_kernel(got_ref, rhs_ref, out_ref):
    total = rhs_ref[...]
    for x in range(2):
        parts, targets = [], []
        for b in range(NODES3 + 1):
            pieces = [got_ref[x * FRONT + g, b, 0:RHS, :].astype(f32) for g in range(FRONT)]
            parts.append((pieces[0] + pieces[1]) + (pieces[2] + pieces[3]))
            targets.append(undigits(got_ref[x * FRONT, b, RHS : RHS + META, :])[0])
        part = jnp.concatenate(parts, axis=1)
        high = part.astype(bf16)
        low = (part - high.astype(f32)).astype(bf16)
        both = mm_nt(
            jnp.concatenate([high, low], axis=0),
            place(jnp.concatenate(targets, axis=1), NODES3 * SHARE3),
        )
        total = total - (both[:RHS] + both[RHS:])
    out_ref[...] = total.astype(bf16)


def level3_kernel(rhs_ref, inverse_ref, out_in, out_hbm, sol_ref, sem):
    del out_in
    for c in range(NODES3):
        own = slice(c * SHARE3, (c + 1) * SHARE3)
        lhs = jnp.concatenate([rhs_ref[g, :, own] for g in range(FRONT)], axis=1)
        sol_ref[:, own] = mm(lhs, inverse_ref[c])
    store = pltpu.make_async_copy(sol_ref, out_hbm.at[:, EDGE2:ROWS], sem)
    store.start()
    store.wait()


def exchange(block, axes):
    return lax.all_to_all(block, axes, split_axis=0, concat_axis=0, tiled=True)


def per_device(
    right_hand_sides,
    elimination_natural_index,
    leaf_diagonal_inverse,
    leaf_update_block,
    leaf_parent_rows,
    leaf_parent_node,
    level1_diagonal_inverse,
    level1_update_block,
    level1_parent_rows,
    level1_parent_node,
    level2_diagonal_inverse,
    level2_update_block,
    level2_parent_rows,
    level2_parent_node,
    level3_diagonal_inverse,
):
    where = jnp.stack([lax.axis_index("core"), lax.axis_index("x0")]).astype(i32)
    by_source, order = lax.sort(
        (elimination_natural_index, lax.iota(i32, ROWS)), num_keys=1, is_stable=False
    )
    asked = exchange((by_source % ROWS).reshape(DEVICES, EACH), ALL)
    tall = pl.pallas_call(
        tall_kernel,
        grid=(13,),
        in_specs=[pl.BlockSpec((RHS, 512), lambda i: (0, i))],
        out_specs=pl.BlockSpec((512, 128), lambda i: (i, 0)),
        out_shape=struct((ROWS, 128), f32),
        name="tall",
    )(right_hand_sides)
    picked = pl.pallas_call(
        pick_kernel,
        in_specs=[SMEM, VMEM],
        out_specs=VMEM,
        out_shape=struct((DEVICES * SLOT, 128), bf16),
        scratch_shapes=[pltpu.VMEM((DEVICES * SLOT, 128), f32)],
        compiler_params=params(16),
        name="pick",
    )(asked, tall)
    arrived = exchange(picked.reshape(DEVICES, SLOT, 128), ALL).reshape(DEVICES * SLOT, 128)
    out, send0, rhs1, rhs2, rhs3 = pl.pallas_call(
        leaf_kernel,
        in_specs=[SMEM, SMEM, SMEM, VMEM, VMEM, HBM, HBM],
        out_specs=[HBM, VMEM, VMEM, VMEM, VMEM],
        out_shape=[
            struct((RHS, ROWS), f32),
            struct((NODES1, RHS + META, BORDER0), bf16),
            struct((NODES1, RHS, SEP1), f32),
            struct((RHS, NODES2 * SHARE2), f32),
            struct((RHS, NODES3 * SHARE3), f32),
        ],
        scratch_shapes=[
            pltpu.VMEM((DEVICES * SLOT, 128), f32),
            pltpu.VMEM((DEVICES * SLOT, 128), f32),
            pltpu.VMEM((ROWS, 128), f32),
            pltpu.VMEM((LEAVES, LEAF, LEAF), bf16),
            pltpu.VMEM((LEAVES, LEAF, BORDER0), bf16),
            pltpu.VMEM((RHS, EDGE0), f32),
            pltpu.VMEM((NODES1, RHS, BORDER0), bf16),
            pltpu.VMEM((NODES1, 8, BORDER0), i32),
            pltpu.SemaphoreType.DMA((3,)),
        ],
        compiler_params=params(28),
        name="leaf",
    )(
        order.reshape(DEVICES, EACH),
        leaf_parent_node,
        where,
        arrived,
        leaf_parent_rows,
        leaf_diagonal_inverse,
        leaf_update_block,
    )
    got0 = lax.ppermute(send0, "core", [(0, 1), (1, 0)])
    out, send1 = pl.pallas_call(
        level1_kernel,
        in_specs=[SMEM, VMEM, VMEM, VMEM, VMEM, VMEM, HBM],
        out_specs=[HBM, VMEM],
        out_shape=[
            struct((RHS, ROWS), f32),
            struct((2 * FRONT, NODES1, RHS + META, PART1), bf16),
        ],
        scratch_shapes=[pltpu.VMEM((RHS, NODES1 * SEP1), f32), pltpu.SemaphoreType.DMA],
        input_output_aliases={6: 0},
        compiler_params=params(24),
        name="level1",
    )(
        level1_parent_node,
        got0,
        rhs1,
        level1_parent_rows,
        level1_diagonal_inverse,
        level1_update_block,
        out,
    )
    got1 = exchange(send1, ("x0", "front"))
    side2 = pl.pallas_call(
        sum2_kernel,
        in_specs=[SMEM, VMEM, VMEM],
        out_specs=VMEM,
        out_shape=struct((RHS, NODES2 * SHARE2), bf16),
        compiler_params=params(24),
        name="sum2",
    )(where, got1, rhs2)
    all2 = lax.all_gather(side2, "front", axis=0, tiled=False)
    out, send2 = pl.pallas_call(
        level2_kernel,
        in_specs=[SMEM, VMEM, VMEM, VMEM, VMEM, HBM],
        out_specs=[HBM, VMEM],
        out_shape=[
            struct((RHS, ROWS), f32),
            struct((2 * FRONT, NODES3 + 1, RHS + META, 128), bf16),
        ],
        scratch_shapes=[
            pltpu.VMEM((RHS, NODES2 * SHARE2), f32),
            pltpu.VMEM((2 * NODES3, RHS, BORDER2), f32),
            pltpu.VMEM((2 * NODES3, 8, BORDER2), i32),
            pltpu.SemaphoreType.DMA,
        ],
        input_output_aliases={5: 0},
        compiler_params=params(24),
        name="level2",
    )(
        level2_parent_node,
        all2,
        level2_parent_rows,
        level2_diagonal_inverse,
        level2_update_block,
        out,
    )
    got2 = exchange(send2, ("x1", "front"))
    side3 = pl.pallas_call(
        sum3_kernel,
        in_specs=[VMEM, VMEM],
        out_specs=VMEM,
        out_shape=struct((RHS, NODES3 * SHARE3), bf16),
        compiler_params=params(24),
        name="sum3",
    )(got2, rhs3)
    all3 = lax.all_gather(side3, "front", axis=0, tiled=False)
    return pl.pallas_call(
        level3_kernel,
        in_specs=[VMEM, VMEM, HBM],
        out_specs=HBM,
        out_shape=struct((RHS, ROWS), f32),
        scratch_shapes=[pltpu.VMEM((RHS, NODES3 * SHARE3), f32), pltpu.SemaphoreType.DMA],
        input_output_aliases={2: 0},
        compiler_params=params(24),
        name="level3",
    )(all3, level3_diagonal_inverse, out)


def solution(mesh):
    fine = Mesh(mesh.devices.reshape(4, 2, 2, 2, 4), ALL)
    return jax.shard_map(
        per_device,
        mesh=fine,
        in_specs=(
            P(None, ALL),
            P(ALL),
            P(ALL, None, None),
            P(ALL, None, None),
            P(ALL, None),
            P(ALL),
            P(ALL, None, None),
            P(ALL, None, None),
            P(ALL, None),
            P(ALL),
            P(SUBTREE, None, "front"),
            P(SUBTREE, "front", None),
            P(SUBTREE, None),
            P(SUBTREE),
            P(SUBTREE, None, "front"),
        ),
        out_specs=P(None, ALL),
        check_vma=False,
    )
```

profile of v0, /device:TPU:0, one launch (start us, length us, event | category | flops | bytes accessed | tf_op | source)
XLA Modules:
  0.0 145.3 jit_solution(1217914149586807263)
XLA Ops:
  0.0 6.4 %sort.15 = (s32[6656]{0:T(1024)S(1)}, s32[6656]{0:T(1024)S(1)}) sort(s32[6656]{0:T(1024)} %param.16, s32[6656]{0:T(1024)S(1)} %iota.3), dimensions={0}, to_apply=%region_0.0 | sort | flops 86528 | bytes 106496 | tf_op jit(solution)/shard_map/sort | solution.py:322
  6.5 0.7 all_to_all.16
  7.2 11.1 %all-to-all-start = ((s32[128,1,52]{2,1,0:T(1,128)}), s32[128,1,52]{2,1,0:T(1,128)S(1)}, u32[]{:S(2)}, u32[]{:S(2)}) async-start(s32[128,1,52]{2,1,0:T(1,128)} %bitcast.2), calls=%async_computation | async-start | bytes 131072 | tf_op jit(solution)/shard_map/all_to_all | solution.py:301
  18.4 8.7 %tall.1.tall_ref = f32[6656,128]{1,0:T(8,128)} custom-call(f32[64,6656]{1,0:T(8,128)} %wide_ref.1), custom_call_target="tpu_custom_call" | custom-call | tf_op jit(solution)/shard_map/tall/pallas_call | solution.py:326
  27.1 0.5 all-to-all-done
  27.6 2.0 %copy-done = f32[6656,128]{1,0:T(8,128)S(1)} copy-done((f32[6656,128]{1,0:T(8,128)S(1)}, f32[6656,128]{1,0:T(8,128)}, u32[]{:S(2)}) %copy-start) | copy-done | bytes 3407896
  29.6 8.7 %pick.1 = bf16[4096,128]{1,0:T(8,128)(2,1)} custom-call(s32[128,52]{1,0:T(8,128)S(1)} %bitcast.13, f32[6656,128]{1,0:T(8,128)S(1)} %copy-done), custom_call_target="tpu_custom_call" | custom-call | tf_op jit(solution)/shard_map/pick/pallas_call | solution.py:334
  38.3 9.2 %all-to-all-start.1 = ((bf16[128,32,128]{2,1,0:T(8,128)(2,1)}), bf16[128,32,128]{2,1,0:T(8,128)(2,1)S(1)}, u32[]{:S(2)}, u32[]{:S(2)}) async-start(bf16[128,32,128]{2,1,0:T(8,128)(2,1)} %bitcast.4), calls=%async_computation.1 | async-start | bytes 2097152 | tf_op jit(solution)/shard_map/all_to_all | solution.py:301
  47.5 0.1 reshape.13.order_ref
  47.6 0.1 pad_add_fusion.where_ref
  47.7 18.5 %all-to-all-done.1 = bf16[128,32,128]{2,1,0:T(8,128)(2,1)S(1)} async-done(((bf16[128,32,128]{2,1,0:T(8,128)(2,1)}), bf16[128,32,128]{2,1,0:T(8,128)(2,1)S(1)}, u32[]{:S(2)}, u32[]{:S(2)}) %all-to-all-start.1) | async-done | bytes 1048608 | tf_op jit(solution)/shard_map/all_to_all | solution.py:301
  66.3 0.0 copy-done.9
  66.3 0.0 copy-start.6
  66.3 1.2 copy-done.6
  67.5 11.6 %leaf.1 = (f32[64,6656]{1,0:T(8,128)}, bf16[2,80,256]{2,1,0:T(8,128)(2,1)S(1)}, f32[2,64,1024]{2,1,0:T(8,128)S(1)}, f32[64,1536]{1,0:T(8,128)S(1)}, f32[64,1024]{1,0:T(8,128)S(1)}) custom-call(s32[128,52]{1,0:T(8,128)S(1)} %reshape.13.order_ref, s32[4]{0:T(128)S(1)} %copy-done.10, s32[2]{0:T(128)S(1)} %pad_add_fusion.where_ref, ...), custom_call_target="tpu_custom_call" | custom-call | tf_op jit(solution)/shard_map/leaf/pallas_call | solution.py:344
  79.1 0.2 collective-permute-start
  79.3 1.2 collective-permute-done.got_ref
  80.5 0.0 copy-start.5
  80.5 1.7 %copy-done.5 = bf16[2,1024,512]{2,1,0:T(8,128)(2,1)S(1)} copy-done((bf16[2,1024,512]{2,1,0:T(8,128)(2,1)S(1)}, bf16[2,1024,512]{2,1,0:T(8,128)(2,1)}, u32[]{:S(2)}) %copy-start.5) | copy-done | bytes 2097176
  82.2 2.8 %level1.1 = (f32[64,6656]{1,0:T(8,128)}, bf16[8,2,80,128]{3,2,1,0:T(8,128)(2,1)S(1)}) custom-call(s32[2]{0:T(128)S(1)} %copy-done.11, bf16[2,80,256]{2,1,0:T(8,128)(2,1)S(1)} %collective-permute-done.got_ref, f32[2,64,1024]{2,1,0:T(8,128)S(1)} %get-tuple-element.19.rhs_ref, s32[2,512]{1,0:T(2,128)S(1)} %copy-done.8, ...), custom_call_target="tpu_custom_call", output_to_operand_aliasing={{0}: (6, {})} | custom-call | tf_op jit(solution)/shard_map/level1/pallas_call | solution.py:378
  85.0 0.0 copy-start.3
  85.0 0.0 copy-start.7
  85.0 0.0 copy-start.12
  85.0 11.2 %all_to_all.26.got_ref = bf16[8,2,80,128]{3,2,1,0:T(8,128)(2,1)S(1)} all-to-all(bf16[8,2,80,128]{3,2,1,0:T(8,128)(2,1)S(1)} %get-tuple-element.21), channel_id=1, replica_groups=mesh['z'=4,'x1'=2,'x0'=2,'core'=2,'front'=4] {'x0','front'}, dimensions={0} | all-to-all | bytes 655360 | tf_op jit(solution)/shard_map/all_to_all | solution.py:301
  96.2 2.6 %sum2.1 = bf16[64,1536]{1,0:T(8,128)(2,1)S(1)} custom-call(s32[2]{0:T(128)S(1)} %pad_add_fusion.where_ref, bf16[8,2,80,128]{3,2,1,0:T(8,128)(2,1)S(1)} %all_to_all.26.got_ref, f32[64,1536]{1,0:T(8,128)S(1)} %get-tuple-element.22.rhs_ref), custom_call_target="tpu_custom_call" | custom-call | tf_op jit(solution)/shard_map/sum2/pallas_call | solution.py:400
  98.8 14.3 %all-gather = bf16[256,1536]{1,0:T(8,128)(2,1)S(1)} all-gather(bf16[64,1536]{1,0:T(8,128)(2,1)S(1)} %sum2.1), channel_id=2, replica_groups=mesh['z'=4,'x1'=2,'x0'=2,'core'=2,'front'=4] {'front'}, dimensions={0}, use_global_device_ids=true | all-gather | bytes 983040 | tf_op jit(solution)/shard_map/all_gather | solution.py:408
  113.1 0.0 copy-start.2
  113.1 3.2 %level2.1 = (f32[64,6656]{1,0:T(8,128)}, bf16[8,3,80,128]{3,2,1,0:T(8,128)(2,1)S(1)}) custom-call(s32[4]{0:T(128)S(1)} %copy-done.12, bf16[4,64,1536]{2,1,0:T(8,128)(2,1)S(1)} %bitcast.11, s32[4,768]{1,0:T(4,128)S(1)} %copy-done.7, bf16[4,1536,384]{2,1,0:T(8,128)(2,1)S(1)} %bitcast.9, ...), custom_call_target="tpu_custom_call", output_to_operand_aliasing={{0}: (5, {})} | custom-call | tf_op jit(solution)/shard_map/level2/pallas_call | solution.py:409
  116.4 14.0 %all_to_all.27.got_ref = bf16[8,3,80,128]{3,2,1,0:T(8,128)(2,1)S(1)} all-to-all(bf16[8,3,80,128]{3,2,1,0:T(8,128)(2,1)S(1)} %get-tuple-element.24), channel_id=1, replica_groups=mesh['z'=4,'x1'=2,'x0'=2,'core'=2,'front'=4] {'x1','front'}, dimensions={0} | all-to-all | bytes 983040 | tf_op jit(solution)/shard_map/all_to_all | solution.py:301
  130.3 0.7 sum3.1
  131.0 12.8 %all-gather.1 = bf16[256,1024]{1,0:T(8,128)(2,1)S(1)} all-gather(bf16[64,1024]{1,0:T(8,128)(2,1)S(1)} %sum3.1), channel_id=3, replica_groups=mesh['z'=4,'x1'=2,'x0'=2,'core'=2,'front'=4] {'front'}, dimensions={0}, use_global_device_ids=true | all-gather | bytes 655360 | tf_op jit(solution)/shard_map/all_gather | solution.py:443
  143.8 1.5 %level3.1 = f32[64,6656]{1,0:T(8,128)} custom-call(bf16[4,64,1024]{2,1,0:T(8,128)(2,1)S(1)} %bitcast.12, bf16[2,2048,512]{2,1,0:T(8,128)(2,1)S(1)} %copy-done.2, f32[64,6656]{1,0:T(8,128)} %get-tuple-element.26.out_in), custom_call_target="tpu_custom_call", output_to_operand_aliasing={{}: (2, {})} | custom-call | tf_op jit(solution)/shard_map/level3/pallas_call | solution.py:444
  (23 shorter events, 0.1 us)
Async XLA Ops:
  7.2 20.4 %all-to-all-start = ((s32[128,1,52]{2,1,0:T(1,128)}), s32[128,1,52]{2,1,0:T(1,128)S(1)}, u32[]{:S(2)}, u32[]{:S(2)}) async-start(s32[128,1,52]{2,1,0:T(1,128)} %bitcast.2), calls=%async_computation | async-start | bytes 131072 | tf_op jit(solution)/shard_map/all_to_all | solution.py:301
  27.6 2.0 %copy-start = (f32[6656,128]{1,0:T(8,128)S(1)}, f32[6656,128]{1,0:T(8,128)}, u32[]{:S(2)}) copy-start(f32[6656,128]{1,0:T(8,128)} %tall.1.tall_ref) | copy-start | bytes 10223620
  38.2 28.0 %copy-start.4 = (bf16[4,512,512]{2,1,0:T(8,128)(2,1)S(1)}, bf16[4,512,512]{2,1,0:T(8,128)(2,1)}, u32[]{:S(2)}) copy-start(bf16[4,512,512]{2,1,0:T(8,128)(2,1)} %inverse_hbm.1) | copy-start | bytes 6291460
  38.2 28.0 %copy-start.9 = (s32[4,256]{1,0:T(4,128)S(1)}, s32[4,256]{1,0:T(4,128)}, u32[]{:S(2)}) copy-start(s32[4,256]{1,0:T(4,128)} %rows_ref.3) | copy-start | bytes 12292
  38.3 28.0 %copy-start.10 = (s32[4]{0:T(128)S(1)}, s32[4]{0:T(128)}, u32[]{:S(2)}) copy-start(s32[4]{0:T(128)} %parent_ref.3) | copy-start | bytes 52
  38.3 28.0 %all-to-all-start.1 = ((bf16[128,32,128]{2,1,0:T(8,128)(2,1)}), bf16[128,32,128]{2,1,0:T(8,128)(2,1)S(1)}, u32[]{:S(2)}, u32[]{:S(2)}) async-start(bf16[128,32,128]{2,1,0:T(8,128)(2,1)} %bitcast.4), calls=%async_computation.1 | async-start | bytes 2097152 | tf_op jit(solution)/shard_map/all_to_all | solution.py:301
  66.3 1.2 copy-start.6
  67.5 13.0 %copy-start.1 = (bf16[2,1024,1024]{2,1,0:T(8,128)(2,1)S(1)}, bf16[2,1024,1024]{2,1,0:T(8,128)(2,1)}, u32[]{:S(2)}) copy-start(bf16[2,1024,1024]{2,1,0:T(8,128)(2,1)} %inverse_ref.3) | copy-start | bytes 12582916
  67.5 13.0 %copy-start.8 = (s32[2,512]{1,0:T(2,128)S(1)}, s32[2,512]{1,0:T(2,128)}, u32[]{:S(2)}) copy-start(s32[2,512]{1,0:T(2,128)} %rows_ref.4) | copy-start | bytes 12292
  67.5 13.0 %copy-start.11 = (s32[2]{0:T(128)S(1)}, s32[2]{0:T(128)}, u32[]{:S(2)}) copy-start(s32[2]{0:T(128)} %parent_ref.4) | copy-start | bytes 28
  79.1 1.4 collective-permute-start
  80.5 32.6 %slice-start = ((s8[4718592]{0:T(1024)(128)(4,1)}), s8[4194304]{0:T(1024)(128)(4,1)S(1)}, s32[]{:S(2)}) async-start(s8[4718592]{0:T(1024)(128)(4,1)} %bitcast.8), calls=%async_computation.4 | async-start | bytes 8388608
  80.5 1.7 %copy-start.5 = (bf16[2,1024,512]{2,1,0:T(8,128)(2,1)S(1)}, bf16[2,1024,512]{2,1,0:T(8,128)(2,1)}, u32[]{:S(2)}) copy-start(bf16[2,1024,512]{2,1,0:T(8,128)(2,1)} %update_ref.2) | copy-start | bytes 6291460
  82.2 30.9 %slice-start.1 = ((s8[4718592]{0:T(1024)(128)(4,1)}), s8[524288]{0:T(1024)(128)(4,1)S(1)}, s32[]{:S(2)}) async-start(s8[4718592]{0:T(1024)(128)(4,1)} %bitcast.8), calls=%async_computation.5 | async-start | bytes 1048576
  85.0 28.1 %copy-start.3 = (bf16[4,384,768]{2,1,0:T(8,128)(2,1)S(1)}, bf16[4,384,768]{2,1,0:T(8,128)(2,1)}, u32[]{:S(2)}) copy-start(bf16[4,384,768]{2,1,0:T(8,128)(2,1)} %update_ref.3) | copy-start | bytes 7077892
  85.0 28.1 %copy-start.7 = (s32[4,768]{1,0:T(4,128)S(1)}, s32[4,768]{1,0:T(4,128)}, u32[]{:S(2)}) copy-start(s32[4,768]{1,0:T(4,128)} %rows_ref.5) | copy-start | bytes 36868
  85.0 28.1 %copy-start.12 = (s32[4]{0:T(128)S(1)}, s32[4]{0:T(128)}, u32[]{:S(2)}) copy-start(s32[4]{0:T(128)} %parent_ref.5) | copy-start | bytes 52
  113.1 30.6 %copy-start.2 = (bf16[2,2048,512]{2,1,0:T(8,128)(2,1)S(1)}, bf16[2,2048,512]{2,1,0:T(8,128)(2,1)}, u32[]{:S(2)}) copy-start(bf16[2,2048,512]{2,1,0:T(8,128)(2,1)} %inverse_ref.5) | copy-start | bytes 12582916
where the time goes:
time: 146 us; the launch traced here: 145 us
  blocking collectives  52.2 us (36%)
  Pallas kernels  39.7 us (27%)
  starting transfers between devices  20.6 us (14%)
  waiting for transfers between devices  20.2 us (14%)
  other arithmetic  6.54 us (4%)
  local copies, waits for them, and re-layouts  5.83 us (4%)
    all_to_all x2, blocking collectives, exchange(): return lax.all_to_all(block, axes, split_axis=0, concat_axis=0, tiled=True)  25.2 us
    all_to_all x2, starting transfers between devices, exchange(): return lax.all_to_all(block, axes, split_axis=0, concat_axis=0, tiled=True)  20.4 us
    all_to_all x2, waiting for transfers between devices, exchange(): return lax.all_to_all(block, axes, split_axis=0, concat_axis=0, tiled=True)  19.1 us
    all_gather x1, blocking collectives, per_device(): all2 = lax.all_gather(side2, 'front', axis=0, tiled=False)  14.3 us
    all_gather x1, blocking collectives, per_device(): all3 = lax.all_gather(side3, 'front', axis=0, tiled=False)  12.8 us
    pallas_call x1, Pallas kernels, per_device(): pl.pallas_call(leaf_kernel, in_specs=[SMEM, SMEM, SMEM, VMEM, VMEM, HBM,...  11.6 us
    pallas_call x1, Pallas kernels, per_device(): pl.pallas_call(tall_kernel, grid=(13,), in_specs=[pl.BlockSpec((RHS, 512)...  8.72 us
    pallas_call x1, Pallas kernels, per_device(): pl.pallas_call(pick_kernel, in_specs=[SMEM, VMEM], out_specs=VMEM, out_sh...  8.69 us
  transfers between devices with their start and end apart: 3, of which 3 were waited for; matrix products, arithmetic and copies ran while one was open for 0% of the time, Pallas kernels for 6%

commit v1 on v0

--- a/solution.py
+++ b/solution.py
@@ -21,7 +21,9 @@
 EDGE0 = LEAVES * LEAF
 EDGE1 = EDGE0 + NODES1 * SEP1
 EDGE2 = EDGE1 + NODES2 * SHARE2
-META = 16
+META = 8
+CHUNKS = 4
+LOW = 256
 
 SUBTREE = ("z", "x1", "x0", "core")
 ALL = SUBTREE + ("front",)
@@ -29,13 +31,17 @@
 bf16, f32, i32 = jnp.bfloat16, jnp.float32, jnp.int32
 VMEM = pl.BlockSpec(memory_space=pltpu.VMEM)
 SMEM = pl.BlockSpec(memory_space=pltpu.SMEM)
-HBM = pl.BlockSpec(memory_space=pl.ANY)
+HBM = pl.BlockSpec(memory_space=pltpu.HBM)
 
 
 def params(mib):
     return pltpu.CompilerParams(vmem_limit_bytes=mib << 20)
 
 
+def in_hbm(x):
+    return pltpu.with_memory_space_constraint(x, pltpu.HBM)
+
+
 def struct(shape, dtype):
     return jax.ShapeDtypeStruct(shape, dtype)
 
@@ -48,50 +54,64 @@
     return lax.dot_general(a, b, (((1,), (1,)), ((), ())), preferred_element_type=f32)
 
 
-def place(targets, width):
-    ids = lax.broadcasted_iota(i32, (width, targets.shape[1]), 0)
-    return jnp.where(ids == targets, 1.0, 0.0).astype(bf16)
+def place(terms, high, low, blocks):
+    n = low.shape[1]
+    ids = lax.broadcasted_iota(i32, (LOW, n), 0).astype(f32)
+    picks = jnp.where(ids == low, 1.0, 0.0).astype(bf16)
+    lhs = [jnp.where(high == h, t, 0.0).astype(bf16) for t in terms for h in range(blocks)]
+    found = mm_nt(jnp.concatenate(lhs, axis=0), picks)
+    out = []
+    for h in range(blocks):
+        parts = [
+            found[(t * blocks + h) * RHS : (t * blocks + h + 1) * RHS] for t in range(len(terms))
+        ]
+        out.append(sum(parts[1:], parts[0]))
+    return jnp.concatenate(out, axis=1)
 
 
 def digits(targets, flag):
     n = targets.shape[1]
     ids = lax.broadcasted_iota(i32, (META, n), 0)
-    high = jnp.broadcast_to(targets >> 6, (META, n))
-    low = jnp.broadcast_to(targets & 63, (META, n))
+    high = jnp.broadcast_to(targets >> 8, (META, n))
+    low = jnp.broadcast_to(targets & (LOW - 1), (META, n))
     rows = jnp.where(ids == 0, high, jnp.where(ids == 1, low, flag))
     return rows.astype(f32).astype(bf16)
 
 
 def undigits(meta):
-    m = meta.astype(f32).astype(i32)
-    return m[0:1] * 64 + m[1:2], m[2:3]
+    m = meta.astype(f32)
+    return m[0:1], m[1:2], m[2:3]
 
 
 def tall_kernel(wide_ref, tall_ref):
-    wide = wide_ref[...]
-    tall_ref[...] = jnp.concatenate([wide, wide], axis=0).T
-
-
-def pick_kernel(asked_ref, tall_ref, out_ref, buf):
+    for b in range(ROWS // 512):
+        wide = wide_ref[:, b * 512 : (b + 1) * 512]
+        tall_ref[b * 512 : (b + 1) * 512, :] = jnp.concatenate([wide, wide], axis=0).T
+
+
+def pick_kernel(asked_ref, tall_ref, out_hbm, buf, narrow, sems):
     low = lax.broadcasted_iota(i32, (1, 128), 1) < RHS
-
-    def gather(d, carry):
-        base = pl.multiple_of(d * SLOT, SLOT)
-        buf[pl.ds(base + 24, 8), :] = jnp.zeros((8, 128), f32)
-        for k in range(HALF):
-            first = tall_ref[pl.ds(asked_ref[d, k], 1), :]
-            second = tall_ref[pl.ds(asked_ref[d, k + HALF], 1), :]
-            buf[pl.ds(base + k, 1), :] = jnp.where(low, first, second)
-        return carry
-
-    lax.fori_loop(0, DEVICES, gather, 0)
-
-    def narrow(d, carry):
-        base = pl.multiple_of(d * 8 * SLOT, 8 * SLOT)
-        out_ref[pl.ds(base, 8 * SLOT), :] = buf[pl.ds(base, 8 * SLOT), :].astype(bf16)
-        return carry
-
-    lax.fori_loop(0, DEVICES // 8, narrow, 0)
+    step = DEVICES // CHUNKS
+    stores = []
+    for c in range(CHUNKS):
+
+        def gather(d, carry):
+            base = pl.multiple_of(d * SLOT, SLOT)
+            buf[pl.ds(base + 24, 8), :] = jnp.zeros((8, 128), f32)
+            for k in range(HALF):
+                first = tall_ref[pl.ds(asked_ref[d, k], 1), :]
+                second = tall_ref[pl.ds(asked_ref[d, k + HALF], 1), :]
+                buf[pl.ds(base + k, 1), :] = jnp.where(low, first, second)
+            return carry
+
+        lax.fori_loop(c * step, (c + 1) * step, gather, 0)
+        part = slice(c * step * SLOT, (c + 1) * step * SLOT)
+        narrow[part, :] = buf[part, :].astype(bf16)
+        store = pltpu.make_async_copy(narrow.at[part], out_hbm.at[part], sems.at[c])
+        store.start()
+        stores.append(store)
+    for store in stores:
+        store.wait()
 
 
 def leaf_kernel(
@@ -102,11 +122,15 @@
     rows_ref,
     inverse_hbm,
     update_hbm,
+    inverse1_hbm,
+    update1_hbm,
     out_hbm,
     send_ref,
     rhs1_ref,
     rhs2_ref,
     rhs3_ref,
+    inverse1_ref,
+    update1_ref,
     flat,
     turned,
     tall,
@@ -119,8 +143,12 @@
 ):
     load_inverse = pltpu.make_async_copy(inverse_hbm, inverse_ref, sems.at[0])
     load_update = pltpu.make_async_copy(update_hbm, update_ref, sems.at[1])
+    load_inverse1 = pltpu.make_async_copy(inverse1_hbm, inverse1_ref, sems.at[3])
+    load_update1 = pltpu.make_async_copy(update1_hbm, update1_ref, sems.at[4])
     load_inverse.start()
     load_update.start()
+    load_inverse1.start()
+    load_update1.start()
 
     def widen(d, carry):
         base = pl.multiple_of(d * 8 * SLOT, 8 * SLOT)
@@ -134,8 +162,10 @@
     def scatter(d, carry):
         base = pl.multiple_of(d * SLOT, SLOT)
         for k in range(HALF):
-            tall[pl.ds(order_ref[d, k], 1), :] = flat[pl.ds(base + k, 1), :]
-            tall[pl.ds(order_ref[d, k + HALF], 1), :] = turned[pl.ds(base + k, 1), :]
+            at = order_ref[d * EACH + k]
+            other = order_ref[d * EACH + k + HALF]
+            tall[pl.ds(at, 1), :] = flat[pl.ds(base + k, 1), :]
+            tall[pl.ds(other, 1), :] = turned[pl.ds(base + k, 1), :]
         return carry
 
     lax.fori_loop(0, DEVICES, scatter, 0)
@@ -166,10 +196,14 @@
     store.start()
     for q in range(NODES1):
         rhs = tall[EDGE0 + q * SEP1 : EDGE0 + (q + 1) * SEP1, :].T[:RHS]
-        rhs1_ref[q] = rhs - mm_nt(kept_ref[q], place(kept_rows[q, 0:1, :], SEP1))
+        rows = kept_rows[q, 0:1, :]
+        high, low = (rows >> 8).astype(f32), (rows & (LOW - 1)).astype(f32)
+        rhs1_ref[q] = rhs - place([kept_ref[q].astype(f32)], high, low, SEP1 // LOW)
     rhs2_ref[...] = tall[EDGE1:EDGE2, :].T[:RHS]
     rhs3_ref[...] = tall[EDGE2:ROWS, :].T[:RHS]
     store.wait()
+    load_inverse1.wait()
+    load_update1.wait()
 
 
 def level1_kernel(
@@ -187,8 +221,9 @@
 ):
     del out_in
     for n in range(NODES1):
-        targets, _ = undigits(got_ref[n, RHS : RHS + META, :])
-        rhs = rhs_ref[n] - mm_nt(got_ref[n, 0:RHS, :], place(targets, SEP1))
+        high, low, _ = undigits(got_ref[n, RHS : RHS + META, :])
+        got = got_ref[n, 0:RHS, :].astype(f32)
+        rhs = rhs_ref[n] - place([got], high, low, SEP1 // LOW)
         sol = mm(rhs.astype(bf16), inverse_ref[n])
         sol_ref[:, n * SEP1 : (n + 1) * SEP1] = sol
         terms = mm(sol.astype(bf16), update_ref[n]).astype(bf16)
@@ -208,18 +243,21 @@
 
 
 def sum2_kernel(where_ref, got_ref, rhs_ref, out_ref):
-    x0 = where_ref[1]
-    total = rhs_ref[...]
+    x0 = where_ref[1].astype(f32)
+    terms, highs, lows = [], [], []
     for e in range(2 * FRONT):
-        lhs, targets = [], []
         for n in range(NODES1):
-            lhs.append(got_ref[e, n, 0:RHS, :])
-            target, side = undigits(got_ref[e, n, RHS : RHS + META, :])
-            targets.append(jnp.where(side == x0, target, -1))
-        total = total - mm_nt(
-            jnp.concatenate(lhs, axis=1), place(jnp.concatenate(targets, axis=1), NODES2 * SHARE2)
-        )
-    out_ref[...] = total.astype(bf16)
+            terms.append(got_ref[e, n, 0:RHS, :].astype(f32))
+            high, low, side = undigits(got_ref[e, n, RHS : RHS + META, :])
+            highs.append(jnp.where(side == x0, high, -1.0))
+            lows.append(low)
+    total = place(
+        [jnp.concatenate(terms, axis=1)],
+        jnp.concatenate(highs, axis=1),
+        jnp.concatenate(lows, axis=1),
+        NODES2 * SHARE2 // LOW,
+    )
+    out_ref[...] = (rhs_ref[...] - total).astype(bf16)
 
 
 def level2_kernel(
@@ -268,22 +306,23 @@
 
 
 def sum3_kernel(got_ref, rhs_ref, out_ref):
-    total = rhs_ref[...]
+    parts, highs, lows = [], [], []
     for x in range(2):
-        parts, targets = [], []
         for b in range(NODES3 + 1):
             pieces = [got_ref[x * FRONT + g, b, 0:RHS, :].astype(f32) for g in range(FRONT)]
             parts.append((pieces[0] + pieces[1]) + (pieces[2] + pieces[3]))
-            targets.append(undigits(got_ref[x * FRONT, b, RHS : RHS + META, :])[0])
-        part = jnp.concatenate(parts, axis=1)
-        high = part.astype(bf16)
-        low = (part - high.astype(f32)).astype(bf16)
-        both = mm_nt(
-            jnp.concatenate([high, low], axis=0),
-            place(jnp.concatenate(targets, axis=1), NODES3 * SHARE3),
-        )
-        total = total - (both[:RHS] + both[RHS:])
-    out_ref[...] = total.astype(bf16)
+            high, low, _ = undigits(got_ref[x * FRONT, b, RHS : RHS + META, :])
+            highs.append(high)
+            lows.append(low)
+    part = jnp.concatenate(parts, axis=1)
+    coarse = part.astype(bf16).astype(f32)
+    total = place(
+        [coarse, part - coarse],
+        jnp.concatenate(highs, axis=1),
+        jnp.concatenate(lows, axis=1),
+        NODES3 * SHARE3 // LOW,
+    )
+    out_ref[...] = (rhs_ref[...] - total).astype(bf16)
 
 
 def level3_kernel(rhs_ref, inverse_ref, out_in, out_hbm, sol_ref, sem):
@@ -325,32 +364,38 @@
     asked = exchange((by_source % ROWS).reshape(DEVICES, EACH), ALL)
     tall = pl.pallas_call(
         tall_kernel,
-        grid=(13,),
-        in_specs=[pl.BlockSpec((RHS, 512), lambda i: (0, i))],
-        out_specs=pl.BlockSpec((512, 128), lambda i: (i, 0)),
+        in_specs=[VMEM],
+        out_specs=VMEM,
         out_shape=struct((ROWS, 128), f32),
+        compiler_params=params(8),
         name="tall",
     )(right_hand_sides)
     picked = pl.pallas_call(
         pick_kernel,
         in_specs=[SMEM, VMEM],
-        out_specs=VMEM,
+        out_specs=HBM,
         out_shape=struct((DEVICES * SLOT, 128), bf16),
-        scratch_shapes=[pltpu.VMEM((DEVICES * SLOT, 128), f32)],
+        scratch_shapes=[
+            pltpu.VMEM((DEVICES * SLOT, 128), f32),
+            pltpu.VMEM((DEVICES * SLOT, 128), bf16),
+            pltpu.SemaphoreType.DMA((CHUNKS,)),
+        ],
         compiler_params=params(16),
         name="pick",
     )(asked, tall)
     arrived = exchange(picked.reshape(DEVICES, SLOT, 128), ALL).reshape(DEVICES * SLOT, 128)
-    out, send0, rhs1, rhs2, rhs3 = pl.pallas_call(
+    out, send0, rhs1, rhs2, rhs3, inverse1, update1 = pl.pallas_call(
         leaf_kernel,
-        in_specs=[SMEM, SMEM, SMEM, VMEM, VMEM, HBM, HBM],
-        out_specs=[HBM, VMEM, VMEM, VMEM, VMEM],
+        in_specs=[SMEM, SMEM, SMEM, VMEM, VMEM, HBM, HBM, HBM, HBM],
+        out_specs=[HBM, VMEM, VMEM, VMEM, VMEM, VMEM, VMEM],
         out_shape=[
             struct((RHS, ROWS), f32),
             struct((NODES1, RHS + META, BORDER0), bf16),
             struct((NODES1, RHS, SEP1), f32),
             struct((RHS, NODES2 * SHARE2), f32),
             struct((RHS, NODES3 * SHARE3), f32),
+            struct((NODES1, SEP1, SEP1), bf16),
+            struct((NODES1, SEP1, BORDER1), bf16),
         ],
         scratch_shapes=[
             pltpu.VMEM((DEVICES * SLOT, 128), f32),
@@ -361,18 +406,20 @@
             pltpu.VMEM((RHS, EDGE0), f32),
             pltpu.VMEM((NODES1, RHS, BORDER0), bf16),
             pltpu.VMEM((NODES1, 8, BORDER0), i32),
-            pltpu.SemaphoreType.DMA((3,)),
+            pltpu.SemaphoreType.DMA((5,)),
         ],
         compiler_params=params(28),
         name="leaf",
     )(
-        order.reshape(DEVICES, EACH),
+        order,
         leaf_parent_node,
         where,
         arrived,
         leaf_parent_rows,
-        leaf_diagonal_inverse,
-        leaf_update_block,
+        in_hbm(leaf_diagonal_inverse),
+        in_hbm(leaf_update_block),
+        in_hbm(level1_diagonal_inverse),
+        in_hbm(level1_update_block),
     )
     got0 = lax.ppermute(send0, "core", [(0, 1), (1, 0)])
     out, send1 = pl.pallas_call(
@@ -392,8 +439,8 @@
         got0,
         rhs1,
         level1_parent_rows,
-        level1_diagonal_inverse,
-        level1_update_block,
+        inverse1,
+        update1,
         out,
     )
     got1 = exchange(send1, ("x0", "front"))

time: 146 us -> 133 us (0.911)
  Pallas kernels: 39.7 us -> 28.7 us
  waiting for transfers between devices: 20.2 us -> 26.7 us
  starting transfers between devices: 20.6 us -> 16.1 us
  local copies, waits for them, and re-layouts: 5.83 us -> 3.21 us
    pallas_call x2, Pallas kernels: 17.4 us -> 8.7 us  [the longest x1 7.77 us: per_device(): pl.pallas_call(pick_kernel, in_specs=[SMEM, VMEM], out_specs=HBM, out_sha...]
    all_to_all x2, waiting for transfers between devices: 19.1 us -> 25.5 us  [exchange(): return lax.all_to_all(block, axes, split_axis=0, concat_axis=0, tiled=True)]
    all_to_all x2, starting transfers between devices: 20.4 us -> 15.9 us  [exchange(): return lax.all_to_all(block, axes, split_axis=0, concat_axis=0, tiled=True)]
    unnamed x30 -> x24, local copies, waits for them, and re-layouts: 4.97 us -> 2.46 us
  transfers between devices with their start and end apart: 3 -> 3, of which waited for: 3 -> 3; matrix products, arithmetic and copies ran while one was open for 0% -> 0% of each run, Pallas kernels for 6% -> 1%
where the time goes in v1:
time: 133 us
  blocking collectives  51.7 us (39%)
  Pallas kernels  28.7 us (22%)
  waiting for transfers between devices  26.7 us (20%)
  starting transfers between devices  16.1 us (12%)
  other arithmetic  6.53 us (5%)
  local copies, waits for them, and re-layouts  3.21 us (2%)
    all_to_all x2, waiting for transfers between devices, exchange(): return lax.all_to_all(block, axes, split_axis=0, concat_axis=0, tiled=True)  25.5 us
    all_to_all x2, blocking collectives, exchange(): return lax.all_to_all(block, axes, split_axis=0, concat_axis=0, tiled=True)  24.6 us
    all_to_all x2, starting transfers between devices, exchange(): return lax.all_to_all(block, axes, split_axis=0, concat_axis=0, tiled=True)  15.9 us
    all_gather x1, blocking collectives, per_device(): all2 = lax.all_gather(side2, 'front', axis=0, tiled=False)  14.3 us
    all_gather x1, blocking collectives, per_device(): all3 = lax.all_gather(side3, 'front', axis=0, tiled=False)  12.8 us
    pallas_call x1, Pallas kernels, per_device(): pl.pallas_call(leaf_kernel, in_specs=[SMEM, SMEM, SMEM, VMEM, VMEM, HBM,...  11.1 us
    pallas_call x1, Pallas kernels, per_device(): pl.pallas_call(pick_kernel, in_specs=[SMEM, VMEM], out_specs=HBM, out_sha...  7.77 us
    sort x1, other arithmetic, per_device(): lax.sort((elimination_natural_index, lax.iota(i32, ROWS)), num_keys=1, is...  6.44 us
  transfers between devices with their start and end apart: 3, of which 3 were waited for; matrix products, arithmetic and copies ran while one was open for 0% of the time, Pallas kernels for 1%

profile of v1, /device:TPU:0, one launch (start us, length us, event | category | flops | bytes accessed | tf_op | source)
XLA Modules:
  0.0 133.0 jit_solution(18289561837036527776)
XLA Ops:
  0.0 6.4 %sort.15 = (s32[6656]{0:T(1024)S(1)}, s32[6656]{0:T(1024)S(1)}) sort(s32[6656]{0:T(1024)} %param.16, s32[6656]{0:T(1024)S(1)} %iota.3), dimensions={0}, to_apply=%region_0.0 | sort | flops 86528 | bytes 106496 | tf_op jit(solution)/shard_map/sort | solution.py:361
  6.5 0.7 all_to_all.16
  7.2 11.1 %all-to-all-start = ((s32[128,1,52]{2,1,0:T(1,128)}), s32[128,1,52]{2,1,0:T(1,128)S(1)}, u32[]{:S(2)}, u32[]{:S(2)}) async-start(s32[128,1,52]{2,1,0:T(1,128)} %bitcast.2), calls=%async_computation | async-start | bytes 131072 | tf_op jit(solution)/shard_map/all_to_all | solution.py:340
  18.4 0.0 copy-start.3
  18.4 1.4 %copy-done.3 = f32[64,6656]{1,0:T(8,128)S(1)} copy-done((f32[64,6656]{1,0:T(8,128)S(1)}, f32[64,6656]{1,0:T(8,128)}, u32[]{:S(2)}) %copy-start.3) | copy-done | bytes 1703960
  19.8 0.9 tall.1.tall_ref
  20.8 6.8 %all-to-all-done = s32[128,1,52]{2,1,0:T(1,128)S(1)} async-done(((s32[128,1,52]{2,1,0:T(1,128)}), s32[128,1,52]{2,1,0:T(1,128)S(1)}, u32[]{:S(2)}, u32[]{:S(2)}) %all-to-all-start) | async-done | bytes 26656 | tf_op jit(solution)/shard_map/all_to_all | solution.py:340
  27.6 7.8 %pick.1 = bf16[4096,128]{1,0:T(8,128)(2,1)S(1)} custom-call(s32[128,52]{1,0:T(8,128)S(1)} %bitcast.14, f32[6656,128]{1,0:T(8,128)S(1)} %tall.1.tall_ref), custom_call_target="tpu_custom_call" | custom-call | tf_op jit(solution)/shard_map/pick/pallas_call | solution.py:373
  35.4 0.0 copy-start
  35.4 1.0 copy-done
  36.4 4.8 %all-to-all-start.1 = ((bf16[128,32,128]{2,1,0:T(8,128)(2,1)}), bf16[128,32,128]{2,1,0:T(8,128)(2,1)S(1)}, u32[]{:S(2)}, u32[]{:S(2)}) async-start(bf16[128,32,128]{2,1,0:T(8,128)(2,1)} %bitcast.10), calls=%async_computation.1 | async-start | bytes 2097152 | tf_op jit(solution)/shard_map/all_to_all | solution.py:340
  41.1 0.1 pad_add_fusion.where_ref
  41.2 18.7 %all-to-all-done.1 = bf16[128,32,128]{2,1,0:T(8,128)(2,1)S(1)} async-done(((bf16[128,32,128]{2,1,0:T(8,128)(2,1)}), bf16[128,32,128]{2,1,0:T(8,128)(2,1)S(1)}, u32[]{:S(2)}, u32[]{:S(2)}) %all-to-all-start.1) | async-done | bytes 1048608 | tf_op jit(solution)/shard_map/all_to_all | solution.py:340
  59.9 0.0 copy-done.5
  59.9 0.0 copy-done.7
  59.9 11.1 %leaf.1 = (f32[64,6656]{1,0:T(8,128)}, bf16[2,72,256]{2,1,0:T(8,128)(2,1)S(1)}, f32[2,64,1024]{2,1,0:T(8,128)S(1)}, f32[64,1536]{1,0:T(8,128)S(1)}, f32[64,1024]...) custom-call(s32[6656]{0:T(1024)S(1)} %get-tuple-element.18.order_ref, ...), custom_call_target="tpu_custom_call" | custom-call | tf_op jit(solution)/shard_map/leaf/pallas_call | solution.py:387
  71.0 0.2 collective-permute-start
  71.2 1.2 collective-permute-done.got_ref
  72.4 2.7 %level1.1 = (f32[64,6656]{1,0:T(8,128)}, bf16[8,2,72,128]{3,2,1,0:T(8,128)(2,1)S(1)}) custom-call(s32[2]{0:T(128)S(1)} %copy-done.8, bf16[2,72,256]{2,1,0:T(8,128)(2,1)S(1)} %collective-permute-done.got_ref, f32[2,64,1024]{2,1,0:T(8,128)S(1)} %get-tuple-element.21.rhs_ref, s32[2,512]{1,0:T(2,128)S(1)} %copy-done.6, ...), custom_call_target="tpu_custom_call", output_to_operand_aliasing={{0}: (6, {})} | custom-call | tf_op jit(solution)/shard_map/level1/pallas_call | solution.py:425
  75.2 0.0 copy-start.2
  75.2 0.0 copy-start.4
  75.2 0.0 copy-start.9
  75.2 10.9 %all_to_all.26.got_ref = bf16[8,2,72,128]{3,2,1,0:T(8,128)(2,1)S(1)} all-to-all(bf16[8,2,72,128]{3,2,1,0:T(8,128)(2,1)S(1)} %get-tuple-element.25), channel_id=1, replica_groups=mesh['z'=4,'x1'=2,'x0'=2,'core'=2,'front'=4] {'x0','front'}, dimensions={0} | all-to-all | bytes 589824 | tf_op jit(solution)/shard_map/all_to_all | solution.py:340
  86.1 1.1 sum2.1
  87.3 14.3 %all-gather = bf16[256,1536]{1,0:T(8,128)(2,1)S(1)} all-gather(bf16[64,1536]{1,0:T(8,128)(2,1)S(1)} %sum2.1), channel_id=2, replica_groups=mesh['z'=4,'x1'=2,'x0'=2,'core'=2,'front'=4] {'front'}, dimensions={0}, use_global_device_ids=true | all-gather | bytes 983040 | tf_op jit(solution)/shard_map/all_gather | solution.py:455
  101.6 0.0 copy-done.2
  101.6 0.0 copy-start.1
  101.7 3.0 %level2.1 = (f32[64,6656]{1,0:T(8,128)}, bf16[8,3,72,128]{3,2,1,0:T(8,128)(2,1)S(1)}) custom-call(s32[4]{0:T(128)S(1)} %copy-done.9, bf16[4,64,1536]{2,1,0:T(8,128)(2,1)S(1)} %bitcast.12, s32[4,768]{1,0:T(4,128)S(1)} %copy-done.4, bf16[4,1536,384]{2,1,0:T(8,128)(2,1)S(1)} %bitcast.9, ...), custom_call_target="tpu_custom_call", output_to_operand_aliasing={{0}: (5, {})} | custom-call | tf_op jit(solution)/shard_map/level2/pallas_call | solution.py:456
  104.6 13.7 %all_to_all.27.got_ref = bf16[8,3,72,128]{3,2,1,0:T(8,128)(2,1)S(1)} all-to-all(bf16[8,3,72,128]{3,2,1,0:T(8,128)(2,1)S(1)} %get-tuple-element.28), channel_id=1, replica_groups=mesh['z'=4,'x1'=2,'x0'=2,'core'=2,'front'=4] {'x1','front'}, dimensions={0} | all-to-all | bytes 884736 | tf_op jit(solution)/shard_map/all_to_all | solution.py:340
  118.3 0.4 sum3.1
  118.7 12.8 %all-gather.1 = bf16[256,1024]{1,0:T(8,128)(2,1)S(1)} all-gather(bf16[64,1024]{1,0:T(8,128)(2,1)S(1)} %sum3.1), channel_id=3, replica_groups=mesh['z'=4,'x1'=2,'x0'=2,'core'=2,'front'=4] {'front'}, dimensions={0}, use_global_device_ids=true | all-gather | bytes 655360 | tf_op jit(solution)/shard_map/all_gather | solution.py:490
  131.5 1.5 %level3.1 = f32[64,6656]{1,0:T(8,128)} custom-call(bf16[4,64,1024]{2,1,0:T(8,128)(2,1)S(1)} %bitcast.13, bf16[2,2048,512]{2,1,0:T(8,128)(2,1)S(1)} %copy-done.1, f32[64,6656]{1,0:T(8,128)} %get-tuple-element.30.out_in), custom_call_target="tpu_custom_call", output_to_operand_aliasing={{}: (2, {})} | custom-call | tf_op jit(solution)/shard_map/level3/pallas_call | solution.py:491
  (16 shorter events, 0.0 us)
Async XLA Ops:
  7.2 20.4 %all-to-all-start = ((s32[128,1,52]{2,1,0:T(1,128)}), s32[128,1,52]{2,1,0:T(1,128)S(1)}, u32[]{:S(2)}, u32[]{:S(2)}) async-start(s32[128,1,52]{2,1,0:T(1,128)} %bitcast.2), calls=%async_computation | async-start | bytes 131072 | tf_op jit(solution)/shard_map/all_to_all | solution.py:340
  18.4 1.5 %copy-start.3 = (f32[64,6656]{1,0:T(8,128)S(1)}, f32[64,6656]{1,0:T(8,128)}, u32[]{:S(2)}) copy-start(f32[64,6656]{1,0:T(8,128)} %wide_ref.1) | copy-start | bytes 5111812
  35.4 1.0 copy-start
  36.4 23.5 %copy-start.5 = (s32[4,256]{1,0:T(4,128)S(1)}, s32[4,256]{1,0:T(4,128)}, u32[]{:S(2)}) copy-start(s32[4,256]{1,0:T(4,128)} %rows_ref.3) | copy-start | bytes 12292
  36.4 23.5 %copy-start.7 = (s32[4]{0:T(128)S(1)}, s32[4]{0:T(128)}, u32[]{:S(2)}) copy-start(s32[4]{0:T(128)} %parent_ref.3) | copy-start | bytes 52
  36.4 23.5 %all-to-all-start.1 = ((bf16[128,32,128]{2,1,0:T(8,128)(2,1)}), bf16[128,32,128]{2,1,0:T(8,128)(2,1)S(1)}, u32[]{:S(2)}, u32[]{:S(2)}) async-start(bf16[128,32,128]{2,1,0:T(8,128)(2,1)} %bitcast.10), calls=%async_computation.1 | async-start | bytes 2097152 | tf_op jit(solution)/shard_map/all_to_all | solution.py:340
  59.9 12.5 %copy-start.6 = (s32[2,512]{1,0:T(2,128)S(1)}, s32[2,512]{1,0:T(2,128)}, u32[]{:S(2)}) copy-start(s32[2,512]{1,0:T(2,128)} %rows_ref.4) | copy-start | bytes 12292
  59.9 12.5 %copy-start.8 = (s32[2]{0:T(128)S(1)}, s32[2]{0:T(128)}, u32[]{:S(2)}) copy-start(s32[2]{0:T(128)} %parent_ref.4) | copy-start | bytes 28
  71.0 1.3 %collective-permute-start = (bf16[2,72,256]{2,1,0:T(8,128)(2,1)S(1)}, bf16[2,72,256]{2,1,0:T(8,128)(2,1)S(1)}, u32[]{:S(2)}, u32[]{:S(2)}) collective-permute-start(bf16[2,72,256]{2,1,0:T(8,128)(2,1)S(1)} %get-tuple-element.20), channel_id=1, source_target_pairs={{0,4},{4,0},{1,5},{5,1},{2,6},{6,2},{3,7},{7,3},{8,12},{12,8},{9,1... | collective-permute-start | bytes 221192 | tf_op jit(solution)/shard_map/ppermute | solution.py:424
  72.4 29.2 %slice-start = ((s8[4718592]{0:T(1024)(128)(4,1)}), s8[4194304]{0:T(1024)(128)(4,1)S(1)}, s32[]{:S(2)}) async-start(s8[4718592]{0:T(1024)(128)(4,1)} %bitcast.8), calls=%async_computation.4 | async-start | bytes 8388608
  72.4 29.2 %slice-start.1 = ((s8[4718592]{0:T(1024)(128)(4,1)}), s8[524288]{0:T(1024)(128)(4,1)S(1)}, s32[]{:S(2)}) async-start(s8[4718592]{0:T(1024)(128)(4,1)} %bitcast.8), calls=%async_computation.5 | async-start | bytes 1048576
  75.2 26.5 %copy-start.2 = (bf16[4,384,768]{2,1,0:T(8,128)(2,1)S(1)}, bf16[4,384,768]{2,1,0:T(8,128)(2,1)}, u32[]{:S(2)}) copy-start(bf16[4,384,768]{2,1,0:T(8,128)(2,1)} %update_ref.1) | copy-start | bytes 7077892
  75.2 26.4 %copy-start.4 = (s32[4,768]{1,0:T(4,128)S(1)}, s32[4,768]{1,0:T(4,128)}, u32[]{:S(2)}) copy-start(s32[4,768]{1,0:T(4,128)} %rows_ref.5) | copy-start | bytes 36868
  75.2 26.4 %copy-start.9 = (s32[4]{0:T(128)S(1)}, s32[4]{0:T(128)}, u32[]{:S(2)}) copy-start(s32[4]{0:T(128)} %parent_ref.5) | copy-start | bytes 52
  101.6 29.9 %copy-start.1 = (bf16[2,2048,512]{2,1,0:T(8,128)(2,1)S(1)}, bf16[2,2048,512]{2,1,0:T(8,128)(2,1)}, u32[]{:S(2)}) copy-start(bf16[2,2048,512]{2,1,0:T(8,128)(2,1)} %inverse_ref.3) | copy-start | bytes 12582916

commit v2 on v1

--- a/solution.py
+++ b/solution.py
@@ -17,12 +17,11 @@
 DEVICES = 128
 EACH = ROWS // DEVICES
 HALF = EACH // 2
-SLOT = 32
+GROUP = 4
 EDGE0 = LEAVES * LEAF
 EDGE1 = EDGE0 + NODES1 * SEP1
 EDGE2 = EDGE1 + NODES2 * SHARE2
 META = 8
-CHUNKS = 4
 LOW = 256
 
 SUBTREE = ("z", "x1", "x0", "core")
@@ -89,29 +88,42 @@
         tall_ref[b * 512 : (b + 1) * 512, :] = jnp.concatenate([wide, wide], axis=0).T
 
 
-def pick_kernel(asked_ref, tall_ref, out_hbm, buf, narrow, sems):
+def pick_kernel(asked_ref, tall_ref, out_hbm, buf, narrow, sem):
     low = lax.broadcasted_iota(i32, (1, 128), 1) < RHS
-    step = DEVICES // CHUNKS
-    stores = []
-    for c in range(CHUNKS):
-
-        def gather(d, carry):
-            base = pl.multiple_of(d * SLOT, SLOT)
-            buf[pl.ds(base + 24, 8), :] = jnp.zeros((8, 128), f32)
+
+    def gather(g, carry):
+        base = pl.multiple_of(g * (GROUP * HALF), 8)
+        for e in range(GROUP):
+            d = g * GROUP + e
             for k in range(HALF):
                 first = tall_ref[pl.ds(asked_ref[d, k], 1), :]
                 second = tall_ref[pl.ds(asked_ref[d, k + HALF], 1), :]
-                buf[pl.ds(base + k, 1), :] = jnp.where(low, first, second)
-            return carry
-
-        lax.fori_loop(c * step, (c + 1) * step, gather, 0)
-        part = slice(c * step * SLOT, (c + 1) * step * SLOT)
-        narrow[part, :] = buf[part, :].astype(bf16)
-        store = pltpu.make_async_copy(narrow.at[part], out_hbm.at[part], sems.at[c])
-        store.start()
-        stores.append(store)
-    for store in stores:
-        store.wait()
+                buf[pl.ds(base + (e * HALF + k), 1), :] = jnp.where(low, first, second)
+        return carry
+
+    lax.fori_loop(0, DEVICES // GROUP, gather, 0)
+    narrow[...] = buf[...].astype(bf16)
+    store = pltpu.make_async_copy(narrow, out_hbm, sem)
+    store.start()
+    store.wait()
+
+
+def restore(order_ref, arrived_ref, flat, turned, tall_ref):
+    piece = arrived_ref[...].astype(f32)
+    flat[...] = piece
+    turned[...] = pltpu.roll(piece, RHS, 1)
+
+    def scatter(g, carry):
+        base = pl.multiple_of(g * (GROUP * HALF), 8)
+        for e in range(GROUP):
+            at = (g * GROUP + e) * EACH
+            for k in range(HALF):
+                row = pl.ds(base + (e * HALF + k), 1)
+                tall_ref[pl.ds(order_ref[at + k], 1), :] = flat[row, :]
+                tall_ref[pl.ds(order_ref[at + k + HALF], 1), :] = turned[row, :]
+        return carry
+
+    lax.fori_loop(0, DEVICES // GROUP, scatter, 0)
 
 
 def leaf_kernel(
@@ -149,34 +161,20 @@
     load_update.start()
     load_inverse1.start()
     load_update1.start()
-
-    def widen(d, carry):
-        base = pl.multiple_of(d * 8 * SLOT, 8 * SLOT)
-        piece = arrived_ref[pl.ds(base, 8 * SLOT), :].astype(f32)
-        flat[pl.ds(base, 8 * SLOT), :] = piece
-        turned[pl.ds(base, 8 * SLOT), :] = pltpu.roll(piece, RHS, 1)
-        return carry
-
-    lax.fori_loop(0, DEVICES // 8, widen, 0)
-
-    def scatter(d, carry):
-        base = pl.multiple_of(d * SLOT, SLOT)
-        for k in range(HALF):
-            at = order_ref[d * EACH + k]
-            other = order_ref[d * EACH + k + HALF]
-            tall[pl.ds(at, 1), :] = flat[pl.ds(base + k, 1), :]
-            tall[pl.ds(other, 1), :] = turned[pl.ds(base + k, 1), :]
-        return carry
-
-    lax.fori_loop(0, DEVICES, scatter, 0)
-    core = where_ref[0]
+    restore(order_ref, arrived_ref, flat, turned, tall)
     load_inverse.wait()
     load_update.wait()
+    sols, terms = [], []
     for n in range(LEAVES):
         lhs = tall[n * LEAF : (n + 1) * LEAF, :].T[:RHS].astype(bf16)
-        sol = mm(lhs, inverse_ref[n])
-        sol_ref[:, n * LEAF : (n + 1) * LEAF] = sol
-        terms = mm(sol.astype(bf16), update_ref[n]).astype(bf16)
+        sols.append(mm(lhs, inverse_ref[n]))
+    for n in range(LEAVES):
+        sol_ref[:, n * LEAF : (n + 1) * LEAF] = sols[n]
+        terms.append(mm(sols[n].astype(bf16), update_ref[n]).astype(bf16))
+    rhs2_ref[...] = tall[EDGE1:EDGE2, :].T[:RHS]
+    rhs3_ref[...] = tall[EDGE2:ROWS, :].T[:RHS]
+    core = where_ref[0]
+    for n in range(LEAVES):
         node = parent_ref[n]
         slot = node & 1
         away = ((node >> 3) & 1) != core
@@ -184,12 +182,12 @@
 
         @pl.when(away)
         def _():
-            send_ref[slot, 0:RHS, :] = terms
+            send_ref[slot, 0:RHS, :] = terms[n]
             send_ref[slot, RHS : RHS + META, :] = digits(targets, 0)
 
         @pl.when(jnp.logical_not(away))
         def _():
-            kept_ref[slot] = terms
+            kept_ref[slot] = terms[n]
             kept_rows[slot] = jnp.broadcast_to(targets, (8, BORDER0))
 
     store = pltpu.make_async_copy(sol_ref, out_hbm.at[:, 0:EDGE0], sems.at[2])
@@ -199,8 +197,6 @@
         rows = kept_rows[q, 0:1, :]
         high, low = (rows >> 8).astype(f32), (rows & (LOW - 1)).astype(f32)
         rhs1_ref[q] = rhs - place([kept_ref[q].astype(f32)], high, low, SEP1 // LOW)
-    rhs2_ref[...] = tall[EDGE1:EDGE2, :].T[:RHS]
-    rhs3_ref[...] = tall[EDGE2:ROWS, :].T[:RHS]
     store.wait()
     load_inverse1.wait()
     load_update1.wait()
@@ -374,16 +370,16 @@
         pick_kernel,
         in_specs=[SMEM, VMEM],
         out_specs=HBM,
-        out_shape=struct((DEVICES * SLOT, 128), bf16),
+        out_shape=pltpu.HBM((DEVICES * HALF, 128), bf16),
         scratch_shapes=[
-            pltpu.VMEM((DEVICES * SLOT, 128), f32),
-            pltpu.VMEM((DEVICES * SLOT, 128), bf16),
-            pltpu.SemaphoreType.DMA((CHUNKS,)),
+            pltpu.VMEM((DEVICES * HALF, 128), f32),
+            pltpu.VMEM((DEVICES * HALF, 128), bf16),
+            pltpu.SemaphoreType.DMA,
         ],
         compiler_params=params(16),
         name="pick",
     )(asked, tall)
-    arrived = exchange(picked.reshape(DEVICES, SLOT, 128), ALL).reshape(DEVICES * SLOT, 128)
+    arrived = exchange(picked.reshape(DEVICES, HALF // 2, 2, 128), ALL)
     out, send0, rhs1, rhs2, rhs3, inverse1, update1 = pl.pallas_call(
         leaf_kernel,
         in_specs=[SMEM, SMEM, SMEM, VMEM, VMEM, HBM, HBM, HBM, HBM],
@@ -398,8 +394,8 @@
             struct((NODES1, SEP1, BORDER1), bf16),
         ],
         scratch_shapes=[
-            pltpu.VMEM((DEVICES * SLOT, 128), f32),
-            pltpu.VMEM((DEVICES * SLOT, 128), f32),
+            pltpu.VMEM((DEVICES * HALF, 128), f32),
+            pltpu.VMEM((DEVICES * HALF, 128), f32),
             pltpu.VMEM((ROWS, 128), f32),
             pltpu.VMEM((LEAVES, LEAF, LEAF), bf16),
             pltpu.VMEM((LEAVES, LEAF, BORDER0), bf16),
@@ -408,13 +404,13 @@
             pltpu.VMEM((NODES1, 8, BORDER0), i32),
             pltpu.SemaphoreType.DMA((5,)),
         ],
-        compiler_params=params(28),
+        compiler_params=params(24),
         name="leaf",
     )(
         order,
         leaf_parent_node,
         where,
-        arrived,
+        arrived.reshape(DEVICES * HALF, 128),
         leaf_parent_rows,
         in_hbm(leaf_diagonal_inverse),
         in_hbm(leaf_update_block),

time: 133 us -> 128 us (0.962)
  Pallas kernels: 28.7 us -> 26.1 us
  waiting for transfers between devices: 26.7 us -> 24.6 us
    pallas_call x1, Pallas kernels: 11.1 us -> 8.34 us  [per_device(): pl.pallas_call(leaf_kernel, in_specs=[SMEM, SMEM, SMEM, VMEM, VMEM, HBM,...]
    all_to_all x2, waiting for transfers between devices: 25.5 us -> 23.4 us  [exchange(): return lax.all_to_all(block, axes, split_axis=0, concat_axis=0, tiled=True)]
where the time goes in v2:
time: 128 us; the launch traced here: 127 us
  blocking collectives  51.7 us (40%)
  Pallas kernels  26.1 us (20%)
  waiting for transfers between devices  24.6 us (19%)
  starting transfers between devices  16 us (12%)
  other arithmetic  6.53 us (5%)
  local copies, waits for them, and re-layouts  2.24 us (2%)
    all_to_all x2, blocking collectives, exchange(): return lax.all_to_all(block, axes, split_axis=0, concat_axis=0, tiled=True)  24.6 us
    all_to_all x2, waiting for transfers between devices, exchange(): return lax.all_to_all(block, axes, split_axis=0, concat_axis=0, tiled=True)  23.4 us
    all_to_all x2, starting transfers between devices, exchange(): return lax.all_to_all(block, axes, split_axis=0, concat_axis=0, tiled=True)  15.8 us
    all_gather x1, blocking collectives, per_device(): all2 = lax.all_gather(side2, 'front', axis=0, tiled=False)  14.3 us
    all_gather x1, blocking collectives, per_device(): all3 = lax.all_gather(side3, 'front', axis=0, tiled=False)  12.8 us
    pallas_call x1, Pallas kernels, per_device(): pl.pallas_call(leaf_kernel, in_specs=[SMEM, SMEM, SMEM, VMEM, VMEM, HBM,...  8.34 us
    pallas_call x1, Pallas kernels, per_device(): pl.pallas_call(pick_kernel, in_specs=[SMEM, VMEM], out_specs=HBM, out_sha...  8.01 us
    sort x1, other arithmetic, per_device(): lax.sort((elimination_natural_index, lax.iota(i32, ROWS)), num_keys=1, is...  6.44 us
  transfers between devices with their start and end apart: 3, of which 3 were waited for; matrix products, arithmetic and copies ran while one was open for 0% of the time, Pallas kernels for 1%

profile of v2, /device:TPU:0, one launch (start us, length us, event | category | flops | bytes accessed | tf_op | source)
XLA Modules:
  0.0 127.3 jit_solution(804339295566035471)
XLA Ops:
  0.0 6.4 %sort.15 = (s32[6656]{0:T(1024)S(1)}, s32[6656]{0:T(1024)S(1)}) sort(s32[6656]{0:T(1024)} %param.16, s32[6656]{0:T(1024)S(1)} %iota.3), dimensions={0}, to_apply=%region_0.0 | sort | flops 86528 | bytes 106496 | tf_op jit(solution)/shard_map/sort | solution.py:357
  6.5 0.7 all_to_all.16
  7.2 11.1 %all-to-all-start = ((s32[128,1,52]{2,1,0:T(1,128)}), s32[128,1,52]{2,1,0:T(1,128)S(1)}, u32[]{:S(2)}, u32[]{:S(2)}) async-start(s32[128,1,52]{2,1,0:T(1,128)} %bitcast.2), calls=%async_computation | async-start | bytes 131072 | tf_op jit(solution)/shard_map/all_to_all | solution.py:336
  18.4 0.0 copy-start.2
  18.4 1.4 %copy-done.2 = f32[64,6656]{1,0:T(8,128)S(1)} copy-done((f32[64,6656]{1,0:T(8,128)S(1)}, f32[64,6656]{1,0:T(8,128)}, u32[]{:S(2)}) %copy-start.2) | copy-done | bytes 1703960
  19.8 0.9 tall.1.tall_ref
  20.8 6.8 %all-to-all-done = s32[128,1,52]{2,1,0:T(1,128)S(1)} async-done(((s32[128,1,52]{2,1,0:T(1,128)}), s32[128,1,52]{2,1,0:T(1,128)S(1)}, u32[]{:S(2)}, u32[]{:S(2)}) %all-to-all-start) | async-done | bytes 26656 | tf_op jit(solution)/shard_map/all_to_all | solution.py:336
  27.6 8.0 %pick.1 = bf16[3328,128]{1,0:T(8,128)(2,1)} custom-call(s32[128,52]{1,0:T(8,128)S(1)} %bitcast.13, f32[6656,128]{1,0:T(8,128)S(1)} %tall.1.tall_ref), custom_call_target="tpu_custom_call" | custom-call | tf_op jit(solution)/shard_map/pick/pallas_call | solution.py:369
  35.6 4.6 %all-to-all-start.1 = ((bf16[128,13,2,128]{3,2,1,0:T(2,128)(2,1)}), bf16[128,13,2,128]{3,2,1,0:T(2,128)(2,1)S(1)}, u32[]{:S(2)}, u32[]{:S(2)}) async-start(bf16[128,13,2,128]{3,2,1,0:T(2,128)(2,1)} %bitcast.14), calls=%async_computation.1 | async-start | bytes 1703936 | tf_op jit(solution)/shard_map/all_to_all | solution.py:336
  40.3 0.1 pad_add_fusion.where_ref
  40.4 16.6 %all-to-all-done.1 = bf16[128,13,2,128]{3,2,1,0:T(2,128)(2,1)S(1)} async-done(((bf16[128,13,2,128]{3,2,1,0:T(2,128)(2,1)}), bf16[128,13,2,128]{3,2,1,0:T(2,128)(2,1)S(1)}, u32[]{:S(2)}, u32[]{:S(2)}) %all-to-all-start.1) | async-done | bytes 852000 | tf_op jit(solution)/shard_map/all_to_all | solution.py:336
  56.9 0.0 copy-done.4
  57.0 0.0 copy-done.6
  57.0 8.3 %leaf.1 = (f32[64,6656]{1,0:T(8,128)}, bf16[2,72,256]{2,1,0:T(8,128)(2,1)S(1)}, f32[2,64,1024]{2,1,0:T(8,128)S(1)}, f32[64,1536]{1,0:T(8,128)S(1)}, f32[64,1024]...) custom-call(s32[6656]{0:T(1024)S(1)} %get-tuple-element.18.order_ref, ...), custom_call_target="tpu_custom_call" | custom-call | tf_op jit(solution)/shard_map/leaf/pallas_call | solution.py:383
  65.3 0.2 collective-permute-start
  65.5 1.2 collective-permute-done.got_ref
  66.7 0.0 copy-done.5
  66.7 2.8 %level1.1 = (f32[64,6656]{1,0:T(8,128)}, bf16[8,2,72,128]{3,2,1,0:T(8,128)(2,1)S(1)}) custom-call(s32[2]{0:T(128)S(1)} %copy-done.7, bf16[2,72,256]{2,1,0:T(8,128)(2,1)S(1)} %collective-permute-done.got_ref, f32[2,64,1024]{2,1,0:T(8,128)S(1)} %get-tuple-element.21.rhs_ref, s32[2,512]{1,0:T(2,128)S(1)} %copy-done.5, ...), custom_call_target="tpu_custom_call", output_to_operand_aliasing={{0}: (6, {})} | custom-call | tf_op jit(solution)/shard_map/level1/pallas_call | solution.py:421
  69.4 0.0 copy-start.1
  69.4 0.0 copy-start.3
  69.5 0.0 copy-start.8
  69.5 10.9 %all_to_all.26.got_ref = bf16[8,2,72,128]{3,2,1,0:T(8,128)(2,1)S(1)} all-to-all(bf16[8,2,72,128]{3,2,1,0:T(8,128)(2,1)S(1)} %get-tuple-element.25), channel_id=1, replica_groups=mesh['z'=4,'x1'=2,'x0'=2,'core'=2,'front'=4] {'x0','front'}, dimensions={0} | all-to-all | bytes 589824 | tf_op jit(solution)/shard_map/all_to_all | solution.py:336
  80.4 1.1 sum2.1
  81.6 14.3 %all-gather = bf16[256,1536]{1,0:T(8,128)(2,1)S(1)} all-gather(bf16[64,1536]{1,0:T(8,128)(2,1)S(1)} %sum2.1), channel_id=2, replica_groups=mesh['z'=4,'x1'=2,'x0'=2,'core'=2,'front'=4] {'front'}, dimensions={0}, use_global_device_ids=true | all-gather | bytes 983040 | tf_op jit(solution)/shard_map/all_gather | solution.py:451
  95.9 0.0 slice-done
  95.9 0.0 copy-done.1
  95.9 0.0 copy-start
  95.9 3.0 %level2.1 = (f32[64,6656]{1,0:T(8,128)}, bf16[8,3,72,128]{3,2,1,0:T(8,128)(2,1)S(1)}) custom-call(s32[4]{0:T(128)S(1)} %copy-done.8, bf16[4,64,1536]{2,1,0:T(8,128)(2,1)S(1)} %bitcast.11, s32[4,768]{1,0:T(4,128)S(1)} %copy-done.3, bf16[4,1536,384]{2,1,0:T(8,128)(2,1)S(1)} %bitcast.9, ...), custom_call_target="tpu_custom_call", output_to_operand_aliasing={{0}: (5, {})} | custom-call | tf_op jit(solution)/shard_map/level2/pallas_call | solution.py:452
  98.9 13.7 %all_to_all.27.got_ref = bf16[8,3,72,128]{3,2,1,0:T(8,128)(2,1)S(1)} all-to-all(bf16[8,3,72,128]{3,2,1,0:T(8,128)(2,1)S(1)} %get-tuple-element.28), channel_id=1, replica_groups=mesh['z'=4,'x1'=2,'x0'=2,'core'=2,'front'=4] {'x1','front'}, dimensions={0} | all-to-all | bytes 884736 | tf_op jit(solution)/shard_map/all_to_all | solution.py:336
  112.6 0.4 sum3.1
  113.0 12.8 %all-gather.1 = bf16[256,1024]{1,0:T(8,128)(2,1)S(1)} all-gather(bf16[64,1024]{1,0:T(8,128)(2,1)S(1)} %sum3.1), channel_id=3, replica_groups=mesh['z'=4,'x1'=2,'x0'=2,'core'=2,'front'=4] {'front'}, dimensions={0}, use_global_device_ids=true | all-gather | bytes 655360 | tf_op jit(solution)/shard_map/all_gather | solution.py:486
  125.8 1.5 %level3.1 = f32[64,6656]{1,0:T(8,128)} custom-call(bf16[4,64,1024]{2,1,0:T(8,128)(2,1)S(1)} %bitcast.12, bf16[2,2048,512]{2,1,0:T(8,128)(2,1)S(1)} %copy-done, f32[64,6656]{1,0:T(8,128)} %get-tuple-element.30.out_in), custom_call_target="tpu_custom_call", output_to_operand_aliasing={{}: (2, {})} | custom-call | tf_op jit(solution)/shard_map/level3/pallas_call | solution.py:487
  (14 shorter events, 0.0 us)
Async XLA Ops:
  7.2 20.4 %all-to-all-start = ((s32[128,1,52]{2,1,0:T(1,128)}), s32[128,1,52]{2,1,0:T(1,128)S(1)}, u32[]{:S(2)}, u32[]{:S(2)}) async-start(s32[128,1,52]{2,1,0:T(1,128)} %bitcast.2), calls=%async_computation | async-start | bytes 131072 | tf_op jit(solution)/shard_map/all_to_all | solution.py:336
  18.4 1.5 %copy-start.2 = (f32[64,6656]{1,0:T(8,128)S(1)}, f32[64,6656]{1,0:T(8,128)}, u32[]{:S(2)}) copy-start(f32[64,6656]{1,0:T(8,128)} %wide_ref.1) | copy-start | bytes 5111812
  27.6 29.4 %copy-start.4 = (s32[4,256]{1,0:T(4,128)S(1)}, s32[4,256]{1,0:T(4,128)}, u32[]{:S(2)}) copy-start(s32[4,256]{1,0:T(4,128)} %rows_ref.3) | copy-start | bytes 12292
  27.6 29.4 %copy-start.6 = (s32[4]{0:T(128)S(1)}, s32[4]{0:T(128)}, u32[]{:S(2)}) copy-start(s32[4]{0:T(128)} %parent_ref.3) | copy-start | bytes 52
  35.6 21.3 %all-to-all-start.1 = ((bf16[128,13,2,128]{3,2,1,0:T(2,128)(2,1)}), bf16[128,13,2,128]{3,2,1,0:T(2,128)(2,1)S(1)}, u32[]{:S(2)}, u32[]{:S(2)}) async-start(bf16[128,13,2,128]{3,2,1,0:T(2,128)(2,1)} %bitcast.14), calls=%async_computation.1 | async-start | bytes 1703936 | tf_op jit(solution)/shard_map/all_to_all | solution.py:336
  57.0 9.7 %copy-start.5 = (s32[2,512]{1,0:T(2,128)S(1)}, s32[2,512]{1,0:T(2,128)}, u32[]{:S(2)}) copy-start(s32[2,512]{1,0:T(2,128)} %rows_ref.4) | copy-start | bytes 12292
  57.0 9.7 %copy-start.7 = (s32[2]{0:T(128)S(1)}, s32[2]{0:T(128)}, u32[]{:S(2)}) copy-start(s32[2]{0:T(128)} %parent_ref.4) | copy-start | bytes 28
  65.3 1.3 %collective-permute-start = (bf16[2,72,256]{2,1,0:T(8,128)(2,1)S(1)}, bf16[2,72,256]{2,1,0:T(8,128)(2,1)S(1)}, u32[]{:S(2)}, u32[]{:S(2)}) collective-permute-start(bf16[2,72,256]{2,1,0:T(8,128)(2,1)S(1)} %get-tuple-element.20), channel_id=1, source_target_pairs={{0,4},{4,0},{1,5},{5,1},{2,6},{6,2},{3,7},{7,3},{8,12},{12,8},{9,1... | collective-permute-start | bytes 221192 | tf_op jit(solution)/shard_map/ppermute | solution.py:420
  66.7 29.2 %slice-start = ((s8[4718592]{0:T(1024)(128)(4,1)}), s8[4194304]{0:T(1024)(128)(4,1)S(1)}, s32[]{:S(2)}) async-start(s8[4718592]{0:T(1024)(128)(4,1)} %bitcast.8), calls=%async_computation.4 | async-start | bytes 8388608
  66.7 29.2 %slice-start.1 = ((s8[4718592]{0:T(1024)(128)(4,1)}), s8[524288]{0:T(1024)(128)(4,1)S(1)}, s32[]{:S(2)}) async-start(s8[4718592]{0:T(1024)(128)(4,1)} %bitcast.8), calls=%async_computation.5 | async-start | bytes 1048576
  69.4 26.5 %copy-start.1 = (bf16[4,384,768]{2,1,0:T(8,128)(2,1)S(1)}, bf16[4,384,768]{2,1,0:T(8,128)(2,1)}, u32[]{:S(2)}) copy-start(bf16[4,384,768]{2,1,0:T(8,128)(2,1)} %update_ref.1) | copy-start | bytes 7077892
  69.4 26.4 %copy-start.3 = (s32[4,768]{1,0:T(4,128)S(1)}, s32[4,768]{1,0:T(4,128)}, u32[]{:S(2)}) copy-start(s32[4,768]{1,0:T(4,128)} %rows_ref.5) | copy-start | bytes 36868
  69.5 26.4 %copy-start.8 = (s32[4]{0:T(128)S(1)}, s32[4]{0:T(128)}, u32[]{:S(2)}) copy-start(s32[4]{0:T(128)} %parent_ref.5) | copy-start | bytes 52
  95.9 29.9 %copy-start = (bf16[2,2048,512]{2,1,0:T(8,128)(2,1)S(1)}, bf16[2,2048,512]{2,1,0:T(8,128)(2,1)}, u32[]{:S(2)}) copy-start(bf16[2,2048,512]{2,1,0:T(8,128)(2,1)} %inverse_ref.3) | copy-start | bytes 12582916

commit v3 on v2

--- a/solution.py
+++ b/solution.py
@@ -17,6 +17,9 @@
 DEVICES = 128
 EACH = ROWS // DEVICES
 HALF = EACH // 2
+LANES = 128
+BLOCKS = ROWS // LANES
+PAIRS = DEVICES * HALF
 GROUP = 4
 EDGE0 = LEAVES * LEAF
 EDGE1 = EDGE0 + NODES1 * SEP1
@@ -108,26 +111,50 @@
     store.wait()
 
 
-def restore(order_ref, arrived_ref, flat, turned, tall_ref):
+def rank_kernel(index_ref, asked_ref, slot_ref):
+    index = index_ref[...].astype(f32)
+    source = jnp.floor((index + 0.5) * (1.0 / ROWS))
+    local = index - source * ROWS
+    high = jnp.floor(local * (1.0 / LANES))
+    low = local - high * LANES
+    rows = lax.broadcasted_iota(i32, (LANES, 2 * LANES), 0)
+    columns = lax.broadcasted_iota(i32, (LANES, 2 * LANES), 1)
+    before = jnp.where((rows < columns) | (columns >= LANES), 1.0, 0.0).astype(bf16)
+    devices = lax.broadcasted_iota(i32, (DEVICES, LANES), 0).astype(f32)
+    ranks = lax.broadcasted_iota(i32, (64, LANES), 0).astype(f32)
+    seen = jnp.zeros((DEVICES, LANES), f32)
+    asked = jnp.zeros((DEVICES, LANES), f32)
+    for b in range(BLOCKS):
+        row = slice(b, b + 1)
+        mine = jnp.where(devices == source[row], 1.0, 0.0)
+        mine16 = mine.astype(bf16)
+        counts = mm(mine16, before)
+        rank = jnp.sum(mine * (seen + counts[:, :LANES]), axis=0, keepdims=True)
+        seen = seen + counts[:, LANES:]
+        at = ranks == rank
+        values = [jnp.where(at, high[row], 0.0), jnp.where(at, low[row], 0.0)]
+        asked = asked + mm_nt(mine16, jnp.concatenate(values, axis=0).astype(bf16))
+        slot = source[row] * HALF + jnp.where(rank < HALF, rank, rank + (PAIRS - HALF))
+        slot_ref[row, :] = slot.astype(i32)
+    asked_ref[...] = (asked * LANES + pltpu.roll(asked, 64, 1)).astype(i32)
+
+
+def restore(slot_ref, arrived_ref, both, tall_ref):
     piece = arrived_ref[...].astype(f32)
-    flat[...] = piece
-    turned[...] = pltpu.roll(piece, RHS, 1)
-
-    def scatter(g, carry):
-        base = pl.multiple_of(g * (GROUP * HALF), 8)
-        for e in range(GROUP):
-            at = (g * GROUP + e) * EACH
-            for k in range(HALF):
-                row = pl.ds(base + (e * HALF + k), 1)
-                tall_ref[pl.ds(order_ref[at + k], 1), :] = flat[row, :]
-                tall_ref[pl.ds(order_ref[at + k + HALF], 1), :] = turned[row, :]
+    both[0:PAIRS, :] = piece
+    both[PAIRS : 2 * PAIRS, :] = pltpu.roll(piece, RHS, 1)
+
+    def gather(r, carry):
+        base = pl.multiple_of(r * LANES, LANES)
+        for k in range(LANES):
+            tall_ref[pl.ds(base + k, 1), :] = both[pl.ds(slot_ref[r, k], 1), :]
         return carry
 
-    lax.fori_loop(0, DEVICES // GROUP, scatter, 0)
+    lax.fori_loop(0, BLOCKS, gather, 0)
 
 
 def leaf_kernel(
-    order_ref,
+    slot_ref,
     parent_ref,
     where_ref,
     arrived_ref,
@@ -143,8 +170,7 @@
     rhs3_ref,
     inverse1_ref,
     update1_ref,
-    flat,
-    turned,
+    both,
     tall,
     inverse_ref,
     update_ref,
@@ -161,7 +187,7 @@
     load_update.start()
     load_inverse1.start()
     load_update1.start()
-    restore(order_ref, arrived_ref, flat, turned, tall)
+    restore(slot_ref, arrived_ref, both, tall)
     load_inverse.wait()
     load_update.wait()
     sols, terms = [], []
@@ -354,10 +380,15 @@
     level3_diagonal_inverse,
 ):
     where = jnp.stack([lax.axis_index("core"), lax.axis_index("x0")]).astype(i32)
-    by_source, order = lax.sort(
-        (elimination_natural_index, lax.iota(i32, ROWS)), num_keys=1, is_stable=False
-    )
-    asked = exchange((by_source % ROWS).reshape(DEVICES, EACH), ALL)
+    requests, slot = pl.pallas_call(
+        rank_kernel,
+        in_specs=[VMEM],
+        out_specs=[VMEM, VMEM],
+        out_shape=[struct((DEVICES, LANES), i32), struct((BLOCKS, LANES), i32)],
+        compiler_params=params(6),
+        name="rank",
+    )(elimination_natural_index.reshape(BLOCKS, LANES))
+    asked = exchange(requests.reshape(DEVICES, 1, LANES), ALL).reshape(DEVICES, LANES)
     tall = pl.pallas_call(
         tall_kernel,
         in_specs=[VMEM],
@@ -394,8 +425,7 @@
             struct((NODES1, SEP1, BORDER1), bf16),
         ],
         scratch_shapes=[
-            pltpu.VMEM((DEVICES * HALF, 128), f32),
-            pltpu.VMEM((DEVICES * HALF, 128), f32),
+            pltpu.VMEM((2 * PAIRS, 128), f32),
             pltpu.VMEM((ROWS, 128), f32),
             pltpu.VMEM((LEAVES, LEAF, LEAF), bf16),
             pltpu.VMEM((LEAVES, LEAF, BORDER0), bf16),
@@ -407,7 +437,7 @@
         compiler_params=params(24),
         name="leaf",
     )(
-        order,
+        slot,
         leaf_parent_node,
         where,
         arrived.reshape(DEVICES * HALF, 128),

time: 128 us -> 125 us (0.977)
  other arithmetic: 6.53 us -> 0.08 us
  Pallas kernels: 26.1 us -> 29.4 us
    sort x1 -> x0, other arithmetic: 6.44 us -> none  [per_device(): lax.sort((elimination_natural_index, lax.iota(i32, ROWS)), num_keys=1, is...]
    pallas_call x0 -> x1, Pallas kernels: none -> 3.23 us  [per_device(): pl.pallas_call(rank_kernel, in_specs=[VMEM], out_specs=[VMEM, VMEM], out_...]
where the time goes in v3:
time: 125 us; the launch traced here: 124 us
  blocking collectives  51.7 us (41%)
  Pallas kernels  29.4 us (24%)
  waiting for transfers between devices  24.6 us (20%)
  starting transfers between devices  16 us (13%)
  local copies, waits for them, and re-layouts  2.24 us (2%)
    all_to_all x2, blocking collectives, exchange(): return lax.all_to_all(block, axes, split_axis=0, concat_axis=0, tiled=True)  24.6 us
    all_to_all x2, waiting for transfers between devices, exchange(): return lax.all_to_all(block, axes, split_axis=0, concat_axis=0, tiled=True)  23.4 us
    all_to_all x2, starting transfers between devices, exchange(): return lax.all_to_all(block, axes, split_axis=0, concat_axis=0, tiled=True)  15.8 us
    all_gather x1, blocking collectives, per_device(): all2 = lax.all_gather(side2, 'front', axis=0, tiled=False)  14.3 us
    all_gather x1, blocking collectives, per_device(): all3 = lax.all_gather(side3, 'front', axis=0, tiled=False)  12.8 us
    pallas_call x1, Pallas kernels, per_device(): pl.pallas_call(leaf_kernel, in_specs=[SMEM, SMEM, SMEM, VMEM, VMEM, HBM,...  8.41 us
    pallas_call x1, Pallas kernels, per_device(): pl.pallas_call(pick_kernel, in_specs=[SMEM, VMEM], out_specs=HBM, out_sha...  8.01 us
    pallas_call x1, Pallas kernels, per_device(): pl.pallas_call(rank_kernel, in_specs=[VMEM], out_specs=[VMEM, VMEM], out_...  3.23 us
  transfers between devices with their start and end apart: 3, of which 3 were waited for; matrix products, arithmetic and copies ran while one was open for 0% of the time, Pallas kernels for 1%

profile of v3, /device:TPU:0, one launch (start us, length us, event | category | flops | bytes accessed | tf_op | source)
XLA Modules:
  0.0 124.2 jit_solution(14486052740239653858)
XLA Ops:
  0.0 0.7 copy-done.3
  0.7 3.2 %rank.1 = (s32[128,128]{1,0:T(8,128)}, s32[52,128]{1,0:T(8,128)S(1)}) custom-call(s32[52,128]{1,0:T(8,128)S(1)} %bitcast.17), custom_call_target="tpu_custom_call" | custom-call | tf_op jit(solution)/shard_map/rank/pallas_call | solution.py:383
  4.0 11.1 %all-to-all-start = ((s32[128,1,128]{2,1,0:T(1,128)}), s32[128,1,128]{2,1,0:T(1,128)S(1)}, u32[]{:S(2)}, u32[]{:S(2)}) async-start(s32[128,1,128]{2,1,0:T(1,128)} %bitcast.4), calls=%async_computation | async-start | bytes 131072 | tf_op jit(solution)/shard_map/all_to_all | solution.py:362
  15.1 0.0 copy-start.2
  15.1 1.4 %copy-done.2 = f32[64,6656]{1,0:T(8,128)S(1)} copy-done((f32[64,6656]{1,0:T(8,128)S(1)}, f32[64,6656]{1,0:T(8,128)}, u32[]{:S(2)}) %copy-start.2) | copy-done | bytes 1703960
  16.6 0.9 tall.1.tall_ref
  17.5 6.8 %all-to-all-done = s32[128,1,128]{2,1,0:T(1,128)S(1)} async-done(((s32[128,1,128]{2,1,0:T(1,128)}), s32[128,1,128]{2,1,0:T(1,128)S(1)}, u32[]{:S(2)}, u32[]{:S(2)}) %all-to-all-start) | async-done | bytes 65568 | tf_op jit(solution)/shard_map/all_to_all | solution.py:362
  24.4 8.0 %pick.1 = bf16[3328,128]{1,0:T(8,128)(2,1)} custom-call(s32[128,128]{1,0:T(8,128)S(1)} %bitcast.16, f32[6656,128]{1,0:T(8,128)S(1)} %tall.1.tall_ref), custom_call_target="tpu_custom_call" | custom-call | tf_op jit(solution)/shard_map/pick/pallas_call | solution.py:400
  32.4 4.6 %all-to-all-start.1 = ((bf16[128,13,2,128]{3,2,1,0:T(2,128)(2,1)}), bf16[128,13,2,128]{3,2,1,0:T(2,128)(2,1)S(1)}, u32[]{:S(2)}, u32[]{:S(2)}) async-start(bf16[128,13,2,128]{3,2,1,0:T(2,128)(2,1)} %bitcast.18), calls=%async_computation.1 | async-start | bytes 1703936 | tf_op jit(solution)/shard_map/all_to_all | solution.py:362
  37.0 0.1 pad_add_fusion.where_ref
  37.1 16.6 %all-to-all-done.1 = bf16[128,13,2,128]{3,2,1,0:T(2,128)(2,1)S(1)} async-done(((bf16[128,13,2,128]{3,2,1,0:T(2,128)(2,1)}), bf16[128,13,2,128]{3,2,1,0:T(2,128)(2,1)S(1)}, u32[]{:S(2)}, u32[]{:S(2)}) %all-to-all-start.1) | async-done | bytes 852000 | tf_op jit(solution)/shard_map/all_to_all | solution.py:362
  53.7 0.0 copy-done.5
  53.7 0.0 copy-done.7
  53.7 8.4 %leaf.1 = (f32[64,6656]{1,0:T(8,128)}, bf16[2,72,256]{2,1,0:T(8,128)(2,1)S(1)}, f32[2,64,1024]{2,1,0:T(8,128)S(1)}, f32[64,1536]{1,0:T(8,128)S(1)}, f32[64,1024]...) custom-call(s32[52,128]{1,0:T(8,128)S(1)} %get-tuple-element.18.slot_ref, ...), custom_call_target="tpu_custom_call" | custom-call | tf_op jit(solution)/shard_map/leaf/pallas_call | solution.py:414
  62.1 0.2 collective-permute-start
  62.3 1.2 collective-permute-done.got_ref
  63.5 0.0 copy-done.6
  63.5 2.8 %level1.1 = (f32[64,6656]{1,0:T(8,128)}, bf16[8,2,72,128]{3,2,1,0:T(8,128)(2,1)S(1)}) custom-call(s32[2]{0:T(128)S(1)} %copy-done.8, bf16[2,72,256]{2,1,0:T(8,128)(2,1)S(1)} %collective-permute-done.got_ref, f32[2,64,1024]{2,1,0:T(8,128)S(1)} %get-tuple-element.21.rhs_ref, s32[2,512]{1,0:T(2,128)S(1)} %copy-done.6, ...), custom_call_target="tpu_custom_call", output_to_operand_aliasing={{0}: (6, {})} | custom-call | tf_op jit(solution)/shard_map/level1/pallas_call | solution.py:451
  66.3 0.0 copy-start.1
  66.3 0.0 copy-start.4
  66.3 0.0 copy-start.9
  66.3 10.9 %all_to_all.20.got_ref = bf16[8,2,72,128]{3,2,1,0:T(8,128)(2,1)S(1)} all-to-all(bf16[8,2,72,128]{3,2,1,0:T(8,128)(2,1)S(1)} %get-tuple-element.25), channel_id=1, replica_groups=mesh['z'=4,'x1'=2,'x0'=2,'core'=2,'front'=4] {'x0','front'}, dimensions={0} | all-to-all | bytes 589824 | tf_op jit(solution)/shard_map/all_to_all | solution.py:362
  77.2 1.1 sum2.1
  78.4 14.3 %all-gather = bf16[256,1536]{1,0:T(8,128)(2,1)S(1)} all-gather(bf16[64,1536]{1,0:T(8,128)(2,1)S(1)} %sum2.1), channel_id=2, replica_groups=mesh['z'=4,'x1'=2,'x0'=2,'core'=2,'front'=4] {'front'}, dimensions={0}, use_global_device_ids=true | all-gather | bytes 983040 | tf_op jit(solution)/shard_map/all_gather | solution.py:481
  92.7 0.0 slice-done
  92.7 0.0 copy-start
  92.8 3.0 %level2.1 = (f32[64,6656]{1,0:T(8,128)}, bf16[8,3,72,128]{3,2,1,0:T(8,128)(2,1)S(1)}) custom-call(s32[4]{0:T(128)S(1)} %copy-done.9, bf16[4,64,1536]{2,1,0:T(8,128)(2,1)S(1)} %bitcast.14, s32[4,768]{1,0:T(4,128)S(1)} %copy-done.4, bf16[4,1536,384]{2,1,0:T(8,128)(2,1)S(1)} %bitcast.12, ...), custom_call_target="tpu_custom_call", output_to_operand_aliasing={{0}: (5, {})} | custom-call | tf_op jit(solution)/shard_map/level2/pallas_call | solution.py:482
  95.7 13.7 %all_to_all.21.got_ref = bf16[8,3,72,128]{3,2,1,0:T(8,128)(2,1)S(1)} all-to-all(bf16[8,3,72,128]{3,2,1,0:T(8,128)(2,1)S(1)} %get-tuple-element.28), channel_id=1, replica_groups=mesh['z'=4,'x1'=2,'x0'=2,'core'=2,'front'=4] {'x1','front'}, dimensions={0} | all-to-all | bytes 884736 | tf_op jit(solution)/shard_map/all_to_all | solution.py:362
  109.4 0.4 sum3.1
  109.8 12.8 %all-gather.1 = bf16[256,1024]{1,0:T(8,128)(2,1)S(1)} all-gather(bf16[64,1024]{1,0:T(8,128)(2,1)S(1)} %sum3.1), channel_id=3, replica_groups=mesh['z'=4,'x1'=2,'x0'=2,'core'=2,'front'=4] {'front'}, dimensions={0}, use_global_device_ids=true | all-gather | bytes 655360 | tf_op jit(solution)/shard_map/all_gather | solution.py:516
  122.6 0.0 copy-done
  122.6 1.5 %level3.1 = f32[64,6656]{1,0:T(8,128)} custom-call(bf16[4,64,1024]{2,1,0:T(8,128)(2,1)S(1)} %bitcast.15, bf16[2,2048,512]{2,1,0:T(8,128)(2,1)S(1)} %copy-done, f32[64,6656]{1,0:T(8,128)} %get-tuple-element.30.out_in), custom_call_target="tpu_custom_call", output_to_operand_aliasing={{}: (2, {})} | custom-call | tf_op jit(solution)/shard_map/level3/pallas_call | solution.py:517
  (13 shorter events, 0.0 us)
Async XLA Ops:
  0.0 0.7 copy-start.3
  4.0 20.4 %all-to-all-start = ((s32[128,1,128]{2,1,0:T(1,128)}), s32[128,1,128]{2,1,0:T(1,128)S(1)}, u32[]{:S(2)}, u32[]{:S(2)}) async-start(s32[128,1,128]{2,1,0:T(1,128)} %bitcast.4), calls=%async_computation | async-start | bytes 131072 | tf_op jit(solution)/shard_map/all_to_all | solution.py:362
  15.1 1.5 %copy-start.2 = (f32[64,6656]{1,0:T(8,128)S(1)}, f32[64,6656]{1,0:T(8,128)}, u32[]{:S(2)}) copy-start(f32[64,6656]{1,0:T(8,128)} %wide_ref.1) | copy-start | bytes 5111812
  24.4 29.4 %copy-start.5 = (s32[4,256]{1,0:T(4,128)S(1)}, s32[4,256]{1,0:T(4,128)}, u32[]{:S(2)}) copy-start(s32[4,256]{1,0:T(4,128)} %rows_ref.3) | copy-start | bytes 12292
  24.4 29.4 %copy-start.7 = (s32[4]{0:T(128)S(1)}, s32[4]{0:T(128)}, u32[]{:S(2)}) copy-start(s32[4]{0:T(128)} %parent_ref.3) | copy-start | bytes 52
  32.4 21.3 %all-to-all-start.1 = ((bf16[128,13,2,128]{3,2,1,0:T(2,128)(2,1)}), bf16[128,13,2,128]{3,2,1,0:T(2,128)(2,1)S(1)}, u32[]{:S(2)}, u32[]{:S(2)}) async-start(bf16[128,13,2,128]{3,2,1,0:T(2,128)(2,1)} %bitcast.18), calls=%async_computation.1 | async-start | bytes 1703936 | tf_op jit(solution)/shard_map/all_to_all | solution.py:362
  53.7 9.8 %copy-start.6 = (s32[2,512]{1,0:T(2,128)S(1)}, s32[2,512]{1,0:T(2,128)}, u32[]{:S(2)}) copy-start(s32[2,512]{1,0:T(2,128)} %rows_ref.4) | copy-start | bytes 12292
  53.7 9.8 %copy-start.8 = (s32[2]{0:T(128)S(1)}, s32[2]{0:T(128)}, u32[]{:S(2)}) copy-start(s32[2]{0:T(128)} %parent_ref.4) | copy-start | bytes 28
  62.1 1.3 %collective-permute-start = (bf16[2,72,256]{2,1,0:T(8,128)(2,1)S(1)}, bf16[2,72,256]{2,1,0:T(8,128)(2,1)S(1)}, u32[]{:S(2)}, u32[]{:S(2)}) collective-permute-start(bf16[2,72,256]{2,1,0:T(8,128)(2,1)S(1)} %get-tuple-element.20), channel_id=1, source_target_pairs={{0,4},{4,0},{1,5},{5,1},{2,6},{6,2},{3,7},{7,3},{8,12},{12,8},{9,1... | collective-permute-start | bytes 221192 | tf_op jit(solution)/shard_map/ppermute | solution.py:450
  63.5 29.2 %slice-start = ((s8[4718592]{0:T(1024)(128)(4,1)}), s8[4194304]{0:T(1024)(128)(4,1)S(1)}, s32[]{:S(2)}) async-start(s8[4718592]{0:T(1024)(128)(4,1)} %bitcast.11), calls=%async_computation.4 | async-start | bytes 8388608
  63.5 29.2 %slice-start.1 = ((s8[4718592]{0:T(1024)(128)(4,1)}), s8[524288]{0:T(1024)(128)(4,1)S(1)}, s32[]{:S(2)}) async-start(s8[4718592]{0:T(1024)(128)(4,1)} %bitcast.11), calls=%async_computation.5 | async-start | bytes 1048576
  66.3 26.5 %copy-start.1 = (bf16[4,384,768]{2,1,0:T(8,128)(2,1)S(1)}, bf16[4,384,768]{2,1,0:T(8,128)(2,1)}, u32[]{:S(2)}) copy-start(bf16[4,384,768]{2,1,0:T(8,128)(2,1)} %update_ref.1) | copy-start | bytes 7077892
  66.3 26.4 %copy-start.4 = (s32[4,768]{1,0:T(4,128)S(1)}, s32[4,768]{1,0:T(4,128)}, u32[]{:S(2)}) copy-start(s32[4,768]{1,0:T(4,128)} %rows_ref.5) | copy-start | bytes 36868
  66.3 26.4 %copy-start.9 = (s32[4]{0:T(128)S(1)}, s32[4]{0:T(128)}, u32[]{:S(2)}) copy-start(s32[4]{0:T(128)} %parent_ref.5) | copy-start | bytes 52
  92.7 29.9 %copy-start = (bf16[2,2048,512]{2,1,0:T(8,128)(2,1)S(1)}, bf16[2,2048,512]{2,1,0:T(8,128)(2,1)}, u32[]{:S(2)}) copy-start(bf16[2,2048,512]{2,1,0:T(8,128)(2,1)} %inverse_ref.3) | copy-start | bytes 12582916

commit v4 on v3

--- a/solution.py
+++ b/solution.py
@@ -21,6 +21,7 @@
 BLOCKS = ROWS // LANES
 PAIRS = DEVICES * HALF
 GROUP = 4
+CHUNKS = 4
 EDGE0 = LEAVES * LEAF
 EDGE1 = EDGE0 + NODES1 * SEP1
 EDGE2 = EDGE1 + NODES2 * SHARE2
@@ -85,26 +86,43 @@
     return m[0:1], m[1:2], m[2:3]
 
 
-def tall_kernel(wide_ref, tall_ref):
+def tall_kernel(wide_hbm, tall_ref, wide_ref, sems):
+    loads = []
     for b in range(ROWS // 512):
-        wide = wide_ref[:, b * 512 : (b + 1) * 512]
-        tall_ref[b * 512 : (b + 1) * 512, :] = jnp.concatenate([wide, wide], axis=0).T
-
-
-def pick_kernel(asked_ref, tall_ref, out_hbm, buf, narrow, sem):
+        part = slice(b * 512, (b + 1) * 512)
+        loads.append(
+            pltpu.make_async_copy(wide_hbm.at[:, part], wide_ref.at[:, part], sems.at[b])
+        )
+        loads[b].start()
+    for b in range(ROWS // 512):
+        part = slice(b * 512, (b + 1) * 512)
+        loads[b].wait()
+        wide = wide_ref[:, part]
+        tall_ref[part, :] = jnp.concatenate([wide, wide], axis=0).T
+
+
+def pick_kernel(asked_ref, tall_ref, out_hbm, buf, narrow, asked, sems, sem):
     low = lax.broadcasted_iota(i32, (1, 128), 1) < RHS
+    step = DEVICES // CHUNKS
+    loads = []
+    for c in range(CHUNKS):
+        part = slice(c * step, (c + 1) * step)
+        loads.append(pltpu.make_async_copy(asked_ref.at[part], asked.at[part], sems.at[c]))
+        loads[c].start()
 
     def gather(g, carry):
         base = pl.multiple_of(g * (GROUP * HALF), 8)
         for e in range(GROUP):
             d = g * GROUP + e
             for k in range(HALF):
-                first = tall_ref[pl.ds(asked_ref[d, k], 1), :]
-                second = tall_ref[pl.ds(asked_ref[d, k + HALF], 1), :]
+                first = tall_ref[pl.ds(asked[d, k], 1), :]
+                second = tall_ref[pl.ds(asked[d, k + HALF], 1), :]
                 buf[pl.ds(base + (e * HALF + k), 1), :] = jnp.where(low, first, second)
         return carry
 
-    lax.fori_loop(0, DEVICES // GROUP, gather, 0)
+    for c in range(CHUNKS):
+        loads[c].wait()
+        lax.fori_loop(c * step // GROUP, (c + 1) * step // GROUP, gather, 0)
     narrow[...] = buf[...].astype(bf16)
     store = pltpu.make_async_copy(narrow, out_hbm, sem)
     store.start()
@@ -139,15 +157,18 @@
     asked_ref[...] = (asked * LANES + pltpu.roll(asked, 64, 1)).astype(i32)
 
 
-def restore(slot_ref, arrived_ref, both, tall_ref):
+def restore(slot_ref, arrived_ref, both, tall_ref, slots, sem):
+    load = pltpu.make_async_copy(slot_ref, slots, sem)
+    load.start()
     piece = arrived_ref[...].astype(f32)
     both[0:PAIRS, :] = piece
     both[PAIRS : 2 * PAIRS, :] = pltpu.roll(piece, RHS, 1)
+    load.wait()
 
     def gather(r, carry):
         base = pl.multiple_of(r * LANES, LANES)
         for k in range(LANES):
-            tall_ref[pl.ds(base + k, 1), :] = both[pl.ds(slot_ref[r, k], 1), :]
+            tall_ref[pl.ds(base + k, 1), :] = both[pl.ds(slots[r, k], 1), :]
         return carry
 
     lax.fori_loop(0, BLOCKS, gather, 0)
@@ -172,6 +193,7 @@
     update1_ref,
     both,
     tall,
+    slots,
     inverse_ref,
     update_ref,
     sol_ref,
@@ -187,7 +209,7 @@
     load_update.start()
     load_inverse1.start()
     load_update1.start()
-    restore(slot_ref, arrived_ref, both, tall)
+    restore(slot_ref, arrived_ref, both, tall, slots, sems.at[5])
     load_inverse.wait()
     load_update.wait()
     sols, terms = [], []
@@ -347,12 +369,18 @@
     out_ref[...] = (rhs_ref[...] - total).astype(bf16)
 
 
-def level3_kernel(rhs_ref, inverse_ref, out_in, out_hbm, sol_ref, sem):
+def level3_kernel(
+    where_ref, own_ref, first_ref, second_ref, third_ref, inverse_ref, out_in, out_hbm, sol_ref, sem
+):
     del out_in
+    front = where_ref[2]
     for c in range(NODES3):
         own = slice(c * SHARE3, (c + 1) * SHARE3)
-        lhs = jnp.concatenate([rhs_ref[g, :, own] for g in range(FRONT)], axis=1)
-        sol_ref[:, own] = mm(lhs, inverse_ref[c])
+        sol = jnp.zeros((RHS, SHARE3), f32)
+        for k, piece in enumerate((own_ref, first_ref, second_ref, third_ref)):
+            at = pl.multiple_of(((front + FRONT - k) & (FRONT - 1)) * SHARE3, SHARE3)
+            sol = sol + mm(piece[:, own], inverse_ref[c, pl.ds(at, SHARE3), :])
+        sol_ref[:, own] = sol
     store = pltpu.make_async_copy(sol_ref, out_hbm.at[:, EDGE2:ROWS], sem)
     store.start()
     store.wait()
@@ -379,7 +407,7 @@
     level2_parent_node,
     level3_diagonal_inverse,
 ):
-    where = jnp.stack([lax.axis_index("core"), lax.axis_index("x0")]).astype(i32)
+    where = jnp.stack([lax.axis_index(a) for a in ("core", "x0", "front")]).astype(i32)
     requests, slot = pl.pallas_call(
         rank_kernel,
         in_specs=[VMEM],
@@ -391,20 +419,26 @@
     asked = exchange(requests.reshape(DEVICES, 1, LANES), ALL).reshape(DEVICES, LANES)
     tall = pl.pallas_call(
         tall_kernel,
-        in_specs=[VMEM],
+        in_specs=[HBM],
         out_specs=VMEM,
         out_shape=struct((ROWS, 128), f32),
+        scratch_shapes=[
+            pltpu.VMEM((RHS, ROWS), f32),
+            pltpu.SemaphoreType.DMA((ROWS // 512,)),
+        ],
         compiler_params=params(8),
         name="tall",
-    )(right_hand_sides)
+    )(in_hbm(right_hand_sides))
     picked = pl.pallas_call(
         pick_kernel,
-        in_specs=[SMEM, VMEM],
+        in_specs=[VMEM, VMEM],
         out_specs=HBM,
         out_shape=pltpu.HBM((DEVICES * HALF, 128), bf16),
         scratch_shapes=[
             pltpu.VMEM((DEVICES * HALF, 128), f32),
             pltpu.VMEM((DEVICES * HALF, 128), bf16),
+            pltpu.SMEM((DEVICES, LANES), i32),
+            pltpu.SemaphoreType.DMA((CHUNKS,)),
             pltpu.SemaphoreType.DMA,
         ],
         compiler_params=params(16),
@@ -413,7 +447,7 @@
     arrived = exchange(picked.reshape(DEVICES, HALF // 2, 2, 128), ALL)
     out, send0, rhs1, rhs2, rhs3, inverse1, update1 = pl.pallas_call(
         leaf_kernel,
-        in_specs=[SMEM, SMEM, SMEM, VMEM, VMEM, HBM, HBM, HBM, HBM],
+        in_specs=[VMEM, SMEM, SMEM, VMEM, VMEM, HBM, HBM, HBM, HBM],
         out_specs=[HBM, VMEM, VMEM, VMEM, VMEM, VMEM, VMEM],
         out_shape=[
             struct((RHS, ROWS), f32),
@@ -427,12 +461,13 @@
         scratch_shapes=[
             pltpu.VMEM((2 * PAIRS, 128), f32),
             pltpu.VMEM((ROWS, 128), f32),
+            pltpu.SMEM((BLOCKS, LANES), i32),
             pltpu.VMEM((LEAVES, LEAF, LEAF), bf16),
             pltpu.VMEM((LEAVES, LEAF, BORDER0), bf16),
             pltpu.VMEM((RHS, EDGE0), f32),
             pltpu.VMEM((NODES1, RHS, BORDER0), bf16),
             pltpu.VMEM((NODES1, 8, BORDER0), i32),
-            pltpu.SemaphoreType.DMA((5,)),
+            pltpu.SemaphoreType.DMA((6,)),
         ],
         compiler_params=params(24),
         name="leaf",
@@ -513,17 +548,20 @@
         compiler_params=params(24),
         name="sum3",
     )(got2, rhs3)
-    all3 = lax.all_gather(side3, "front", axis=0, tiled=False)
+    pieces = [
+        lax.ppermute(side3, "front", [(f, (f + k) % FRONT) for f in range(FRONT)])
+        for k in range(1, FRONT)
+    ]
     return pl.pallas_call(
         level3_kernel,
-        in_specs=[VMEM, VMEM, HBM],
+        in_specs=[SMEM, VMEM, VMEM, VMEM, VMEM, VMEM, HBM],
         out_specs=HBM,
         out_shape=struct((RHS, ROWS), f32),
         scratch_shapes=[pltpu.VMEM((RHS, NODES3 * SHARE3), f32), pltpu.SemaphoreType.DMA],
-        input_output_aliases={2: 0},
+        input_output_aliases={6: 0},
         compiler_params=params(24),
         name="level3",
-    )(all3, level3_diagonal_inverse, out)
+    )(where, side3, *pieces, level3_diagonal_inverse, out)
 
 
 def solution(mesh):

time: 125 us -> 121 us (0.968)
  blocking collectives: 51.7 us -> 39 us
  waiting for transfers between devices: 24.6 us -> 30.4 us
  starting transfers between devices: 16 us -> 18.7 us
  Pallas kernels: 29.4 us -> 31.4 us
  local copies, waits for them, and re-layouts: 2.24 us -> 0.79 us
    all_gather x1 -> x0, blocking collectives: 12.8 us -> none  [per_device(): all3 = lax.all_gather(side3, 'front', axis=0, tiled=False)]
    ppermute x0 -> x3, waiting for transfers between devices: none -> 6.22 us  [per_device(): lax.ppermute(side3, 'front', [(f, (f + k) % FRONT) for f in range(FRONT)])]
    ppermute x0 -> x3, starting transfers between devices: none -> 2.72 us  [per_device(): lax.ppermute(side3, 'front', [(f, (f + k) % FRONT) for f in range(FRONT)])]
    pallas_call x4, Pallas kernels: 18.9 us -> 20.9 us  [the longest x1 8.78 us: per_device(): pl.pallas_call(leaf_kernel, in_specs=[VMEM, SMEM, SMEM, VMEM, VMEM, HBM,...]
    unnamed x24 -> x22, local copies, waits for them, and re-layouts: 2.24 us -> 0.79 us
  transfers between devices with their start and end apart: 3 -> 6, of which waited for: 3 -> 6; matrix products, arithmetic and copies ran while one was open for 0% -> 0% of each run, Pallas kernels for 1% -> 2%
where the time goes in v4:
time: 121 us
  blocking collectives  39 us (32%)
  Pallas kernels  31.4 us (26%)
  waiting for transfers between devices  30.4 us (25%)
  starting transfers between devices  18.7 us (15%)
    all_to_all x2, blocking collectives, exchange(): return lax.all_to_all(block, axes, split_axis=0, concat_axis=0, tiled=True)  24.6 us
    all_to_all x2, waiting for transfers between devices, exchange(): return lax.all_to_all(block, axes, split_axis=0, concat_axis=0, tiled=True)  23 us
    all_to_all x2, starting transfers between devices, exchange(): return lax.all_to_all(block, axes, split_axis=0, concat_axis=0, tiled=True)  15.8 us
    all_gather x1, blocking collectives, per_device(): all2 = lax.all_gather(side2, 'front', axis=0, tiled=False)  14.3 us
    pallas_call x1, Pallas kernels, per_device(): pl.pallas_call(leaf_kernel, in_specs=[VMEM, SMEM, SMEM, VMEM, VMEM, HBM,...  8.78 us
    pallas_call x1, Pallas kernels, per_device(): pl.pallas_call(pick_kernel, in_specs=[VMEM, VMEM], out_specs=HBM, out_sha...  7.26 us
    ppermute x3, waiting for transfers between devices, per_device(): lax.ppermute(side3, 'front', [(f, (f + k) % FRONT) for f in range(FRONT)])  6.22 us
    pallas_call x1, Pallas kernels, per_device(): pl.pallas_call(rank_kernel, in_specs=[VMEM], out_specs=[VMEM, VMEM], out_...  3.23 us
  transfers between devices with their start and end apart: 6, of which 6 were waited for; matrix products, arithmetic and copies ran while one was open for 0% of the time, Pallas kernels for 2%

profile of v4, /device:TPU:0, one launch (start us, length us, event | category | flops | bytes accessed | tf_op | source)
XLA Modules:
  0.0 120.5 jit_solution(8219241089538539086)
XLA Ops:
  0.0 0.7 copy-done.2
  0.7 3.2 %rank.1 = (s32[128,128]{1,0:T(8,128)}, s32[52,128]{1,0:T(8,128)S(1)}) custom-call(s32[52,128]{1,0:T(8,128)S(1)} %bitcast.16), custom_call_target="tpu_custom_call" | custom-call | tf_op jit(solution)/shard_map/rank/pallas_call | solution.py:411
  4.0 11.1 %all-to-all-start = ((s32[128,1,128]{2,1,0:T(1,128)}), s32[128,1,128]{2,1,0:T(1,128)S(1)}, u32[]{:S(2)}, u32[]{:S(2)}) async-start(s32[128,1,128]{2,1,0:T(1,128)} %bitcast.5), calls=%async_computation | async-start | bytes 131072 | tf_op jit(solution)/shard_map/all_to_all | solution.py:390
  15.1 2.8 %tall.1.tall_ref = f32[6656,128]{1,0:T(8,128)S(1)} custom-call(f32[64,6656]{1,0:T(8,128)} %wide_hbm.1), custom_call_target="tpu_custom_call" | custom-call | tf_op jit(solution)/shard_map/tall/pallas_call | solution.py:420
  17.9 6.5 %all-to-all-done = s32[128,1,128]{2,1,0:T(1,128)S(1)} async-done(((s32[128,1,128]{2,1,0:T(1,128)}), s32[128,1,128]{2,1,0:T(1,128)S(1)}, u32[]{:S(2)}, u32[]{:S(2)}) %all-to-all-start) | async-done | bytes 65568 | tf_op jit(solution)/shard_map/all_to_all | solution.py:390
  24.4 7.3 %pick.1 = bf16[3328,128]{1,0:T(8,128)(2,1)} custom-call(s32[128,128]{1,0:T(8,128)S(1)} %bitcast.15, f32[6656,128]{1,0:T(8,128)S(1)} %tall.1.tall_ref), custom_call_target="tpu_custom_call" | custom-call | tf_op jit(solution)/shard_map/pick/pallas_call | solution.py:432
  31.6 4.6 %all-to-all-start.1 = ((bf16[128,13,2,128]{3,2,1,0:T(2,128)(2,1)}), bf16[128,13,2,128]{3,2,1,0:T(2,128)(2,1)S(1)}, u32[]{:S(2)}, u32[]{:S(2)}) async-start(bf16[128,13,2,128]{3,2,1,0:T(2,128)(2,1)} %bitcast.17), calls=%async_computation.1 | async-start | bytes 1703936 | tf_op jit(solution)/shard_map/all_to_all | solution.py:390
  36.3 0.1 pad_add_fusion.where_ref
  36.4 16.6 %all-to-all-done.1 = bf16[128,13,2,128]{3,2,1,0:T(2,128)(2,1)S(1)} async-done(((bf16[128,13,2,128]{3,2,1,0:T(2,128)(2,1)}), bf16[128,13,2,128]{3,2,1,0:T(2,128)(2,1)S(1)}, u32[]{:S(2)}, u32[]{:S(2)}) %all-to-all-start.1) | async-done | bytes 852000 | tf_op jit(solution)/shard_map/all_to_all | solution.py:390
  53.0 0.0 copy-done.4
  53.0 0.0 copy-done.6
  53.0 8.8 %leaf.1 = (f32[64,6656]{1,0:T(8,128)}, bf16[2,72,256]{2,1,0:T(8,128)(2,1)S(1)}, f32[2,64,1024]{2,1,0:T(8,128)S(1)}, f32[64,1536]{1,0:T(8,128)S(1)}, f32[64,1024]...) custom-call(s32[52,128]{1,0:T(8,128)S(1)} %get-tuple-element.18.slot_ref, ...), custom_call_target="tpu_custom_call" | custom-call | tf_op jit(solution)/shard_map/leaf/pallas_call | solution.py:448
  61.8 0.2 collective-permute-start
  62.0 1.2 collective-permute-done.got_ref
  63.1 2.8 %level1.1 = (f32[64,6656]{1,0:T(8,128)}, bf16[8,2,72,128]{3,2,1,0:T(8,128)(2,1)S(1)}) custom-call(s32[2]{0:T(128)S(1)} %copy-done.7, bf16[2,72,256]{2,1,0:T(8,128)(2,1)S(1)} %collective-permute-done.got_ref, f32[2,64,1024]{2,1,0:T(8,128)S(1)} %get-tuple-element.21.rhs_ref, s32[2,512]{1,0:T(2,128)S(1)} %copy-done.5, ...), custom_call_target="tpu_custom_call", output_to_operand_aliasing={{0}: (6, {})} | custom-call | tf_op jit(solution)/shard_map/level1/pallas_call | solution.py:486
  65.9 0.0 copy-start.1
  65.9 0.0 copy-start.3
  65.9 0.0 copy-start.8
  65.9 10.9 %all_to_all.20.got_ref = bf16[8,2,72,128]{3,2,1,0:T(8,128)(2,1)S(1)} all-to-all(bf16[8,2,72,128]{3,2,1,0:T(8,128)(2,1)S(1)} %get-tuple-element.25), channel_id=1, replica_groups=mesh['z'=4,'x1'=2,'x0'=2,'core'=2,'front'=4] {'x0','front'}, dimensions={0} | all-to-all | bytes 589824 | tf_op jit(solution)/shard_map/all_to_all | solution.py:390
  76.9 1.1 sum2.1
  78.0 14.3 %all-gather = bf16[256,1536]{1,0:T(8,128)(2,1)S(1)} all-gather(bf16[64,1536]{1,0:T(8,128)(2,1)S(1)} %sum2.1), channel_id=2, replica_groups=mesh['z'=4,'x1'=2,'x0'=2,'core'=2,'front'=4] {'front'}, dimensions={0}, use_global_device_ids=true | all-gather | bytes 983040 | tf_op jit(solution)/shard_map/all_gather | solution.py:516
  92.4 0.0 copy-start
  92.4 3.0 %level2.1 = (f32[64,6656]{1,0:T(8,128)}, bf16[8,3,72,128]{3,2,1,0:T(8,128)(2,1)S(1)}) custom-call(s32[4]{0:T(128)S(1)} %copy-done.8, bf16[4,64,1536]{2,1,0:T(8,128)(2,1)S(1)} %bitcast.14, s32[4,768]{1,0:T(4,128)S(1)} %copy-done.3, bf16[4,1536,384]{2,1,0:T(8,128)(2,1)S(1)} %bitcast.12, ...), custom_call_target="tpu_custom_call", output_to_operand_aliasing={{0}: (5, {})} | custom-call | tf_op jit(solution)/shard_map/level2/pallas_call | solution.py:517
  95.3 13.7 %all_to_all.21.got_ref = bf16[8,3,72,128]{3,2,1,0:T(8,128)(2,1)S(1)} all-to-all(bf16[8,3,72,128]{3,2,1,0:T(8,128)(2,1)S(1)} %get-tuple-element.28), channel_id=1, replica_groups=mesh['z'=4,'x1'=2,'x0'=2,'core'=2,'front'=4] {'x1','front'}, dimensions={0} | all-to-all | bytes 884736 | tf_op jit(solution)/shard_map/all_to_all | solution.py:390
  109.0 0.4 sum3.1.own_ref
  109.5 1.1 collective-permute-start.3
  110.5 1.6 %collective-permute-start.2 = (bf16[64,1024]{1,0:T(8,128)(2,1)S(1)}, bf16[64,1024]{1,0:T(8,128)(2,1)S(1)}, u32[]{:S(2)}, u32[]{:S(2)}) collective-permute-start(bf16[64,1024]{1,0:T(8,128)(2,1)S(1)} %sum3.1.own_ref), channel_id=1, source_target_pairs={{0,2},{1,3},{2,0},{3,1},{4,6},{5,7},{6,4},{7,5},{8,10},{9,11},{10,... | collective-permute-start | bytes 393224 | tf_op jit(solution)/shard_map/ppermute | solution.py:552
  112.2 0.0 collective-permute-start.1
  112.2 2.3 %collective-permute-done.3.third_ref = bf16[64,1024]{1,0:T(8,128)(2,1)S(1)} collective-permute-done((bf16[64,1024]{1,0:T(8,128)(2,1)S(1)}, bf16[64,1024]{1,0:T(8,128)(2,1)S(1)}, u32[]{:S(2)}, u32[]{:S(2)}) %collective-permute-start.3) | collective-permute-done | bytes 131104 | tf_op jit(solution)/shard_map/ppermute | solution.py:552
  114.5 2.5 %collective-permute-done.2.second_ref = bf16[64,1024]{1,0:T(8,128)(2,1)S(1)} collective-permute-done((bf16[64,1024]{1,0:T(8,128)(2,1)S(1)}, bf16[64,1024]{1,0:T(8,128)(2,1)S(1)}, u32[]{:S(2)}, u32[]{:S(2)}) %collective-permute-start.2) | collective-permute-done | bytes 131104 | tf_op jit(solution)/shard_map/ppermute | solution.py:552
  117.0 1.4 %collective-permute-done.1.first_ref = bf16[64,1024]{1,0:T(8,128)(2,1)S(1)} collective-permute-done((bf16[64,1024]{1,0:T(8,128)(2,1)S(1)}, bf16[64,1024]{1,0:T(8,128)(2,1)S(1)}, u32[]{:S(2)}, u32[]{:S(2)}) %collective-permute-start.1) | collective-permute-done | bytes 131104 | tf_op jit(solution)/shard_map/ppermute | solution.py:552
  118.4 2.1 %level3.1 = f32[64,6656]{1,0:T(8,128)} custom-call(s32[3]{0:T(128)S(1)} %pad_add_fusion.where_ref, bf16[64,1024]{1,0:T(8,128)(2,1)S(1)} %sum3.1.own_ref, bf16[64,1024]{1,0:T(8,128)(2,1)S(1)} %collective-permute-done.1.first_ref, bf16[64,1024]{1,0:T(8,128)(2,1)S(1)} %collective-permute-done.2.second_ref, ...), custom_call_target="tpu_custom_call", output_to_operand_aliasing={{}: (6, {})} | custom-call | tf_op jit(solution)/shard_map/level3/pallas_call | solution.py:555
  (16 shorter events, 0.0 us)
Async XLA Ops:
  0.0 0.7 copy-start.2
  4.0 20.4 %all-to-all-start = ((s32[128,1,128]{2,1,0:T(1,128)}), s32[128,1,128]{2,1,0:T(1,128)S(1)}, u32[]{:S(2)}, u32[]{:S(2)}) async-start(s32[128,1,128]{2,1,0:T(1,128)} %bitcast.5), calls=%async_computation | async-start | bytes 131072 | tf_op jit(solution)/shard_map/all_to_all | solution.py:390
  24.4 28.6 %copy-start.4 = (s32[4,256]{1,0:T(4,128)S(1)}, s32[4,256]{1,0:T(4,128)}, u32[]{:S(2)}) copy-start(s32[4,256]{1,0:T(4,128)} %rows_ref.3) | copy-start | bytes 12292
  24.4 28.6 %copy-start.6 = (s32[4]{0:T(128)S(1)}, s32[4]{0:T(128)}, u32[]{:S(2)}) copy-start(s32[4]{0:T(128)} %parent_ref.3) | copy-start | bytes 52
  31.6 21.3 %all-to-all-start.1 = ((bf16[128,13,2,128]{3,2,1,0:T(2,128)(2,1)}), bf16[128,13,2,128]{3,2,1,0:T(2,128)(2,1)S(1)}, u32[]{:S(2)}, u32[]{:S(2)}) async-start(bf16[128,13,2,128]{3,2,1,0:T(2,128)(2,1)} %bitcast.17), calls=%async_computation.1 | async-start | bytes 1703936 | tf_op jit(solution)/shard_map/all_to_all | solution.py:390
  53.0 10.1 %copy-start.5 = (s32[2,512]{1,0:T(2,128)S(1)}, s32[2,512]{1,0:T(2,128)}, u32[]{:S(2)}) copy-start(s32[2,512]{1,0:T(2,128)} %rows_ref.4) | copy-start | bytes 12292
  53.0 10.1 %copy-start.7 = (s32[2]{0:T(128)S(1)}, s32[2]{0:T(128)}, u32[]{:S(2)}) copy-start(s32[2]{0:T(128)} %parent_ref.4) | copy-start | bytes 28
  61.8 1.3 %collective-permute-start = (bf16[2,72,256]{2,1,0:T(8,128)(2,1)S(1)}, bf16[2,72,256]{2,1,0:T(8,128)(2,1)S(1)}, u32[]{:S(2)}, u32[]{:S(2)}) collective-permute-start(bf16[2,72,256]{2,1,0:T(8,128)(2,1)S(1)} %get-tuple-element.20), channel_id=1, source_target_pairs={{0,4},{4,0},{1,5},{5,1},{2,6},{6,2},{3,7},{7,3},{8,12},{12,8},{9,1... | collective-permute-start | bytes 221192 | tf_op jit(solution)/shard_map/ppermute | solution.py:485
  63.1 29.2 %slice-start = ((s8[4718592]{0:T(1024)(128)(4,1)}), s8[4194304]{0:T(1024)(128)(4,1)S(1)}, s32[]{:S(2)}) async-start(s8[4718592]{0:T(1024)(128)(4,1)} %bitcast.11), calls=%async_computation.4 | async-start | bytes 8388608
  63.1 29.2 %slice-start.1 = ((s8[4718592]{0:T(1024)(128)(4,1)}), s8[524288]{0:T(1024)(128)(4,1)S(1)}, s32[]{:S(2)}) async-start(s8[4718592]{0:T(1024)(128)(4,1)} %bitcast.11), calls=%async_computation.5 | async-start | bytes 1048576
  65.9 26.4 %copy-start.1 = (bf16[4,384,768]{2,1,0:T(8,128)(2,1)S(1)}, bf16[4,384,768]{2,1,0:T(8,128)(2,1)}, u32[]{:S(2)}) copy-start(bf16[4,384,768]{2,1,0:T(8,128)(2,1)} %update_ref.1) | copy-start | bytes 7077892
  65.9 26.4 %copy-start.3 = (s32[4,768]{1,0:T(4,128)S(1)}, s32[4,768]{1,0:T(4,128)}, u32[]{:S(2)}) copy-start(s32[4,768]{1,0:T(4,128)} %rows_ref.5) | copy-start | bytes 36868
  65.9 26.4 %copy-start.8 = (s32[4]{0:T(128)S(1)}, s32[4]{0:T(128)}, u32[]{:S(2)}) copy-start(s32[4]{0:T(128)} %parent_ref.5) | copy-start | bytes 52
  92.4 26.1 %copy-start = (bf16[2,2048,512]{2,1,0:T(8,128)(2,1)S(1)}, bf16[2,2048,512]{2,1,0:T(8,128)(2,1)}, u32[]{:S(2)}) copy-start(bf16[2,2048,512]{2,1,0:T(8,128)(2,1)} %inverse_ref.3) | copy-start | bytes 12582916
  109.5 5.0 %collective-permute-start.3 = (bf16[64,1024]{1,0:T(8,128)(2,1)S(1)}, bf16[64,1024]{1,0:T(8,128)(2,1)S(1)}, u32[]{:S(2)}, u32[]{:S(2)}) collective-permute-start(bf16[64,1024]{1,0:T(8,128)(2,1)S(1)} %sum3.1.own_ref), channel_id=1, source_target_pairs={{0,3},{1,0},{2,1},{3,2},{4,7},{5,4},{6,5},{7,6},{8,11},{9,8},{10,9... | collective-permute-start | bytes 393224 | tf_op jit(solution)/shard_map/ppermute | solution.py:552
  110.5 6.5 %collective-permute-start.2 = (bf16[64,1024]{1,0:T(8,128)(2,1)S(1)}, bf16[64,1024]{1,0:T(8,128)(2,1)S(1)}, u32[]{:S(2)}, u32[]{:S(2)}) collective-permute-start(bf16[64,1024]{1,0:T(8,128)(2,1)S(1)} %sum3.1.own_ref), channel_id=1, source_target_pairs={{0,2},{1,3},{2,0},{3,1},{4,6},{5,7},{6,4},{7,5},{8,10},{9,11},{10,... | collective-permute-start | bytes 393224 | tf_op jit(solution)/shard_map/ppermute | solution.py:552
  112.2 6.2 %collective-permute-start.1 = (bf16[64,1024]{1,0:T(8,128)(2,1)S(1)}, bf16[64,1024]{1,0:T(8,128)(2,1)S(1)}, u32[]{:S(2)}, u32[]{:S(2)}) collective-permute-start(bf16[64,1024]{1,0:T(8,128)(2,1)S(1)} %sum3.1.own_ref), channel_id=1, source_target_pairs={{0,1},{1,2},{2,3},{3,0},{4,5},{5,6},{6,7},{7,4},{8,9},{9,10},{10,1... | collective-permute-start | bytes 393224 | tf_op jit(solution)/shard_map/ppermute | solution.py:552

commit v5 on v3

--- a/solution.py
+++ b/solution.py
@@ -1,3 +1,5 @@
+import functools
+
 import jax
 import jax.numpy as jnp
 from jax import lax
@@ -21,6 +23,7 @@
 BLOCKS = ROWS // LANES
 PAIRS = DEVICES * HALF
 GROUP = 4
+CHUNKS = 4
 EDGE0 = LEAVES * LEAF
 EDGE1 = EDGE0 + NODES1 * SEP1
 EDGE2 = EDGE1 + NODES2 * SHARE2
@@ -91,20 +94,28 @@
         tall_ref[b * 512 : (b + 1) * 512, :] = jnp.concatenate([wide, wide], axis=0).T
 
 
-def pick_kernel(asked_ref, tall_ref, out_hbm, buf, narrow, sem):
+def pick_kernel(asked_ref, tall_ref, out_hbm, buf, narrow, asked, sems, sem):
     low = lax.broadcasted_iota(i32, (1, 128), 1) < RHS
+    step = DEVICES // CHUNKS
+    loads = []
+    for c in range(CHUNKS):
+        part = slice(c * step, (c + 1) * step)
+        loads.append(pltpu.make_async_copy(asked_ref.at[part], asked.at[part], sems.at[c]))
+        loads[c].start()
 
     def gather(g, carry):
         base = pl.multiple_of(g * (GROUP * HALF), 8)
         for e in range(GROUP):
             d = g * GROUP + e
             for k in range(HALF):
-                first = tall_ref[pl.ds(asked_ref[d, k], 1), :]
-                second = tall_ref[pl.ds(asked_ref[d, k + HALF], 1), :]
+                first = tall_ref[pl.ds(asked[d, k], 1), :]
+                second = tall_ref[pl.ds(asked[d, k + HALF], 1), :]
                 buf[pl.ds(base + (e * HALF + k), 1), :] = jnp.where(low, first, second)
         return carry
 
-    lax.fori_loop(0, DEVICES // GROUP, gather, 0)
+    for c in range(CHUNKS):
+        loads[c].wait()
+        lax.fori_loop(c * step // GROUP, (c + 1) * step // GROUP, gather, 0)
     narrow[...] = buf[...].astype(bf16)
     store = pltpu.make_async_copy(narrow, out_hbm, sem)
     store.start()
@@ -123,7 +134,7 @@
     devices = lax.broadcasted_iota(i32, (DEVICES, LANES), 0).astype(f32)
     ranks = lax.broadcasted_iota(i32, (64, LANES), 0).astype(f32)
     seen = jnp.zeros((DEVICES, LANES), f32)
-    asked = jnp.zeros((DEVICES, LANES), f32)
+    mines, picks = [], []
     for b in range(BLOCKS):
         row = slice(b, b + 1)
         mine = jnp.where(devices == source[row], 1.0, 0.0)
@@ -133,24 +144,40 @@
         seen = seen + counts[:, LANES:]
         at = ranks == rank
         values = [jnp.where(at, high[row], 0.0), jnp.where(at, low[row], 0.0)]
-        asked = asked + mm_nt(mine16, jnp.concatenate(values, axis=0).astype(bf16))
+        mines.append(mine16)
+        picks.append(jnp.concatenate(values, axis=0).astype(bf16))
         slot = source[row] * HALF + jnp.where(rank < HALF, rank, rank + (PAIRS - HALF))
         slot_ref[row, :] = slot.astype(i32)
+    asked = mm_nt(jnp.concatenate(mines, axis=1), jnp.concatenate(picks, axis=1))
     asked_ref[...] = (asked * LANES + pltpu.roll(asked, 64, 1)).astype(i32)
 
 
-def restore(slot_ref, arrived_ref, both, tall_ref):
-    piece = arrived_ref[...].astype(f32)
-    both[0:PAIRS, :] = piece
-    both[PAIRS : 2 * PAIRS, :] = pltpu.roll(piece, RHS, 1)
-
+def restore(first, last, slot_ref, both_ref, tall_ref):
     def gather(r, carry):
-        base = pl.multiple_of(r * LANES, LANES)
+        base = pl.multiple_of((r - first // LANES) * LANES, LANES)
         for k in range(LANES):
-            tall_ref[pl.ds(base + k, 1), :] = both[pl.ds(slot_ref[r, k], 1), :]
+            tall_ref[pl.ds(base + k, 1), :] = both_ref[pl.ds(slot_ref[r, k], 1), :]
         return carry
 
-    lax.fori_loop(0, BLOCKS, gather, 0)
+    lax.fori_loop(first // LANES, last // LANES, gather, 0)
+
+
+def rhs_kernel(first, last, slot_ref, both_ref, after_ref, rhs_ref, tall):
+    del after_ref
+    restore(first, last, slot_ref, both_ref, tall)
+    rhs_ref[...] = tall[...].T[:RHS]
+
+
+def late_rhs(first, last, slot, both, after):
+    return pl.pallas_call(
+        functools.partial(rhs_kernel, first, last),
+        in_specs=[SMEM, VMEM, VMEM],
+        out_specs=VMEM,
+        out_shape=struct((RHS, last - first), f32),
+        scratch_shapes=[pltpu.VMEM((last - first, 128), f32)],
+        compiler_params=params(4),
+        name="rhs",
+    )(slot, both, after)
 
 
 def leaf_kernel(
@@ -166,11 +193,9 @@
     out_hbm,
     send_ref,
     rhs1_ref,
-    rhs2_ref,
-    rhs3_ref,
+    both,
     inverse1_ref,
     update1_ref,
-    both,
     tall,
     inverse_ref,
     update_ref,
@@ -187,7 +212,10 @@
     load_update.start()
     load_inverse1.start()
     load_update1.start()
-    restore(slot_ref, arrived_ref, both, tall)
+    piece = arrived_ref[...].astype(f32)
+    both[0:PAIRS, :] = piece
+    both[PAIRS : 2 * PAIRS, :] = pltpu.roll(piece, RHS, 1)
+    restore(0, EDGE1, slot_ref, both, tall)
     load_inverse.wait()
     load_update.wait()
     sols, terms = [], []
@@ -197,8 +225,6 @@
     for n in range(LEAVES):
         sol_ref[:, n * LEAF : (n + 1) * LEAF] = sols[n]
         terms.append(mm(sols[n].astype(bf16), update_ref[n]).astype(bf16))
-    rhs2_ref[...] = tall[EDGE1:EDGE2, :].T[:RHS]
-    rhs3_ref[...] = tall[EDGE2:ROWS, :].T[:RHS]
     core = where_ref[0]
     for n in range(LEAVES):
         node = parent_ref[n]
@@ -235,13 +261,14 @@
     rows_ref,
     inverse_ref,
     update_ref,
+    after_ref,
     out_in,
     out_hbm,
     send_ref,
     sol_ref,
     sem,
 ):
-    del out_in
+    del out_in, after_ref
     for n in range(NODES1):
         high, low, _ = undigits(got_ref[n, RHS : RHS + META, :])
         got = got_ref[n, 0:RHS, :].astype(f32)
@@ -282,21 +309,33 @@
     out_ref[...] = (rhs_ref[...] - total).astype(bf16)
 
 
+def gathered(front, pieces, rhs_ref):
+    for k, piece in enumerate(pieces):
+        rhs_ref[(front + FRONT - k) & (FRONT - 1)] = piece[...]
+
+
 def level2_kernel(
+    where_ref,
     parent_ref,
-    rhs_ref,
+    own_ref,
+    first_ref,
+    second_ref,
+    third_ref,
     rows_ref,
     inverse_ref,
     update_ref,
+    after_ref,
     out_in,
     out_hbm,
     send_ref,
     sol_ref,
     terms_ref,
     terms_rows,
+    rhs_ref,
     sem,
 ):
-    del out_in
+    del out_in, after_ref
+    gathered(where_ref[2], (own_ref, first_ref, second_ref, third_ref), rhs_ref)
     for c in range(NODES2):
         own = slice(c * SHARE2, (c + 1) * SHARE2)
         lhs = jnp.concatenate([rhs_ref[g, :, own] for g in range(FRONT)], axis=1)
@@ -347,8 +386,21 @@
     out_ref[...] = (rhs_ref[...] - total).astype(bf16)
 
 
-def level3_kernel(rhs_ref, inverse_ref, out_in, out_hbm, sol_ref, sem):
+def level3_kernel(
+    where_ref,
+    own_ref,
+    first_ref,
+    second_ref,
+    third_ref,
+    inverse_ref,
+    out_in,
+    out_hbm,
+    sol_ref,
+    rhs_ref,
+    sem,
+):
     del out_in
+    gathered(where_ref[2], (own_ref, first_ref, second_ref, third_ref), rhs_ref)
     for c in range(NODES3):
         own = slice(c * SHARE3, (c + 1) * SHARE3)
         lhs = jnp.concatenate([rhs_ref[g, :, own] for g in range(FRONT)], axis=1)
@@ -356,6 +408,13 @@
     store = pltpu.make_async_copy(sol_ref, out_hbm.at[:, EDGE2:ROWS], sem)
     store.start()
     store.wait()
+
+
+def front_pieces(side):
+    return [
+        lax.ppermute(side, "front", [(f, (f + k) % FRONT) for f in range(FRONT)])
+        for k in range(1, FRONT)
+    ]
 
 
 def exchange(block, axes):
@@ -379,7 +438,7 @@
     level2_parent_node,
     level3_diagonal_inverse,
 ):
-    where = jnp.stack([lax.axis_index("core"), lax.axis_index("x0")]).astype(i32)
+    where = jnp.stack([lax.axis_index(a) for a in ("core", "x0", "front")]).astype(i32)
     requests, slot = pl.pallas_call(
         rank_kernel,
         in_specs=[VMEM],
@@ -399,34 +458,34 @@
     )(right_hand_sides)
     picked = pl.pallas_call(
         pick_kernel,
-        in_specs=[SMEM, VMEM],
+        in_specs=[VMEM, VMEM],
         out_specs=HBM,
         out_shape=pltpu.HBM((DEVICES * HALF, 128), bf16),
         scratch_shapes=[
             pltpu.VMEM((DEVICES * HALF, 128), f32),
             pltpu.VMEM((DEVICES * HALF, 128), bf16),
+            pltpu.SMEM((DEVICES, LANES), i32),
+            pltpu.SemaphoreType.DMA((CHUNKS,)),
             pltpu.SemaphoreType.DMA,
         ],
         compiler_params=params(16),
         name="pick",
     )(asked, tall)
     arrived = exchange(picked.reshape(DEVICES, HALF // 2, 2, 128), ALL)
-    out, send0, rhs1, rhs2, rhs3, inverse1, update1 = pl.pallas_call(
+    out, send0, rhs1, both, inverse1, update1 = pl.pallas_call(
         leaf_kernel,
         in_specs=[SMEM, SMEM, SMEM, VMEM, VMEM, HBM, HBM, HBM, HBM],
-        out_specs=[HBM, VMEM, VMEM, VMEM, VMEM, VMEM, VMEM],
+        out_specs=[HBM, VMEM, VMEM, VMEM, VMEM, VMEM],
         out_shape=[
             struct((RHS, ROWS), f32),
             struct((NODES1, RHS + META, BORDER0), bf16),
             struct((NODES1, RHS, SEP1), f32),
-            struct((RHS, NODES2 * SHARE2), f32),
-            struct((RHS, NODES3 * SHARE3), f32),
+            struct((2 * PAIRS, 128), f32),
             struct((NODES1, SEP1, SEP1), bf16),
             struct((NODES1, SEP1, BORDER1), bf16),
         ],
         scratch_shapes=[
-            pltpu.VMEM((2 * PAIRS, 128), f32),
-            pltpu.VMEM((ROWS, 128), f32),
+            pltpu.VMEM((EDGE1, 128), f32),
             pltpu.VMEM((LEAVES, LEAF, LEAF), bf16),
             pltpu.VMEM((LEAVES, LEAF, BORDER0), bf16),
             pltpu.VMEM((RHS, EDGE0), f32),
@@ -448,16 +507,17 @@
         in_hbm(level1_update_block),
     )
     got0 = lax.ppermute(send0, "core", [(0, 1), (1, 0)])
+    rhs2 = late_rhs(EDGE1, EDGE2, slot, both, send0)
     out, send1 = pl.pallas_call(
         level1_kernel,
-        in_specs=[SMEM, VMEM, VMEM, VMEM, VMEM, VMEM, HBM],
+        in_specs=[SMEM] + [VMEM] * 6 + [HBM],
         out_specs=[HBM, VMEM],
         out_shape=[
             struct((RHS, ROWS), f32),
             struct((2 * FRONT, NODES1, RHS + META, PART1), bf16),
         ],
         scratch_shapes=[pltpu.VMEM((RHS, NODES1 * SEP1), f32), pltpu.SemaphoreType.DMA],
-        input_output_aliases={6: 0},
+        input_output_aliases={7: 0},
         compiler_params=params(24),
         name="level1",
     )(
@@ -467,6 +527,7 @@
         level1_parent_rows,
         inverse1,
         update1,
+        rhs2,
         out,
     )
     got1 = exchange(send1, ("x0", "front"))
@@ -478,10 +539,11 @@
         compiler_params=params(24),
         name="sum2",
     )(where, got1, rhs2)
-    all2 = lax.all_gather(side2, "front", axis=0, tiled=False)
+    pieces = front_pieces(side2)
+    rhs3 = late_rhs(EDGE2, ROWS, slot, both, side2)
     out, send2 = pl.pallas_call(
         level2_kernel,
-        in_specs=[SMEM, VMEM, VMEM, VMEM, VMEM, HBM],
+        in_specs=[SMEM, SMEM] + [VMEM] * 8 + [HBM],
         out_specs=[HBM, VMEM],
         out_shape=[
             struct((RHS, ROWS), f32),
@@ -491,17 +553,21 @@
             pltpu.VMEM((RHS, NODES2 * SHARE2), f32),
             pltpu.VMEM((2 * NODES3, RHS, BORDER2), f32),
             pltpu.VMEM((2 * NODES3, 8, BORDER2), i32),
+            pltpu.VMEM((FRONT, RHS, NODES2 * SHARE2), bf16),
             pltpu.SemaphoreType.DMA,
         ],
-        input_output_aliases={5: 0},
+        input_output_aliases={10: 0},
         compiler_params=params(24),
         name="level2",
     )(
+        where,
         level2_parent_node,
-        all2,
+        side2,
+        *pieces,
         level2_parent_rows,
         level2_diagonal_inverse,
         level2_update_block,
+        rhs3,
         out,
     )
     got2 = exchange(send2, ("x1", "front"))
@@ -513,17 +579,21 @@
         compiler_params=params(24),
         name="sum3",
     )(got2, rhs3)
-    all3 = lax.all_gather(side3, "front", axis=0, tiled=False)
+    pieces = front_pieces(side3)
     return pl.pallas_call(
         level3_kernel,
-        in_specs=[VMEM, VMEM, HBM],
+        in_specs=[SMEM, VMEM, VMEM, VMEM, VMEM, VMEM, HBM],
         out_specs=HBM,
         out_shape=struct((RHS, ROWS), f32),
-        scratch_shapes=[pltpu.VMEM((RHS, NODES3 * SHARE3), f32), pltpu.SemaphoreType.DMA],
-        input_output_aliases={2: 0},
+        scratch_shapes=[
+            pltpu.VMEM((RHS, NODES3 * SHARE3), f32),
+            pltpu.VMEM((FRONT, RHS, NODES3 * SHARE3), bf16),
+            pltpu.SemaphoreType.DMA,
+        ],
+        input_output_aliases={6: 0},
         compiler_params=params(24),
         name="level3",
-    )(all3, level3_diagonal_inverse, out)
+    )(where, side3, *pieces, level3_diagonal_inverse, out)
 
 
 def solution(mesh):

time: 125 us -> 118 us (0.944)
  blocking collectives: 51.7 us -> 25.6 us
  waiting for transfers between devices: 24.6 us -> 37.8 us
  starting transfers between devices: 16 us -> 21.2 us
  Pallas kernels: 29.4 us -> 30.9 us
    all_gather x2 -> x0, blocking collectives: 27.1 us -> none  [the longest x1 14.3 us: per_device(): all2 = lax.all_gather(side2, 'front', axis=0, tiled=False)]
    ppermute x0 -> x6, waiting for transfers between devices: none -> 14.4 us  [front_pieces(): lax.ppermute(side, 'front', [(f, (f + k) % FRONT) for f in range(FRONT)])]
    ppermute x0 -> x6, starting transfers between devices: none -> 5.23 us  [front_pieces(): lax.ppermute(side, 'front', [(f, (f + k) % FRONT) for f in range(FRONT)])]
    pallas_call x4 -> x6, Pallas kernels: 15.3 us -> 19.7 us  [the longest x1 7.26 us: per_device(): pl.pallas_call(pick_kernel, in_specs=[VMEM, VMEM], out_specs=HBM, out_sha...]
    pallas_call x1, Pallas kernels: 8.41 us -> 6.3 us  [per_device(): pl.pallas_call(leaf_kernel, in_specs=[SMEM, SMEM, SMEM, VMEM, VMEM, HBM,...]
  transfers between devices with their start and end apart: 3 -> 9, of which waited for: 3 -> 8; matrix products, arithmetic and copies ran while one was open for 0% -> 0% of each run, Pallas kernels for 1% -> 5%
where the time goes in v5:
time: 118 us
  waiting for transfers between devices  37.8 us (32%)
  Pallas kernels  30.9 us (26%)
  blocking collectives  25.6 us (22%)
  starting transfers between devices  21.2 us (18%)
  local copies, waits for them, and re-layouts  2.25 us (2%)
    all_to_all x2, blocking collectives, exchange(): return lax.all_to_all(block, axes, split_axis=0, concat_axis=0, tiled=True)  25.6 us
    all_to_all x2, waiting for transfers between devices, exchange(): return lax.all_to_all(block, axes, split_axis=0, concat_axis=0, tiled=True)  23.4 us
    all_to_all x2, starting transfers between devices, exchange(): return lax.all_to_all(block, axes, split_axis=0, concat_axis=0, tiled=True)  15.8 us
    ppermute x6, waiting for transfers between devices, front_pieces(): lax.ppermute(side, 'front', [(f, (f + k) % FRONT) for f in range(FRONT)])  14.4 us
    pallas_call x1, Pallas kernels, per_device(): pl.pallas_call(pick_kernel, in_specs=[VMEM, VMEM], out_specs=HBM, out_sha...  7.26 us
    pallas_call x1, Pallas kernels, per_device(): pl.pallas_call(leaf_kernel, in_specs=[SMEM, SMEM, SMEM, VMEM, VMEM, HBM,...  6.3 us
    ppermute x6, starting transfers between devices, front_pieces(): lax.ppermute(side, 'front', [(f, (f + k) % FRONT) for f in range(FRONT)])  5.23 us
    pallas_call x2, Pallas kernels, late_rhs(): pl.pallas_call(functools.partial(rhs_kernel, first, last), in_specs=[SMEM...  4.55 us
  transfers between devices with their start and end apart: 9, of which 8 were waited for; matrix products, arithmetic and copies ran while one was open for 0% of the time, Pallas kernels for 5%

profile of v5, /device:TPU:0, one launch (start us, length us, event | category | flops | bytes accessed | tf_op | source)
XLA Modules:
  0.0 118.1 jit_solution(7024161051568365363)
XLA Ops:
  0.0 0.7 copy-done.3
  0.7 2.4 %rank.1 = (s32[128,128]{1,0:T(8,128)}, s32[52,128]{1,0:T(8,128)S(1)}) custom-call(s32[52,128]{1,0:T(8,128)S(1)} %bitcast.14), custom_call_target="tpu_custom_call" | custom-call | tf_op jit(solution)/shard_map/rank/pallas_call | solution.py:442
  3.2 11.1 %all-to-all-start = ((s32[128,1,128]{2,1,0:T(1,128)}), s32[128,1,128]{2,1,0:T(1,128)S(1)}, u32[]{:S(2)}, u32[]{:S(2)}) async-start(s32[128,1,128]{2,1,0:T(1,128)} %bitcast.5), calls=%async_computation | async-start | bytes 131072 | tf_op jit(solution)/shard_map/all_to_all | solution.py:421
  14.4 1.4 %copy-done.2 = f32[64,6656]{1,0:T(8,128)S(1)} copy-done((f32[64,6656]{1,0:T(8,128)S(1)}, f32[64,6656]{1,0:T(8,128)}, u32[]{:S(2)}) %copy-start.2) | copy-done | bytes 1703960
  15.8 0.9 tall.1.tall_ref
  16.7 6.8 %all-to-all-done = s32[128,1,128]{2,1,0:T(1,128)S(1)} async-done(((s32[128,1,128]{2,1,0:T(1,128)}), s32[128,1,128]{2,1,0:T(1,128)S(1)}, u32[]{:S(2)}, u32[]{:S(2)}) %all-to-all-start) | async-done | bytes 65568 | tf_op jit(solution)/shard_map/all_to_all | solution.py:421
  23.6 7.3 %pick.1 = bf16[3328,128]{1,0:T(8,128)(2,1)} custom-call(s32[128,128]{1,0:T(8,128)S(1)} %bitcast.13, f32[6656,128]{1,0:T(8,128)S(1)} %tall.1.tall_ref), custom_call_target="tpu_custom_call" | custom-call | tf_op jit(solution)/shard_map/pick/pallas_call | solution.py:459
  30.9 4.6 %all-to-all-start.1 = ((bf16[128,13,2,128]{3,2,1,0:T(2,128)(2,1)}), bf16[128,13,2,128]{3,2,1,0:T(2,128)(2,1)S(1)}, u32[]{:S(2)}, u32[]{:S(2)}) async-start(bf16[128,13,2,128]{3,2,1,0:T(2,128)(2,1)} %bitcast.15), calls=%async_computation.1 | async-start | bytes 1703936 | tf_op jit(solution)/shard_map/all_to_all | solution.py:421
  35.5 0.1 pad_add_fusion.where_ref
  35.6 16.6 %all-to-all-done.1 = bf16[128,13,2,128]{3,2,1,0:T(2,128)(2,1)S(1)} async-done(((bf16[128,13,2,128]{3,2,1,0:T(2,128)(2,1)}), bf16[128,13,2,128]{3,2,1,0:T(2,128)(2,1)S(1)}, u32[]{:S(2)}, u32[]{:S(2)}) %all-to-all-start.1) | async-done | bytes 852000 | tf_op jit(solution)/shard_map/all_to_all | solution.py:421
  52.2 6.3 %leaf.1 = (f32[64,6656]{1,0:T(8,128)}, bf16[2,72,256]{2,1,0:T(8,128)(2,1)S(1)}, f32[2,64,1024]{2,1,0:T(8,128)S(1)}, f32[6656,128]{1,0:T(8,128)S(1)}, bf16[2,1024...) custom-call(s32[52,128]{1,0:T(8,128)S(1)} %get-tuple-element.17.slot_ref, s32[4]{0:T(128)S(1)} %copy-done.7, ...), custom_call_target="tpu_custom_call" | custom-call | tf_op jit(solution)/shard_map/leaf/pallas_call | solution.py:475
  58.5 0.2 collective-permute-start
  58.7 2.5 %rhs.2.after_ref.rhs_ref = f32[64,1536]{1,0:T(8,128)S(1)} custom-call(s32[52,128]{1,0:T(8,128)S(1)} %get-tuple-element.17.slot_ref, f32[6656,128]{1,0:T(8,128)S(1)} %get-tuple-element.23.both_ref, bf16[2,72,256]{2,1,0:T(8,128)(2,1)S(1)} %get-tuple-element.19.after_ref), custom_call_target="tpu_custom_call" | custom-call | tf_op jit(solution)/shard_map/rhs/pallas_call | solution.py:172
  61.2 0.0 slice-start
  61.3 2.8 %level1.1 = (f32[64,6656]{1,0:T(8,128)}, bf16[8,2,72,128]{3,2,1,0:T(8,128)(2,1)S(1)}) custom-call(s32[2]{0:T(128)S(1)} %copy-done.8, bf16[2,72,256]{2,1,0:T(8,128)(2,1)S(1)} %collective-permute-done.got_ref, f32[2,64,1024]{2,1,0:T(8,128)S(1)} %get-tuple-element.20.rhs_ref, s32[2,512]{1,0:T(2,128)S(1)} %copy-done.5, ...), custom_call_target="tpu_custom_call", output_to_operand_aliasing={{0}: (7, {})} | custom-call | tf_op jit(solution)/shard_map/level1/pallas_call | solution.py:511
  64.0 11.1 %all_to_all.20.got_ref = bf16[8,2,72,128]{3,2,1,0:T(8,128)(2,1)S(1)} all-to-all(bf16[8,2,72,128]{3,2,1,0:T(8,128)(2,1)S(1)} %get-tuple-element.25), channel_id=1, replica_groups=mesh['z'=4,'x1'=2,'x0'=2,'core'=2,'front'=4] {'x0','front'}, dimensions={0} | all-to-all | bytes 589824 | tf_op jit(solution)/shard_map/all_to_all | solution.py:421
  75.1 1.1 sum2.1.after_ref.own_ref
  76.3 1.2 %collective-permute-start.3 = (bf16[64,1536]{1,0:T(8,128)(2,1)S(1)}, bf16[64,1536]{1,0:T(8,128)(2,1)S(1)}, u32[]{:S(2)}, u32[]{:S(2)}) collective-permute-start(bf16[64,1536]{1,0:T(8,128)(2,1)S(1)} %sum2.1.after_ref.own_ref), channel_id=1, source_target_pairs={{0,3},{1,0},{2,1},{3,2},{4,7},{5,4},{6,5},{7,6},{8,11},{9,8},{10,9... | collective-permute-start | bytes 589832 | tf_op jit(solution)/shard_map/ppermute | solution.py:415
  77.6 1.5 %collective-permute-start.2 = (bf16[64,1536]{1,0:T(8,128)(2,1)S(1)}, bf16[64,1536]{1,0:T(8,128)(2,1)S(1)}, u32[]{:S(2)}, u32[]{:S(2)}) collective-permute-start(bf16[64,1536]{1,0:T(8,128)(2,1)S(1)} %sum2.1.after_ref.own_ref), channel_id=1, source_target_pairs={{0,2},{1,3},{2,0},{3,1},{4,6},{5,7},{6,4},{7,5},{8,10},{9,11},{10,... | collective-permute-start | bytes 589832 | tf_op jit(solution)/shard_map/ppermute | solution.py:415
  79.0 2.0 %rhs.3.after_ref.rhs_ref = f32[64,1024]{1,0:T(8,128)S(1)} custom-call(s32[52,128]{1,0:T(8,128)S(1)} %get-tuple-element.17.slot_ref, f32[6656,128]{1,0:T(8,128)S(1)} %get-tuple-element.23.both_ref, bf16[64,1536]{1,0:T(8,128)(2,1)S(1)} %sum2.1.after_ref.own_ref), custom_call_target="tpu_custom_call" | custom-call | tf_op jit(solution)/shard_map/rhs/pallas_call | solution.py:172
  81.1 3.2 %collective-permute-done.3.third_ref = bf16[64,1536]{1,0:T(8,128)(2,1)S(1)} collective-permute-done((bf16[64,1536]{1,0:T(8,128)(2,1)S(1)}, bf16[64,1536]{1,0:T(8,128)(2,1)S(1)}, u32[]{:S(2)}, u32[]{:S(2)}) %collective-permute-start.3) | collective-permute-done | bytes 196640 | tf_op jit(solution)/shard_map/ppermute | solution.py:415
  84.2 2.7 %collective-permute-done.2.second_ref = bf16[64,1536]{1,0:T(8,128)(2,1)S(1)} collective-permute-done((bf16[64,1536]{1,0:T(8,128)(2,1)S(1)}, bf16[64,1536]{1,0:T(8,128)(2,1)S(1)}, u32[]{:S(2)}, u32[]{:S(2)}) %collective-permute-start.2) | collective-permute-done | bytes 196640 | tf_op jit(solution)/shard_map/ppermute | solution.py:415
  86.9 2.2 %collective-permute-done.1.first_ref = bf16[64,1536]{1,0:T(8,128)(2,1)S(1)} collective-permute-done((bf16[64,1536]{1,0:T(8,128)(2,1)S(1)}, bf16[64,1536]{1,0:T(8,128)(2,1)S(1)}, u32[]{:S(2)}, u32[]{:S(2)}) %collective-permute-start.1) | collective-permute-done | bytes 196640 | tf_op jit(solution)/shard_map/ppermute | solution.py:415
  89.1 3.0 %level2.1 = (f32[64,6656]{1,0:T(8,128)}, bf16[8,3,72,128]{3,2,1,0:T(8,128)(2,1)S(1)}) custom-call(s32[3]{0:T(128)S(1)} %pad_add_fusion.where_ref, s32[4]{0:T(128)S(1)} %copy-done.9, bf16[64,1536]{1,0:T(8,128)(2,1)S(1)} %sum2.1.after_ref.own_ref, bf16[64,1536]{1,0:T(8,128)(2,1)S(1)} %collective-permute-done.1.first_ref, ...), custom_call_target="tpu_custom_call", output_to_operand_aliasing={{0}: (10, {})} | custom-call | tf_op jit(solution)/shard_map/level2/pallas_call | solution.py:544
  92.1 14.5 %all_to_all.21.got_ref = bf16[8,3,72,128]{3,2,1,0:T(8,128)(2,1)S(1)} all-to-all(bf16[8,3,72,128]{3,2,1,0:T(8,128)(2,1)S(1)} %get-tuple-element.27), channel_id=1, replica_groups=mesh['z'=4,'x1'=2,'x0'=2,'core'=2,'front'=4] {'x1','front'}, dimensions={0} | all-to-all | bytes 884736 | tf_op jit(solution)/shard_map/all_to_all | solution.py:421
  106.6 0.4 sum3.1.own_ref
  107.0 1.0 collective-permute-start.6
  108.1 1.5 %collective-permute-start.5 = (bf16[64,1024]{1,0:T(8,128)(2,1)S(1)}, bf16[64,1024]{1,0:T(8,128)(2,1)S(1)}, u32[]{:S(2)}, u32[]{:S(2)}) collective-permute-start(bf16[64,1024]{1,0:T(8,128)(2,1)S(1)} %sum3.1.own_ref), channel_id=1, source_target_pairs={{0,2},{1,3},{2,0},{3,1},{4,6},{5,7},{6,4},{7,5},{8,10},{9,11},{10,... | collective-permute-start | bytes 393224 | tf_op jit(solution)/shard_map/ppermute | solution.py:415
  109.5 2.5 %collective-permute-done.6.third_ref = bf16[64,1024]{1,0:T(8,128)(2,1)S(1)} collective-permute-done((bf16[64,1024]{1,0:T(8,128)(2,1)S(1)}, bf16[64,1024]{1,0:T(8,128)(2,1)S(1)}, u32[]{:S(2)}, u32[]{:S(2)}) %collective-permute-start.6) | collective-permute-done | bytes 131104 | tf_op jit(solution)/shard_map/ppermute | solution.py:415
  112.1 2.5 %collective-permute-done.5.second_ref = bf16[64,1024]{1,0:T(8,128)(2,1)S(1)} collective-permute-done((bf16[64,1024]{1,0:T(8,128)(2,1)S(1)}, bf16[64,1024]{1,0:T(8,128)(2,1)S(1)}, u32[]{:S(2)}, u32[]{:S(2)}) %collective-permute-start.5) | collective-permute-done | bytes 131104 | tf_op jit(solution)/shard_map/ppermute | solution.py:415
  114.6 1.4 %collective-permute-done.4.first_ref = bf16[64,1024]{1,0:T(8,128)(2,1)S(1)} collective-permute-done((bf16[64,1024]{1,0:T(8,128)(2,1)S(1)}, bf16[64,1024]{1,0:T(8,128)(2,1)S(1)}, u32[]{:S(2)}, u32[]{:S(2)}) %collective-permute-start.4) | collective-permute-done | bytes 131104 | tf_op jit(solution)/shard_map/ppermute | solution.py:415
  116.0 2.1 %level3.1 = f32[64,6656]{1,0:T(8,128)} custom-call(s32[3]{0:T(128)S(1)} %pad_add_fusion.where_ref, bf16[64,1024]{1,0:T(8,128)(2,1)S(1)} %sum3.1.own_ref, bf16[64,1024]{1,0:T(8,128)(2,1)S(1)} %collective-permute-done.4.first_ref, bf16[64,1024]{1,0:T(8,128)(2,1)S(1)} %collective-permute-done.5.second_ref, ...), custom_call_target="tpu_custom_call", output_to_operand_aliasing={{}: (6, {})} | custom-call | tf_op jit(solution)/shard_map/level3/pallas_call | solution.py:583
  (25 shorter events, 0.1 us)
Async XLA Ops:
  0.0 0.7 copy-start.3
  3.2 20.4 %all-to-all-start = ((s32[128,1,128]{2,1,0:T(1,128)}), s32[128,1,128]{2,1,0:T(1,128)S(1)}, u32[]{:S(2)}, u32[]{:S(2)}) async-start(s32[128,1,128]{2,1,0:T(1,128)} %bitcast.5), calls=%async_computation | async-start | bytes 131072 | tf_op jit(solution)/shard_map/all_to_all | solution.py:421
  14.3 1.5 %copy-start.2 = (f32[64,6656]{1,0:T(8,128)S(1)}, f32[64,6656]{1,0:T(8,128)}, u32[]{:S(2)}) copy-start(f32[64,6656]{1,0:T(8,128)} %wide_ref.1) | copy-start | bytes 5111812
  23.6 28.6 %copy-start.6 = (s32[4,256]{1,0:T(4,128)S(1)}, s32[4,256]{1,0:T(4,128)}, u32[]{:S(2)}) copy-start(s32[4,256]{1,0:T(4,128)} %rows_ref.3) | copy-start | bytes 12292
  23.6 28.6 %copy-start.7 = (s32[4]{0:T(128)S(1)}, s32[4]{0:T(128)}, u32[]{:S(2)}) copy-start(s32[4]{0:T(128)} %parent_ref.3) | copy-start | bytes 52
  30.9 21.3 %all-to-all-start.1 = ((bf16[128,13,2,128]{3,2,1,0:T(2,128)(2,1)}), bf16[128,13,2,128]{3,2,1,0:T(2,128)(2,1)S(1)}, u32[]{:S(2)}, u32[]{:S(2)}) async-start(bf16[128,13,2,128]{3,2,1,0:T(2,128)(2,1)} %bitcast.15), calls=%async_computation.1 | async-start | bytes 1703936 | tf_op jit(solution)/shard_map/all_to_all | solution.py:421
  58.5 2.8 %copy-start.5 = (s32[2,512]{1,0:T(2,128)S(1)}, s32[2,512]{1,0:T(2,128)}, u32[]{:S(2)}) copy-start(s32[2,512]{1,0:T(2,128)} %rows_ref.4) | copy-start | bytes 12292
  58.5 2.8 %copy-start.8 = (s32[2]{0:T(128)S(1)}, s32[2]{0:T(128)}, u32[]{:S(2)}) copy-start(s32[2]{0:T(128)} %parent_ref.4) | copy-start | bytes 28
  58.5 2.7 %collective-permute-start = (bf16[2,72,256]{2,1,0:T(8,128)(2,1)S(1)}, bf16[2,72,256]{2,1,0:T(8,128)(2,1)S(1)}, u32[]{:S(2)}, u32[]{:S(2)}) collective-permute-start(bf16[2,72,256]{2,1,0:T(8,128)(2,1)S(1)} %get-tuple-element.19.after_ref), channel_id=1, source_target_pairs={{0,4},{4,0},{1,5},{5,1},{2,6},{6,2},{3,7},{7,3},{8,12},{12,8},{9,1... | collective-permute-start | bytes 221192 | tf_op jit(solution)/shard_map/ppermute | solution.py:509
  61.2 27.8 %slice-start = ((s8[4718592]{0:T(1024)(128)(4,1)}), s8[4194304]{0:T(1024)(128)(4,1)S(1)}, s32[]{:S(2)}) async-start(s8[4718592]{0:T(1024)(128)(4,1)} %bitcast.10), calls=%async_computation.4 | async-start | bytes 8388608
  61.3 27.8 %slice-start.1 = ((s8[4718592]{0:T(1024)(128)(4,1)}), s8[524288]{0:T(1024)(128)(4,1)S(1)}, s32[]{:S(2)}) async-start(s8[4718592]{0:T(1024)(128)(4,1)} %bitcast.10), calls=%async_computation.5 | async-start | bytes 1048576
  76.3 12.8 %copy-start.1 = (bf16[4,384,768]{2,1,0:T(8,128)(2,1)S(1)}, bf16[4,384,768]{2,1,0:T(8,128)(2,1)}, u32[]{:S(2)}) copy-start(bf16[4,384,768]{2,1,0:T(8,128)(2,1)} %update_ref.1) | copy-start | bytes 7077892
  76.3 12.8 %copy-start.4 = (s32[4,768]{1,0:T(4,128)S(1)}, s32[4,768]{1,0:T(4,128)}, u32[]{:S(2)}) copy-start(s32[4,768]{1,0:T(4,128)} %rows_ref.5) | copy-start | bytes 36868
  76.3 12.8 %copy-start.9 = (s32[4]{0:T(128)S(1)}, s32[4]{0:T(128)}, u32[]{:S(2)}) copy-start(s32[4]{0:T(128)} %parent_ref.5) | copy-start | bytes 52
  76.3 7.9 %collective-permute-start.3 = (bf16[64,1536]{1,0:T(8,128)(2,1)S(1)}, bf16[64,1536]{1,0:T(8,128)(2,1)S(1)}, u32[]{:S(2)}, u32[]{:S(2)}) collective-permute-start(bf16[64,1536]{1,0:T(8,128)(2,1)S(1)} %sum2.1.after_ref.own_ref), channel_id=1, source_target_pairs={{0,3},{1,0},{2,1},{3,2},{4,7},{5,4},{6,5},{7,6},{8,11},{9,8},{10,9... | collective-permute-start | bytes 589832 | tf_op jit(solution)/shard_map/ppermute | solution.py:415
  77.6 9.3 %collective-permute-start.2 = (bf16[64,1536]{1,0:T(8,128)(2,1)S(1)}, bf16[64,1536]{1,0:T(8,128)(2,1)S(1)}, u32[]{:S(2)}, u32[]{:S(2)}) collective-permute-start(bf16[64,1536]{1,0:T(8,128)(2,1)S(1)} %sum2.1.after_ref.own_ref), channel_id=1, source_target_pairs={{0,2},{1,3},{2,0},{3,1},{4,6},{5,7},{6,4},{7,5},{8,10},{9,11},{10,... | collective-permute-start | bytes 589832 | tf_op jit(solution)/shard_map/ppermute | solution.py:415
  79.0 10.0 %collective-permute-start.1 = (bf16[64,1536]{1,0:T(8,128)(2,1)S(1)}, bf16[64,1536]{1,0:T(8,128)(2,1)S(1)}, u32[]{:S(2)}, u32[]{:S(2)}) collective-permute-start(bf16[64,1536]{1,0:T(8,128)(2,1)S(1)} %sum2.1.after_ref.own_ref), channel_id=1, source_target_pairs={{0,1},{1,2},{2,3},{3,0},{4,5},{5,6},{6,7},{7,4},{8,9},{9,10},{10,1... | collective-permute-start | bytes 589832 | tf_op jit(solution)/shard_map/ppermute | solution.py:415
  89.1 26.9 %copy-start = (bf16[2,2048,512]{2,1,0:T(8,128)(2,1)S(1)}, bf16[2,2048,512]{2,1,0:T(8,128)(2,1)}, u32[]{:S(2)}) copy-start(bf16[2,2048,512]{2,1,0:T(8,128)(2,1)} %inverse_ref.3) | copy-start | bytes 12582916
  107.0 5.0 %collective-permute-start.6 = (bf16[64,1024]{1,0:T(8,128)(2,1)S(1)}, bf16[64,1024]{1,0:T(8,128)(2,1)S(1)}, u32[]{:S(2)}, u32[]{:S(2)}) collective-permute-start(bf16[64,1024]{1,0:T(8,128)(2,1)S(1)} %sum3.1.own_ref), channel_id=1, source_target_pairs={{0,3},{1,0},{2,1},{3,2},{4,7},{5,4},{6,5},{7,6},{8,11},{9,8},{10,9... | collective-permute-start | bytes 393224 | tf_op jit(solution)/shard_map/ppermute | solution.py:415
  108.1 6.5 %collective-permute-start.5 = (bf16[64,1024]{1,0:T(8,128)(2,1)S(1)}, bf16[64,1024]{1,0:T(8,128)(2,1)S(1)}, u32[]{:S(2)}, u32[]{:S(2)}) collective-permute-start(bf16[64,1024]{1,0:T(8,128)(2,1)S(1)} %sum3.1.own_ref), channel_id=1, source_target_pairs={{0,2},{1,3},{2,0},{3,1},{4,6},{5,7},{6,4},{7,5},{8,10},{9,11},{10,... | collective-permute-start | bytes 393224 | tf_op jit(solution)/shard_map/ppermute | solution.py:415
  109.5 6.4 %collective-permute-start.4 = (bf16[64,1024]{1,0:T(8,128)(2,1)S(1)}, bf16[64,1024]{1,0:T(8,128)(2,1)S(1)}, u32[]{:S(2)}, u32[]{:S(2)}) collective-permute-start(bf16[64,1024]{1,0:T(8,128)(2,1)S(1)} %sum3.1.own_ref), channel_id=1, source_target_pairs={{0,1},{1,2},{2,3},{3,0},{4,5},{5,6},{6,7},{7,4},{8,9},{9,10},{10,1... | collective-permute-start | bytes 393224 | tf_op jit(solution)/shard_map/ppermute | solution.py:415

commit v6 on v5

--- a/solution.py
+++ b/solution.py
@@ -94,10 +94,10 @@
         tall_ref[b * 512 : (b + 1) * 512, :] = jnp.concatenate([wide, wide], axis=0).T
 
 
-def pick_kernel(asked_ref, tall_ref, out_hbm, buf, narrow, asked, sems, sem):
+def pick_kernel(asked_ref, tall_ref, out_hbm, buf, narrow, asked, sems):
     low = lax.broadcasted_iota(i32, (1, 128), 1) < RHS
     step = DEVICES // CHUNKS
-    loads = []
+    loads, stores = [], []
     for c in range(CHUNKS):
         part = slice(c * step, (c + 1) * step)
         loads.append(pltpu.make_async_copy(asked_ref.at[part], asked.at[part], sems.at[c]))
@@ -116,10 +116,14 @@
     for c in range(CHUNKS):
         loads[c].wait()
         lax.fori_loop(c * step // GROUP, (c + 1) * step // GROUP, gather, 0)
-    narrow[...] = buf[...].astype(bf16)
-    store = pltpu.make_async_copy(narrow, out_hbm, sem)
-    store.start()
-    store.wait()
+        part = slice(c * step * HALF, (c + 1) * step * HALF)
+        narrow[part, :] = buf[part, :].astype(bf16)
+        stores.append(
+            pltpu.make_async_copy(narrow.at[part], out_hbm.at[part], sems.at[CHUNKS + c])
+        )
+        stores[c].start()
+    for store in stores:
+        store.wait()
 
 
 def rank_kernel(index_ref, asked_ref, slot_ref):
@@ -183,7 +187,6 @@
 def leaf_kernel(
     slot_ref,
     parent_ref,
-    where_ref,
     arrived_ref,
     rows_ref,
     inverse_hbm,
@@ -225,7 +228,9 @@
     for n in range(LEAVES):
         sol_ref[:, n * LEAF : (n + 1) * LEAF] = sols[n]
         terms.append(mm(sols[n].astype(bf16), update_ref[n]).astype(bf16))
-    core = where_ref[0]
+    store = pltpu.make_async_copy(sol_ref, out_hbm.at[:, 0:EDGE0], sems.at[2])
+    store.start()
+    core = lax.axis_index("core")
     for n in range(LEAVES):
         node = parent_ref[n]
         slot = node & 1
@@ -242,8 +247,6 @@
             kept_ref[slot] = terms[n]
             kept_rows[slot] = jnp.broadcast_to(targets, (8, BORDER0))
 
-    store = pltpu.make_async_copy(sol_ref, out_hbm.at[:, 0:EDGE0], sems.at[2])
-    store.start()
     for q in range(NODES1):
         rhs = tall[EDGE0 + q * SEP1 : EDGE0 + (q + 1) * SEP1, :].T[:RHS]
         rows = kept_rows[q, 0:1, :]
@@ -255,7 +258,7 @@
 
 
 def level1_kernel(
-    parent_ref,
+    parent_vmem,
     got_ref,
     rhs_ref,
     rows_ref,
@@ -266,16 +269,28 @@
     out_hbm,
     send_ref,
     sol_ref,
-    sem,
+    parent_ref,
+    sems,
 ):
     del out_in, after_ref
+    load = pltpu.make_async_copy(parent_vmem, parent_ref, sems.at[NODES1])
+    load.start()
+    stores = []
     for n in range(NODES1):
         high, low, _ = undigits(got_ref[n, RHS : RHS + META, :])
         got = got_ref[n, 0:RHS, :].astype(f32)
         rhs = rhs_ref[n] - place([got], high, low, SEP1 // LOW)
         sol = mm(rhs.astype(bf16), inverse_ref[n])
-        sol_ref[:, n * SEP1 : (n + 1) * SEP1] = sol
+        own = slice(n * SEP1, (n + 1) * SEP1)
+        sol_ref[:, own] = sol
+        part = slice(EDGE0 + n * SEP1, EDGE0 + (n + 1) * SEP1)
+        stores.append(
+            pltpu.make_async_copy(sol_ref.at[:, own], out_hbm.at[:, part], sems.at[n])
+        )
+        stores[n].start()
         terms = mm(sol.astype(bf16), update_ref[n]).astype(bf16)
+        if n == 0:
+            load.wait()
         node = parent_ref[n]
         slot = node & 3
         side = (node >> 3) & 1
@@ -286,13 +301,12 @@
             for x in range(2):
                 send_ref[x * FRONT + f, n, 0:RHS, :] = terms[:, own]
                 send_ref[x * FRONT + f, n, RHS : RHS + META, :] = meta
-    store = pltpu.make_async_copy(sol_ref, out_hbm.at[:, EDGE0:EDGE1], sem)
-    store.start()
-    store.wait()
-
-
-def sum2_kernel(where_ref, got_ref, rhs_ref, out_ref):
-    x0 = where_ref[1].astype(f32)
+    for store in stores:
+        store.wait()
+
+
+def sum2_kernel(got_ref, rhs_ref, out_ref):
+    x0 = lax.axis_index("x0").astype(f32)
     terms, highs, lows = [], [], []
     for e in range(2 * FRONT):
         for n in range(NODES1):
@@ -309,14 +323,14 @@
     out_ref[...] = (rhs_ref[...] - total).astype(bf16)
 
 
-def gathered(front, pieces, rhs_ref):
+def gathered(pieces, rhs_ref):
+    front = lax.axis_index("front")
     for k, piece in enumerate(pieces):
         rhs_ref[(front + FRONT - k) & (FRONT - 1)] = piece[...]
 
 
 def level2_kernel(
-    where_ref,
-    parent_ref,
+    parent_vmem,
     own_ref,
     first_ref,
     second_ref,
@@ -332,20 +346,25 @@
     terms_ref,
     terms_rows,
     rhs_ref,
-    sem,
+    parent_ref,
+    sems,
 ):
     del out_in, after_ref
-    gathered(where_ref[2], (own_ref, first_ref, second_ref, third_ref), rhs_ref)
+    load = pltpu.make_async_copy(parent_vmem, parent_ref, sems.at[1])
+    load.start()
+    gathered((own_ref, first_ref, second_ref, third_ref), rhs_ref)
     for c in range(NODES2):
         own = slice(c * SHARE2, (c + 1) * SHARE2)
         lhs = jnp.concatenate([rhs_ref[g, :, own] for g in range(FRONT)], axis=1)
         sol = mm(lhs, inverse_ref[c])
         sol_ref[:, own] = sol
+        if c == 0:
+            load.wait()
         node = parent_ref[c]
         slot = ((node >> 3) & 1) * NODES3 + (node & 1)
         terms_ref[slot] = mm(sol.astype(bf16), update_ref[c])
         terms_rows[slot] = jnp.broadcast_to(rows_ref[c : c + 1, :], (8, BORDER2))
-    store = pltpu.make_async_copy(sol_ref, out_hbm.at[:, EDGE1:EDGE2], sem)
+    store = pltpu.make_async_copy(sol_ref, out_hbm.at[:, EDGE1:EDGE2], sems.at[0])
     store.start()
     for x in range(2):
         for f in range(FRONT):
@@ -387,7 +406,6 @@
 
 
 def level3_kernel(
-    where_ref,
     own_ref,
     first_ref,
     second_ref,
@@ -397,17 +415,22 @@
     out_hbm,
     sol_ref,
     rhs_ref,
-    sem,
+    sems,
 ):
     del out_in
-    gathered(where_ref[2], (own_ref, first_ref, second_ref, third_ref), rhs_ref)
+    gathered((own_ref, first_ref, second_ref, third_ref), rhs_ref)
+    stores = []
     for c in range(NODES3):
         own = slice(c * SHARE3, (c + 1) * SHARE3)
         lhs = jnp.concatenate([rhs_ref[g, :, own] for g in range(FRONT)], axis=1)
         sol_ref[:, own] = mm(lhs, inverse_ref[c])
-    store = pltpu.make_async_copy(sol_ref, out_hbm.at[:, EDGE2:ROWS], sem)
-    store.start()
-    store.wait()
+        part = slice(EDGE2 + c * SHARE3, EDGE2 + (c + 1) * SHARE3)
+        stores.append(
+            pltpu.make_async_copy(sol_ref.at[:, own], out_hbm.at[:, part], sems.at[c])
+        )
+        stores[c].start()
+    for store in stores:
+        store.wait()
 
 
 def front_pieces(side):
@@ -438,7 +461,6 @@
     level2_parent_node,
     level3_diagonal_inverse,
 ):
-    where = jnp.stack([lax.axis_index(a) for a in ("core", "x0", "front")]).astype(i32)
     requests, slot = pl.pallas_call(
         rank_kernel,
         in_specs=[VMEM],
@@ -465,8 +487,7 @@
             pltpu.VMEM((DEVICES * HALF, 128), f32),
             pltpu.VMEM((DEVICES * HALF, 128), bf16),
             pltpu.SMEM((DEVICES, LANES), i32),
-            pltpu.SemaphoreType.DMA((CHUNKS,)),
-            pltpu.SemaphoreType.DMA,
+            pltpu.SemaphoreType.DMA((2 * CHUNKS,)),
         ],
         compiler_params=params(16),
         name="pick",
@@ -474,7 +495,7 @@
     arrived = exchange(picked.reshape(DEVICES, HALF // 2, 2, 128), ALL)
     out, send0, rhs1, both, inverse1, update1 = pl.pallas_call(
         leaf_kernel,
-        in_specs=[SMEM, SMEM, SMEM, VMEM, VMEM, HBM, HBM, HBM, HBM],
+        in_specs=[SMEM, SMEM, VMEM, VMEM, HBM, HBM, HBM, HBM],
         out_specs=[HBM, VMEM, VMEM, VMEM, VMEM, VMEM],
         out_shape=[
             struct((RHS, ROWS), f32),
@@ -498,7 +519,6 @@
     )(
         slot,
         leaf_parent_node,
-        where,
         arrived.reshape(DEVICES * HALF, 128),
         leaf_parent_rows,
         in_hbm(leaf_diagonal_inverse),
@@ -510,13 +530,17 @@
     rhs2 = late_rhs(EDGE1, EDGE2, slot, both, send0)
     out, send1 = pl.pallas_call(
         level1_kernel,
-        in_specs=[SMEM] + [VMEM] * 6 + [HBM],
+        in_specs=[VMEM] * 7 + [HBM],
         out_specs=[HBM, VMEM],
         out_shape=[
             struct((RHS, ROWS), f32),
             struct((2 * FRONT, NODES1, RHS + META, PART1), bf16),
         ],
-        scratch_shapes=[pltpu.VMEM((RHS, NODES1 * SEP1), f32), pltpu.SemaphoreType.DMA],
+        scratch_shapes=[
+            pltpu.VMEM((RHS, NODES1 * SEP1), f32),
+            pltpu.SMEM((NODES1,), i32),
+            pltpu.SemaphoreType.DMA((NODES1 + 1,)),
+        ],
         input_output_aliases={7: 0},
         compiler_params=params(24),
         name="level1",
@@ -533,17 +557,17 @@
     got1 = exchange(send1, ("x0", "front"))
     side2 = pl.pallas_call(
         sum2_kernel,
-        in_specs=[SMEM, VMEM, VMEM],
+        in_specs=[VMEM, VMEM],
         out_specs=VMEM,
         out_shape=struct((RHS, NODES2 * SHARE2), bf16),
         compiler_params=params(24),
         name="sum2",
-    )(where, got1, rhs2)
+    )(got1, rhs2)
     pieces = front_pieces(side2)
     rhs3 = late_rhs(EDGE2, ROWS, slot, both, side2)
     out, send2 = pl.pallas_call(
         level2_kernel,
-        in_specs=[SMEM, SMEM] + [VMEM] * 8 + [HBM],
+        in_specs=[VMEM] * 9 + [HBM],
         out_specs=[HBM, VMEM],
         out_shape=[
             struct((RHS, ROWS), f32),
@@ -554,13 +578,13 @@
             pltpu.VMEM((2 * NODES3, RHS, BORDER2), f32),
             pltpu.VMEM((2 * NODES3, 8, BORDER2), i32),
             pltpu.VMEM((FRONT, RHS, NODES2 * SHARE2), bf16),
-            pltpu.SemaphoreType.DMA,
-        ],
-        input_output_aliases={10: 0},
+            pltpu.SMEM((NODES2,), i32),
+            pltpu.SemaphoreType.DMA((2,)),
+        ],
+        input_output_aliases={9: 0},
         compiler_params=params(24),
         name="level2",
     )(
-        where,
         level2_parent_node,
         side2,
         *pieces,
@@ -582,18 +606,18 @@
     pieces = front_pieces(side3)
     return pl.pallas_call(
         level3_kernel,
-        in_specs=[SMEM, VMEM, VMEM, VMEM, VMEM, VMEM, HBM],
+        in_specs=[VMEM] * 5 + [HBM],
         out_specs=HBM,
         out_shape=struct((RHS, ROWS), f32),
         scratch_shapes=[
             pltpu.VMEM((RHS, NODES3 * SHARE3), f32),
             pltpu.VMEM((FRONT, RHS, NODES3 * SHARE3), bf16),
-            pltpu.SemaphoreType.DMA,
-        ],
-        input_output_aliases={6: 0},
+            pltpu.SemaphoreType.DMA((NODES3,)),
+        ],
+        input_output_aliases={5: 0},
         compiler_params=params(24),
         name="level3",
-    )(where, side3, *pieces, level3_diagonal_inverse, out)
+    )(side3, *pieces, level3_diagonal_inverse, out)
 
 
 def solution(mesh):

time: 118 us -> 116 us (0.983)
  blocking collectives: 25.6 us -> 47.1 us
  waiting for transfers between devices: 37.8 us -> 21.2 us
  starting transfers between devices: 21.2 us -> 16.6 us
  Pallas kernels: 30.9 us -> 28.6 us
    all_to_all x2 -> x3, blocking collectives: 25.6 us -> 47.1 us  [exchange(): return lax.all_to_all(block, axes, split_axis=0, concat_axis=0, tiled=True)]
    all_to_all x2 -> x1, waiting for transfers between devices: 23.4 us -> 6.84 us  [exchange(): return lax.all_to_all(block, axes, split_axis=0, concat_axis=0, tiled=True)]
    all_to_all x2 -> x1, starting transfers between devices: 15.8 us -> 11.1 us  [exchange(): return lax.all_to_all(block, axes, split_axis=0, concat_axis=0, tiled=True)]
    pallas_call x5, Pallas kernels: 15.3 us -> 13.2 us  [the longest x1 6.08 us: per_device(): pl.pallas_call(leaf_kernel, in_specs=[SMEM, SMEM, VMEM, VMEM, HBM, HBM, H...]
  transfers between devices with their start and end apart: 9 -> 8, of which waited for: 8 -> 7; matrix products, arithmetic and copies ran while one was open for 0% -> 0% of each run, Pallas kernels for 5% -> 5%
where the time goes in v6:
time: 116 us
  blocking collectives  47.1 us (41%)
  Pallas kernels  28.6 us (25%)
  waiting for transfers between devices  21.2 us (18%)
  starting transfers between devices  16.6 us (14%)
  local copies, waits for them, and re-layouts  2.25 us (2%)
    all_to_all x3, blocking collectives, exchange(): return lax.all_to_all(block, axes, split_axis=0, concat_axis=0, tiled=True)  47.1 us
    ppermute x6, waiting for transfers between devices, front_pieces(): lax.ppermute(side, 'front', [(f, (f + k) % FRONT) for f in range(FRONT)])  14.4 us
    all_to_all x1, starting transfers between devices, exchange(): return lax.all_to_all(block, axes, split_axis=0, concat_axis=0, tiled=True)  11.1 us
    pallas_call x1, Pallas kernels, per_device(): pl.pallas_call(pick_kernel, in_specs=[VMEM, VMEM], out_specs=HBM, out_sha...  7.08 us
    all_to_all x1, waiting for transfers between devices, exchange(): return lax.all_to_all(block, axes, split_axis=0, concat_axis=0, tiled=True)  6.84 us
    pallas_call x1, Pallas kernels, per_device(): pl.pallas_call(leaf_kernel, in_specs=[SMEM, SMEM, VMEM, VMEM, HBM, HBM, H...  6.08 us
    ppermute x6, starting transfers between devices, front_pieces(): lax.ppermute(side, 'front', [(f, (f + k) % FRONT) for f in range(FRONT)])  5.23 us
    pallas_call x2, Pallas kernels, late_rhs(): pl.pallas_call(functools.partial(rhs_kernel, first, last), in_specs=[SMEM...  4.55 us
  transfers between devices with their start and end apart: 8, of which 7 were waited for; matrix products, arithmetic and copies ran while one was open for 0% of the time, Pallas kernels for 5%

profile of v6, /device:TPU:0, one launch (start us, length us, event | category | flops | bytes accessed | tf_op | source)
XLA Modules:
  0.0 116.0 jit_solution(17329781838461580531)
XLA Ops:
  0.0 0.7 copy-done.3
  0.7 2.4 %rank.1 = (s32[128,128]{1,0:T(8,128)}, s32[52,128]{1,0:T(8,128)S(1)}) custom-call(s32[52,128]{1,0:T(8,128)S(1)} %bitcast.11), custom_call_target="tpu_custom_call" | custom-call | tf_op jit(solution)/shard_map/rank/pallas_call | solution.py:464
  3.2 11.1 %all-to-all-start = ((s32[128,1,128]{2,1,0:T(1,128)}), s32[128,1,128]{2,1,0:T(1,128)S(1)}, u32[]{:S(2)}, u32[]{:S(2)}) async-start(s32[128,1,128]{2,1,0:T(1,128)} %bitcast.2), calls=%async_computation | async-start | bytes 131072 | tf_op jit(solution)/shard_map/all_to_all | solution.py:444
  14.3 0.0 copy-start.2
  14.4 1.4 %copy-done.2 = f32[64,6656]{1,0:T(8,128)S(1)} copy-done((f32[64,6656]{1,0:T(8,128)S(1)}, f32[64,6656]{1,0:T(8,128)}, u32[]{:S(2)}) %copy-start.2) | copy-done | bytes 1703960
  15.8 0.9 tall.1.tall_ref
  16.7 6.8 %all-to-all-done = s32[128,1,128]{2,1,0:T(1,128)S(1)} async-done(((s32[128,1,128]{2,1,0:T(1,128)}), s32[128,1,128]{2,1,0:T(1,128)S(1)}, u32[]{:S(2)}, u32[]{:S(2)}) %all-to-all-start) | async-done | bytes 65568 | tf_op jit(solution)/shard_map/all_to_all | solution.py:444
  23.6 7.1 %pick.1 = bf16[3328,128]{1,0:T(8,128)(2,1)} custom-call(s32[128,128]{1,0:T(8,128)S(1)} %bitcast.10, f32[6656,128]{1,0:T(8,128)S(1)} %tall.1.tall_ref), custom_call_target="tpu_custom_call" | custom-call | tf_op jit(solution)/shard_map/pick/pallas_call | solution.py:481
  30.7 21.6 %all_to_all.20 = bf16[128,13,2,128]{3,2,1,0:T(2,128)(2,1)S(1)} all-to-all(bf16[128,13,2,128]{3,2,1,0:T(2,128)(2,1)} %bitcast.12), channel_id=1, replica_groups=mesh['z'=4,'x1'=2,'x0'=2,'core'=2,'front'=4] {'z','x1','x0','core','front'}, dimensions={0} | all-to-all | bytes 1703936 | tf_op jit(solution)/shard_map/all_to_all | solution.py:444
  52.2 6.1 %leaf.1 = (f32[64,6656]{1,0:T(8,128)}, bf16[2,72,256]{2,1,0:T(8,128)(2,1)S(1)}, f32[2,64,1024]{2,1,0:T(8,128)S(1)}, f32[6656,128]{1,0:T(8,128)S(1)}, bf16[2,1024...) custom-call(s32[52,128]{1,0:T(8,128)S(1)} %get-tuple-element.17.slot_ref, s32[4]{0:T(128)S(1)} %copy-done.9, ...), custom_call_target="tpu_custom_call" | custom-call | tf_op jit(solution)/shard_map/leaf/pallas_call | solution.py:496
  58.3 0.0 copy-start.7
  58.3 0.2 collective-permute-start
  58.5 2.5 %rhs.2.after_ref.rhs_ref = f32[64,1536]{1,0:T(8,128)S(1)} custom-call(s32[52,128]{1,0:T(8,128)S(1)} %get-tuple-element.17.slot_ref, f32[6656,128]{1,0:T(8,128)S(1)} %get-tuple-element.23.both_ref, bf16[2,72,256]{2,1,0:T(8,128)(2,1)S(1)} %get-tuple-element.19.after_ref), custom_call_target="tpu_custom_call" | custom-call | tf_op jit(solution)/shard_map/rhs/pallas_call | solution.py:176
  61.1 0.0 slice-start
  61.1 2.3 %level1.1 = (f32[64,6656]{1,0:T(8,128)}, bf16[8,2,72,128]{3,2,1,0:T(8,128)(2,1)S(1)}) custom-call(s32[2]{0:T(128)S(1)} %copy-done.7, bf16[2,72,256]{2,1,0:T(8,128)(2,1)S(1)} %collective-permute-done.got_ref, f32[2,64,1024]{2,1,0:T(8,128)S(1)} %get-tuple-element.20.rhs_ref, s32[2,512]{1,0:T(2,128)S(1)} %copy-done.5, ...), custom_call_target="tpu_custom_call", output_to_operand_aliasing={{0}: (7, {})} | custom-call | tf_op jit(solution)/shard_map/level1/pallas_call | solution.py:531
  63.4 11.1 %all_to_all.21.got_ref = bf16[8,2,72,128]{3,2,1,0:T(8,128)(2,1)S(1)} all-to-all(bf16[8,2,72,128]{3,2,1,0:T(8,128)(2,1)S(1)} %get-tuple-element.25), channel_id=1, replica_groups=mesh['z'=4,'x1'=2,'x0'=2,'core'=2,'front'=4] {'x0','front'}, dimensions={0} | all-to-all | bytes 589824 | tf_op jit(solution)/shard_map/all_to_all | solution.py:444
  74.5 0.6 sum2.1.after_ref.own_ref
  75.1 1.2 %collective-permute-start.3 = (bf16[64,1536]{1,0:T(8,128)(2,1)S(1)}, bf16[64,1536]{1,0:T(8,128)(2,1)S(1)}, u32[]{:S(2)}, u32[]{:S(2)}) collective-permute-start(bf16[64,1536]{1,0:T(8,128)(2,1)S(1)} %sum2.1.after_ref.own_ref), channel_id=1, source_target_pairs={{0,3},{1,0},{2,1},{3,2},{4,7},{5,4},{6,5},{7,6},{8,11},{9,8},{10,9... | collective-permute-start | bytes 589832 | tf_op jit(solution)/shard_map/ppermute | solution.py:438
  76.4 1.5 %collective-permute-start.2 = (bf16[64,1536]{1,0:T(8,128)(2,1)S(1)}, bf16[64,1536]{1,0:T(8,128)(2,1)S(1)}, u32[]{:S(2)}, u32[]{:S(2)}) collective-permute-start(bf16[64,1536]{1,0:T(8,128)(2,1)S(1)} %sum2.1.after_ref.own_ref), channel_id=1, source_target_pairs={{0,2},{1,3},{2,0},{3,1},{4,6},{5,7},{6,4},{7,5},{8,10},{9,11},{10,... | collective-permute-start | bytes 589832 | tf_op jit(solution)/shard_map/ppermute | solution.py:438
  77.8 2.0 %rhs.3.after_ref.rhs_ref = f32[64,1024]{1,0:T(8,128)S(1)} custom-call(s32[52,128]{1,0:T(8,128)S(1)} %get-tuple-element.17.slot_ref, f32[6656,128]{1,0:T(8,128)S(1)} %get-tuple-element.23.both_ref, bf16[64,1536]{1,0:T(8,128)(2,1)S(1)} %sum2.1.after_ref.own_ref), custom_call_target="tpu_custom_call" | custom-call | tf_op jit(solution)/shard_map/rhs/pallas_call | solution.py:176
  79.9 3.2 %collective-permute-done.3.third_ref = bf16[64,1536]{1,0:T(8,128)(2,1)S(1)} collective-permute-done((bf16[64,1536]{1,0:T(8,128)(2,1)S(1)}, bf16[64,1536]{1,0:T(8,128)(2,1)S(1)}, u32[]{:S(2)}, u32[]{:S(2)}) %collective-permute-start.3) | collective-permute-done | bytes 196640 | tf_op jit(solution)/shard_map/ppermute | solution.py:438
  83.0 2.7 %collective-permute-done.2.second_ref = bf16[64,1536]{1,0:T(8,128)(2,1)S(1)} collective-permute-done((bf16[64,1536]{1,0:T(8,128)(2,1)S(1)}, bf16[64,1536]{1,0:T(8,128)(2,1)S(1)}, u32[]{:S(2)}, u32[]{:S(2)}) %collective-permute-start.2) | collective-permute-done | bytes 196640 | tf_op jit(solution)/shard_map/ppermute | solution.py:438
  85.7 2.2 %collective-permute-done.1.first_ref = bf16[64,1536]{1,0:T(8,128)(2,1)S(1)} collective-permute-done((bf16[64,1536]{1,0:T(8,128)(2,1)S(1)}, bf16[64,1536]{1,0:T(8,128)(2,1)S(1)}, u32[]{:S(2)}, u32[]{:S(2)}) %collective-permute-start.1) | collective-permute-done | bytes 196640 | tf_op jit(solution)/shard_map/ppermute | solution.py:438
  87.9 2.7 %level2.1 = (f32[64,6656]{1,0:T(8,128)}, bf16[8,3,72,128]{3,2,1,0:T(8,128)(2,1)S(1)}) custom-call(s32[4]{0:T(128)S(1)} %copy-done.8, bf16[64,1536]{1,0:T(8,128)(2,1)S(1)} %sum2.1.after_ref.own_ref, bf16[64,1536]{1,0:T(8,128)(2,1)S(1)} %collective-permute-done.1.first_ref, ...), custom_call_target="tpu_custom_call", output_to_operand_aliasing={{0}: (9, {})} | custom-call | tf_op jit(solution)/shard_map/level2/pallas_call | solution.py:568
  90.6 14.5 %all_to_all.22.got_ref = bf16[8,3,72,128]{3,2,1,0:T(8,128)(2,1)S(1)} all-to-all(bf16[8,3,72,128]{3,2,1,0:T(8,128)(2,1)S(1)} %get-tuple-element.27), channel_id=1, replica_groups=mesh['z'=4,'x1'=2,'x0'=2,'core'=2,'front'=4] {'x1','front'}, dimensions={0} | all-to-all | bytes 884736 | tf_op jit(solution)/shard_map/all_to_all | solution.py:444
  105.1 0.4 sum3.1.own_ref
  105.5 1.0 collective-permute-start.6
  106.6 1.5 %collective-permute-start.5 = (bf16[64,1024]{1,0:T(8,128)(2,1)S(1)}, bf16[64,1024]{1,0:T(8,128)(2,1)S(1)}, u32[]{:S(2)}, u32[]{:S(2)}) collective-permute-start(bf16[64,1024]{1,0:T(8,128)(2,1)S(1)} %sum3.1.own_ref), channel_id=1, source_target_pairs={{0,2},{1,3},{2,0},{3,1},{4,6},{5,7},{6,4},{7,5},{8,10},{9,11},{10,... | collective-permute-start | bytes 393224 | tf_op jit(solution)/shard_map/ppermute | solution.py:438
  108.0 2.5 %collective-permute-done.6.third_ref = bf16[64,1024]{1,0:T(8,128)(2,1)S(1)} collective-permute-done((bf16[64,1024]{1,0:T(8,128)(2,1)S(1)}, bf16[64,1024]{1,0:T(8,128)(2,1)S(1)}, u32[]{:S(2)}, u32[]{:S(2)}) %collective-permute-start.6) | collective-permute-done | bytes 131104 | tf_op jit(solution)/shard_map/ppermute | solution.py:438
  110.6 2.5 %collective-permute-done.5.second_ref = bf16[64,1024]{1,0:T(8,128)(2,1)S(1)} collective-permute-done((bf16[64,1024]{1,0:T(8,128)(2,1)S(1)}, bf16[64,1024]{1,0:T(8,128)(2,1)S(1)}, u32[]{:S(2)}, u32[]{:S(2)}) %collective-permute-start.5) | collective-permute-done | bytes 131104 | tf_op jit(solution)/shard_map/ppermute | solution.py:438
  113.1 1.4 %collective-permute-done.4.first_ref = bf16[64,1024]{1,0:T(8,128)(2,1)S(1)} collective-permute-done((bf16[64,1024]{1,0:T(8,128)(2,1)S(1)}, bf16[64,1024]{1,0:T(8,128)(2,1)S(1)}, u32[]{:S(2)}, u32[]{:S(2)}) %collective-permute-start.4) | collective-permute-done | bytes 131104 | tf_op jit(solution)/shard_map/ppermute | solution.py:438
  114.5 1.5 %level3.1 = f32[64,6656]{1,0:T(8,128)} custom-call(bf16[64,1024]{1,0:T(8,128)(2,1)S(1)} %sum3.1.own_ref, bf16[64,1024]{1,0:T(8,128)(2,1)S(1)} %collective-permute-done.4.first_ref, bf16[64,1024]{1,0:T(8,128)(2,1)S(1)} %collective-permute-done.5.second_ref, bf16[64,1024]{1,0:T(8,128)(2,1)S(1)} %collective-permute-done.6.third_ref, ...), custom_call_target="tpu_custom_call", output_to_operand_aliasing={{}: (5, {})} | custom-call | tf_op jit(solution)/shard_map/level3/pallas_call | solution.py:607
  (23 shorter events, 0.1 us)
Async XLA Ops:
  0.0 0.7 copy-start.3
  3.2 20.4 %all-to-all-start = ((s32[128,1,128]{2,1,0:T(1,128)}), s32[128,1,128]{2,1,0:T(1,128)S(1)}, u32[]{:S(2)}, u32[]{:S(2)}) async-start(s32[128,1,128]{2,1,0:T(1,128)} %bitcast.2), calls=%async_computation | async-start | bytes 131072 | tf_op jit(solution)/shard_map/all_to_all | solution.py:444
  14.3 1.5 %copy-start.2 = (f32[64,6656]{1,0:T(8,128)S(1)}, f32[64,6656]{1,0:T(8,128)}, u32[]{:S(2)}) copy-start(f32[64,6656]{1,0:T(8,128)} %wide_ref.1) | copy-start | bytes 5111812
  23.6 28.6 %copy-start.6 = (s32[4,256]{1,0:T(4,128)S(1)}, s32[4,256]{1,0:T(4,128)}, u32[]{:S(2)}) copy-start(s32[4,256]{1,0:T(4,128)} %rows_ref.3) | copy-start | bytes 12292
  23.6 28.6 %copy-start.9 = (s32[4]{0:T(128)S(1)}, s32[4]{0:T(128)}, u32[]{:S(2)}) copy-start(s32[4]{0:T(128)} %parent_ref.1) | copy-start | bytes 52
  58.3 2.8 %copy-start.5 = (s32[2,512]{1,0:T(2,128)S(1)}, s32[2,512]{1,0:T(2,128)}, u32[]{:S(2)}) copy-start(s32[2,512]{1,0:T(2,128)} %rows_ref.4) | copy-start | bytes 12292
  58.3 2.8 %copy-start.7 = (s32[2]{0:T(128)S(1)}, s32[2]{0:T(128)}, u32[]{:S(2)}) copy-start(s32[2]{0:T(128)} %parent_vmem.2) | copy-start | bytes 28
  58.3 2.7 %collective-permute-start = (bf16[2,72,256]{2,1,0:T(8,128)(2,1)S(1)}, bf16[2,72,256]{2,1,0:T(8,128)(2,1)S(1)}, u32[]{:S(2)}, u32[]{:S(2)}) collective-permute-start(bf16[2,72,256]{2,1,0:T(8,128)(2,1)S(1)} %get-tuple-element.19.after_ref), channel_id=1, source_target_pairs={{0,4},{4,0},{1,5},{5,1},{2,6},{6,2},{3,7},{7,3},{8,12},{12,8},{9,1... | collective-permute-start | bytes 221192 | tf_op jit(solution)/shard_map/ppermute | solution.py:529
  61.1 26.8 %slice-start = ((s8[4718592]{0:T(1024)(128)(4,1)}), s8[4194304]{0:T(1024)(128)(4,1)S(1)}, s32[]{:S(2)}) async-start(s8[4718592]{0:T(1024)(128)(4,1)} %bitcast.7), calls=%async_computation.4 | async-start | bytes 8388608
  61.1 26.8 %slice-start.1 = ((s8[4718592]{0:T(1024)(128)(4,1)}), s8[524288]{0:T(1024)(128)(4,1)S(1)}, s32[]{:S(2)}) async-start(s8[4718592]{0:T(1024)(128)(4,1)} %bitcast.7), calls=%async_computation.5 | async-start | bytes 1048576
  75.1 12.8 %copy-start.1 = (bf16[4,384,768]{2,1,0:T(8,128)(2,1)S(1)}, bf16[4,384,768]{2,1,0:T(8,128)(2,1)}, u32[]{:S(2)}) copy-start(bf16[4,384,768]{2,1,0:T(8,128)(2,1)} %update_ref.1) | copy-start | bytes 7077892
  75.1 12.8 %copy-start.4 = (s32[4,768]{1,0:T(4,128)S(1)}, s32[4,768]{1,0:T(4,128)}, u32[]{:S(2)}) copy-start(s32[4,768]{1,0:T(4,128)} %rows_ref.5) | copy-start | bytes 36868
  75.1 12.8 %copy-start.8 = (s32[4]{0:T(128)S(1)}, s32[4]{0:T(128)}, u32[]{:S(2)}) copy-start(s32[4]{0:T(128)} %parent_vmem.3) | copy-start | bytes 52
  75.1 7.9 %collective-permute-start.3 = (bf16[64,1536]{1,0:T(8,128)(2,1)S(1)}, bf16[64,1536]{1,0:T(8,128)(2,1)S(1)}, u32[]{:S(2)}, u32[]{:S(2)}) collective-permute-start(bf16[64,1536]{1,0:T(8,128)(2,1)S(1)} %sum2.1.after_ref.own_ref), channel_id=1, source_target_pairs={{0,3},{1,0},{2,1},{3,2},{4,7},{5,4},{6,5},{7,6},{8,11},{9,8},{10,9... | collective-permute-start | bytes 589832 | tf_op jit(solution)/shard_map/ppermute | solution.py:438
  76.4 9.3 %collective-permute-start.2 = (bf16[64,1536]{1,0:T(8,128)(2,1)S(1)}, bf16[64,1536]{1,0:T(8,128)(2,1)S(1)}, u32[]{:S(2)}, u32[]{:S(2)}) collective-permute-start(bf16[64,1536]{1,0:T(8,128)(2,1)S(1)} %sum2.1.after_ref.own_ref), channel_id=1, source_target_pairs={{0,2},{1,3},{2,0},{3,1},{4,6},{5,7},{6,4},{7,5},{8,10},{9,11},{10,... | collective-permute-start | bytes 589832 | tf_op jit(solution)/shard_map/ppermute | solution.py:438
  77.8 10.0 %collective-permute-start.1 = (bf16[64,1536]{1,0:T(8,128)(2,1)S(1)}, bf16[64,1536]{1,0:T(8,128)(2,1)S(1)}, u32[]{:S(2)}, u32[]{:S(2)}) collective-permute-start(bf16[64,1536]{1,0:T(8,128)(2,1)S(1)} %sum2.1.after_ref.own_ref), channel_id=1, source_target_pairs={{0,1},{1,2},{2,3},{3,0},{4,5},{5,6},{6,7},{7,4},{8,9},{9,10},{10,1... | collective-permute-start | bytes 589832 | tf_op jit(solution)/shard_map/ppermute | solution.py:438
  87.9 26.6 %copy-start = (bf16[2,2048,512]{2,1,0:T(8,128)(2,1)S(1)}, bf16[2,2048,512]{2,1,0:T(8,128)(2,1)}, u32[]{:S(2)}) copy-start(bf16[2,2048,512]{2,1,0:T(8,128)(2,1)} %inverse_ref.3) | copy-start | bytes 12582916
  105.5 5.0 %collective-permute-start.6 = (bf16[64,1024]{1,0:T(8,128)(2,1)S(1)}, bf16[64,1024]{1,0:T(8,128)(2,1)S(1)}, u32[]{:S(2)}, u32[]{:S(2)}) collective-permute-start(bf16[64,1024]{1,0:T(8,128)(2,1)S(1)} %sum3.1.own_ref), channel_id=1, source_target_pairs={{0,3},{1,0},{2,1},{3,2},{4,7},{5,4},{6,5},{7,6},{8,11},{9,8},{10,9... | collective-permute-start | bytes 393224 | tf_op jit(solution)/shard_map/ppermute | solution.py:438
  106.6 6.5 %collective-permute-start.5 = (bf16[64,1024]{1,0:T(8,128)(2,1)S(1)}, bf16[64,1024]{1,0:T(8,128)(2,1)S(1)}, u32[]{:S(2)}, u32[]{:S(2)}) collective-permute-start(bf16[64,1024]{1,0:T(8,128)(2,1)S(1)} %sum3.1.own_ref), channel_id=1, source_target_pairs={{0,2},{1,3},{2,0},{3,1},{4,6},{5,7},{6,4},{7,5},{8,10},{9,11},{10,... | collective-permute-start | bytes 393224 | tf_op jit(solution)/shard_map/ppermute | solution.py:438
  108.0 6.4 %collective-permute-start.4 = (bf16[64,1024]{1,0:T(8,128)(2,1)S(1)}, bf16[64,1024]{1,0:T(8,128)(2,1)S(1)}, u32[]{:S(2)}, u32[]{:S(2)}) collective-permute-start(bf16[64,1024]{1,0:T(8,128)(2,1)S(1)} %sum3.1.own_ref), channel_id=1, source_target_pairs={{0,1},{1,2},{2,3},{3,0},{4,5},{5,6},{6,7},{7,4},{8,9},{9,10},{10,1... | collective-permute-start | bytes 393224 | tf_op jit(solution)/shard_map/ppermute | solution.py:438

commit v7 on v6

--- a/solution.py
+++ b/solution.py
@@ -323,18 +323,35 @@
     out_ref[...] = (rhs_ref[...] - total).astype(bf16)
 
 
-def gathered(pieces, rhs_ref):
+def ahead(k, share):
     front = lax.axis_index("front")
-    for k, piece in enumerate(pieces):
-        rhs_ref[(front + FRONT - k) & (FRONT - 1)] = piece[...]
+    return pl.ds(pl.multiple_of(((front + FRONT - k) & (FRONT - 1)) * share, share), share)
+
+
+def part_kernel(own_ref, third_ref, second_ref, inverse_ref, part_ref):
+    nodes, share = inverse_ref.shape[0], inverse_ref.shape[2]
+    for c in range(nodes):
+        own = slice(c * share, (c + 1) * share)
+        total = mm(own_ref[:, own], inverse_ref[c, ahead(0, share), :])
+        total = total + mm(third_ref[:, own], inverse_ref[c, ahead(3, share), :])
+        part_ref[:, own] = total + mm(second_ref[:, own], inverse_ref[c, ahead(2, share), :])
+
+
+def three_pieces(side, pieces, inverse):
+    return pl.pallas_call(
+        part_kernel,
+        in_specs=[VMEM] * 4,
+        out_specs=VMEM,
+        out_shape=struct(side.shape, f32),
+        compiler_params=params(6),
+        name="part",
+    )(side, pieces[2], pieces[1], inverse)
 
 
 def level2_kernel(
     parent_vmem,
-    own_ref,
+    part_ref,
     first_ref,
-    second_ref,
-    third_ref,
     rows_ref,
     inverse_ref,
     update_ref,
@@ -345,18 +362,15 @@
     sol_ref,
     terms_ref,
     terms_rows,
-    rhs_ref,
     parent_ref,
     sems,
 ):
     del out_in, after_ref
     load = pltpu.make_async_copy(parent_vmem, parent_ref, sems.at[1])
     load.start()
-    gathered((own_ref, first_ref, second_ref, third_ref), rhs_ref)
     for c in range(NODES2):
         own = slice(c * SHARE2, (c + 1) * SHARE2)
-        lhs = jnp.concatenate([rhs_ref[g, :, own] for g in range(FRONT)], axis=1)
-        sol = mm(lhs, inverse_ref[c])
+        sol = part_ref[:, own] + mm(first_ref[:, own], inverse_ref[c, ahead(1, SHARE2), :])
         sol_ref[:, own] = sol
         if c == 0:
             load.wait()
@@ -406,24 +420,20 @@
 
 
 def level3_kernel(
-    own_ref,
+    part_ref,
     first_ref,
-    second_ref,
-    third_ref,
     inverse_ref,
     out_in,
     out_hbm,
     sol_ref,
-    rhs_ref,
     sems,
 ):
     del out_in
-    gathered((own_ref, first_ref, second_ref, third_ref), rhs_ref)
     stores = []
     for c in range(NODES3):
         own = slice(c * SHARE3, (c + 1) * SHARE3)
-        lhs = jnp.concatenate([rhs_ref[g, :, own] for g in range(FRONT)], axis=1)
-        sol_ref[:, own] = mm(lhs, inverse_ref[c])
+        last = mm(first_ref[:, own], inverse_ref[c, ahead(1, SHARE3), :])
+        sol_ref[:, own] = part_ref[:, own] + last
         part = slice(EDGE2 + c * SHARE3, EDGE2 + (c + 1) * SHARE3)
         stores.append(
             pltpu.make_async_copy(sol_ref.at[:, own], out_hbm.at[:, part], sems.at[c])
@@ -567,7 +577,7 @@
     rhs3 = late_rhs(EDGE2, ROWS, slot, both, side2)
     out, send2 = pl.pallas_call(
         level2_kernel,
-        in_specs=[VMEM] * 9 + [HBM],
+        in_specs=[VMEM] * 7 + [HBM],
         out_specs=[HBM, VMEM],
         out_shape=[
             struct((RHS, ROWS), f32),
@@ -577,17 +587,16 @@
             pltpu.VMEM((RHS, NODES2 * SHARE2), f32),
             pltpu.VMEM((2 * NODES3, RHS, BORDER2), f32),
             pltpu.VMEM((2 * NODES3, 8, BORDER2), i32),
-            pltpu.VMEM((FRONT, RHS, NODES2 * SHARE2), bf16),
             pltpu.SMEM((NODES2,), i32),
             pltpu.SemaphoreType.DMA((2,)),
         ],
-        input_output_aliases={9: 0},
+        input_output_aliases={7: 0},
         compiler_params=params(24),
         name="level2",
     )(
         level2_parent_node,
-        side2,
-        *pieces,
+        three_pieces(side2, pieces, level2_diagonal_inverse),
+        pieces[0],
         level2_parent_rows,
         level2_diagonal_inverse,
         level2_update_block,
@@ -606,18 +615,22 @@
     pieces = front_pieces(side3)
     return pl.pallas_call(
         level3_kernel,
-        in_specs=[VMEM] * 5 + [HBM],
+        in_specs=[VMEM] * 3 + [HBM],
         out_specs=HBM,
         out_shape=struct((RHS, ROWS), f32),
         scratch_shapes=[
             pltpu.VMEM((RHS, NODES3 * SHARE3), f32),
-            pltpu.VMEM((FRONT, RHS, NODES3 * SHARE3), bf16),
             pltpu.SemaphoreType.DMA((NODES3,)),
         ],
-        input_output_aliases={5: 0},
+        input_output_aliases={3: 0},
         compiler_params=params(24),
         name="level3",
-    )(side3, *pieces, level3_diagonal_inverse, out)
+    )(
+        three_pieces(side3, pieces, level3_diagonal_inverse),
+        pieces[0],
+        level3_diagonal_inverse,
+        out,
+    )
 
 
 def solution(mesh):

time: 116 us -> 115 us (level)
  waiting for transfers between devices: 21.2 us -> 18.1 us
  starting transfers between devices: 16.6 us -> 17.8 us
    ppermute x6, waiting for transfers between devices: 14.4 us -> 11.3 us  [front_pieces(): lax.ppermute(side, 'front', [(f, (f + k) % FRONT) for f in range(FRONT)])]
    ppermute x6, starting transfers between devices: 5.23 us -> 6.45 us  [front_pieces(): lax.ppermute(side, 'front', [(f, (f + k) % FRONT) for f in range(FRONT)])]
    pallas_call x2 -> x4, Pallas kernels: 4.21 us -> 4.39 us  [the longest x1 2.08 us: per_device(): pl.pallas_call(level2_kernel, in_specs=[VMEM] * 7 + [HBM], out_specs=[HBM...]
  transfers between devices with their start and end apart: 8 -> 8, of which waited for: 7 -> 6; matrix products, arithmetic and copies ran while one was open for 0% -> 0% of each run, Pallas kernels for 5% -> 6%
where the time goes in v7:
time: 115 us; the launch traced here: 114 us
  blocking collectives  47.2 us (41%)
  Pallas kernels  28.8 us (25%)
  waiting for transfers between devices  18.1 us (16%)
  starting transfers between devices  17.8 us (15%)
  local copies, waits for them, and re-layouts  2.25 us (2%)
    all_to_all x3, blocking collectives, exchange(): return lax.all_to_all(block, axes, split_axis=0, concat_axis=0, tiled=True)  47.2 us
    ppermute x6, waiting for transfers between devices, front_pieces(): lax.ppermute(side, 'front', [(f, (f + k) % FRONT) for f in range(FRONT)])  11.3 us
    all_to_all x1, starting transfers between devices, exchange(): return lax.all_to_all(block, axes, split_axis=0, concat_axis=0, tiled=True)  11.1 us
    pallas_call x1, Pallas kernels, per_device(): pl.pallas_call(pick_kernel, in_specs=[VMEM, VMEM], out_specs=HBM, out_sha...  7.08 us
    all_to_all x1, waiting for transfers between devices, exchange(): return lax.all_to_all(block, axes, split_axis=0, concat_axis=0, tiled=True)  6.84 us
    ppermute x6, starting transfers between devices, front_pieces(): lax.ppermute(side, 'front', [(f, (f + k) % FRONT) for f in range(FRONT)])  6.45 us
    pallas_call x1, Pallas kernels, per_device(): pl.pallas_call(leaf_kernel, in_specs=[SMEM, SMEM, VMEM, VMEM, HBM, HBM, H...  6.08 us
    pallas_call x2, Pallas kernels, late_rhs(): pl.pallas_call(functools.partial(rhs_kernel, first, last), in_specs=[SMEM...  4.55 us
  transfers between devices with their start and end apart: 8, of which 6 were waited for; matrix products, arithmetic and copies ran while one was open for 0% of the time, Pallas kernels for 6%

profile of v7, /device:TPU:0, one launch (start us, length us, event | category | flops | bytes accessed | tf_op | source)
XLA Modules:
  0.0 114.3 jit_solution(10640815776523284161)
XLA Ops:
  0.0 0.7 copy-done.3
  0.7 2.4 %rank.1 = (s32[128,128]{1,0:T(8,128)}, s32[52,128]{1,0:T(8,128)S(1)}) custom-call(s32[52,128]{1,0:T(8,128)S(1)} %bitcast.11), custom_call_target="tpu_custom_call" | custom-call | tf_op jit(solution)/shard_map/rank/pallas_call | solution.py:474
  3.2 11.1 %all-to-all-start = ((s32[128,1,128]{2,1,0:T(1,128)}), s32[128,1,128]{2,1,0:T(1,128)S(1)}, u32[]{:S(2)}, u32[]{:S(2)}) async-start(s32[128,1,128]{2,1,0:T(1,128)} %bitcast.2), calls=%async_computation | async-start | bytes 131072 | tf_op jit(solution)/shard_map/all_to_all | solution.py:454
  14.4 1.4 %copy-done.2 = f32[64,6656]{1,0:T(8,128)S(1)} copy-done((f32[64,6656]{1,0:T(8,128)S(1)}, f32[64,6656]{1,0:T(8,128)}, u32[]{:S(2)}) %copy-start.2) | copy-done | bytes 1703960
  15.8 0.9 tall.1.tall_ref
  16.7 6.8 %all-to-all-done = s32[128,1,128]{2,1,0:T(1,128)S(1)} async-done(((s32[128,1,128]{2,1,0:T(1,128)}), s32[128,1,128]{2,1,0:T(1,128)S(1)}, u32[]{:S(2)}, u32[]{:S(2)}) %all-to-all-start) | async-done | bytes 65568 | tf_op jit(solution)/shard_map/all_to_all | solution.py:454
  23.6 7.1 %pick.1 = bf16[3328,128]{1,0:T(8,128)(2,1)} custom-call(s32[128,128]{1,0:T(8,128)S(1)} %bitcast.10, f32[6656,128]{1,0:T(8,128)S(1)} %tall.1.tall_ref), custom_call_target="tpu_custom_call" | custom-call | tf_op jit(solution)/shard_map/pick/pallas_call | solution.py:491
  30.7 21.6 %all_to_all.20 = bf16[128,13,2,128]{3,2,1,0:T(2,128)(2,1)S(1)} all-to-all(bf16[128,13,2,128]{3,2,1,0:T(2,128)(2,1)} %bitcast.12), channel_id=1, replica_groups=mesh['z'=4,'x1'=2,'x0'=2,'core'=2,'front'=4] {'z','x1','x0','core','front'}, dimensions={0} | all-to-all | bytes 1703936 | tf_op jit(solution)/shard_map/all_to_all | solution.py:454
  52.2 6.1 %leaf.1 = (f32[64,6656]{1,0:T(8,128)}, bf16[2,72,256]{2,1,0:T(8,128)(2,1)S(1)}, f32[2,64,1024]{2,1,0:T(8,128)S(1)}, f32[6656,128]{1,0:T(8,128)S(1)}, bf16[2,1024...) custom-call(s32[52,128]{1,0:T(8,128)S(1)} %get-tuple-element.17.slot_ref, s32[4]{0:T(128)S(1)} %copy-done.8, ...), custom_call_target="tpu_custom_call" | custom-call | tf_op jit(solution)/shard_map/leaf/pallas_call | solution.py:506
  58.3 0.0 copy-start.5
  58.3 0.2 collective-permute-start
  58.5 2.5 %rhs.2.after_ref.rhs_ref = f32[64,1536]{1,0:T(8,128)S(1)} custom-call(s32[52,128]{1,0:T(8,128)S(1)} %get-tuple-element.17.slot_ref, f32[6656,128]{1,0:T(8,128)S(1)} %get-tuple-element.23.both_ref, bf16[2,72,256]{2,1,0:T(8,128)(2,1)S(1)} %get-tuple-element.19.after_ref), custom_call_target="tpu_custom_call" | custom-call | tf_op jit(solution)/shard_map/rhs/pallas_call | solution.py:176
  61.1 0.0 slice-start
  61.1 2.3 %level1.1 = (f32[64,6656]{1,0:T(8,128)}, bf16[8,2,72,128]{3,2,1,0:T(8,128)(2,1)S(1)}) custom-call(s32[2]{0:T(128)S(1)} %copy-done.7, bf16[2,72,256]{2,1,0:T(8,128)(2,1)S(1)} %collective-permute-done.got_ref, f32[2,64,1024]{2,1,0:T(8,128)S(1)} %get-tuple-element.20.rhs_ref, s32[2,512]{1,0:T(2,128)S(1)} %copy-done.5, ...), custom_call_target="tpu_custom_call", output_to_operand_aliasing={{0}: (7, {})} | custom-call | tf_op jit(solution)/shard_map/level1/pallas_call | solution.py:541
  63.4 11.0 %all_to_all.21.got_ref = bf16[8,2,72,128]{3,2,1,0:T(8,128)(2,1)S(1)} all-to-all(bf16[8,2,72,128]{3,2,1,0:T(8,128)(2,1)S(1)} %get-tuple-element.25), channel_id=1, replica_groups=mesh['z'=4,'x1'=2,'x0'=2,'core'=2,'front'=4] {'x0','front'}, dimensions={0} | all-to-all | bytes 589824 | tf_op jit(solution)/shard_map/all_to_all | solution.py:454
  74.4 0.6 sum2.1.own_ref.after_ref
  75.0 1.2 %collective-permute-start.2 = (bf16[64,1536]{1,0:T(8,128)(2,1)S(1)}, bf16[64,1536]{1,0:T(8,128)(2,1)S(1)}, u32[]{:S(2)}, u32[]{:S(2)}) collective-permute-start(bf16[64,1536]{1,0:T(8,128)(2,1)S(1)} %sum2.1.own_ref.after_ref), channel_id=1, source_target_pairs={{0,2},{1,3},{2,0},{3,1},{4,6},{5,7},{6,4},{7,5},{8,10},{9,11},{10,... | collective-permute-start | bytes 589832 | tf_op jit(solution)/shard_map/ppermute | solution.py:448
  76.3 2.1 %collective-permute-start.1 = (bf16[64,1536]{1,0:T(8,128)(2,1)S(1)}, bf16[64,1536]{1,0:T(8,128)(2,1)S(1)}, u32[]{:S(2)}, u32[]{:S(2)}) collective-permute-start(bf16[64,1536]{1,0:T(8,128)(2,1)S(1)} %sum2.1.own_ref.after_ref), channel_id=1, source_target_pairs={{0,3},{1,0},{2,1},{3,2},{4,7},{5,4},{6,5},{7,6},{8,11},{9,8},{10,9... | collective-permute-start | bytes 589832 | tf_op jit(solution)/shard_map/ppermute | solution.py:448
  78.4 2.0 %rhs.3.after_ref.rhs_ref = f32[64,1024]{1,0:T(8,128)S(1)} custom-call(s32[52,128]{1,0:T(8,128)S(1)} %get-tuple-element.17.slot_ref, f32[6656,128]{1,0:T(8,128)S(1)} %get-tuple-element.23.both_ref, bf16[64,1536]{1,0:T(8,128)(2,1)S(1)} %sum2.1.own_ref.after_ref), custom_call_target="tpu_custom_call" | custom-call | tf_op jit(solution)/shard_map/rhs/pallas_call | solution.py:176
  80.4 4.0 %collective-permute-done.2.second_ref = bf16[64,1536]{1,0:T(8,128)(2,1)S(1)} collective-permute-done((bf16[64,1536]{1,0:T(8,128)(2,1)S(1)}, bf16[64,1536]{1,0:T(8,128)(2,1)S(1)}, u32[]{:S(2)}, u32[]{:S(2)}) %collective-permute-start.2) | collective-permute-done | bytes 196640 | tf_op jit(solution)/shard_map/ppermute | solution.py:448
  84.5 0.8 collective-permute-done.1.third_ref
  85.3 0.7 part.2.part_ref
  86.0 0.9 collective-permute-done.3.first_ref
  86.9 2.1 %level2.1 = (f32[64,6656]{1,0:T(8,128)}, bf16[8,3,72,128]{3,2,1,0:T(8,128)(2,1)S(1)}) custom-call(s32[4]{0:T(128)S(1)} %copy-done.9, f32[64,1536]{1,0:T(8,128)S(1)} %part.2.part_ref, bf16[64,1536]{1,0:T(8,128)(2,1)S(1)} %collective-permute-done.3.first_ref, s32[4,768]{1,0:T(4,128)S(1)} %copy-done.4, ...), custom_call_target="tpu_custom_call", output_to_operand_aliasing={{0}: (7, {})} | custom-call | tf_op jit(solution)/shard_map/level2/pallas_call | solution.py:578
  89.0 14.6 %all_to_all.22.got_ref = bf16[8,3,72,128]{3,2,1,0:T(8,128)(2,1)S(1)} all-to-all(bf16[8,3,72,128]{3,2,1,0:T(8,128)(2,1)S(1)} %get-tuple-element.27), channel_id=1, replica_groups=mesh['z'=4,'x1'=2,'x0'=2,'core'=2,'front'=4] {'x1','front'}, dimensions={0} | all-to-all | bytes 884736 | tf_op jit(solution)/shard_map/all_to_all | solution.py:454
  103.6 0.4 sum3.1.own_ref
  104.0 0.9 collective-permute-start.5
  105.0 2.2 %collective-permute-start.4 = (bf16[64,1024]{1,0:T(8,128)(2,1)S(1)}, bf16[64,1024]{1,0:T(8,128)(2,1)S(1)}, u32[]{:S(2)}, u32[]{:S(2)}) collective-permute-start(bf16[64,1024]{1,0:T(8,128)(2,1)S(1)} %sum3.1.own_ref), channel_id=1, source_target_pairs={{0,3},{1,0},{2,1},{3,2},{4,7},{5,4},{6,5},{7,6},{8,11},{9,8},{10,9... | collective-permute-start | bytes 393224 | tf_op jit(solution)/shard_map/ppermute | solution.py:448
  107.2 3.5 %collective-permute-done.5.second_ref = bf16[64,1024]{1,0:T(8,128)(2,1)S(1)} collective-permute-done((bf16[64,1024]{1,0:T(8,128)(2,1)S(1)}, bf16[64,1024]{1,0:T(8,128)(2,1)S(1)}, u32[]{:S(2)}, u32[]{:S(2)}) %collective-permute-start.5) | collective-permute-done | bytes 131104 | tf_op jit(solution)/shard_map/ppermute | solution.py:448
  110.7 0.7 part.3.part_ref
  111.3 2.0 %collective-permute-done.6.first_ref = bf16[64,1024]{1,0:T(8,128)(2,1)S(1)} collective-permute-done((bf16[64,1024]{1,0:T(8,128)(2,1)S(1)}, bf16[64,1024]{1,0:T(8,128)(2,1)S(1)}, u32[]{:S(2)}, u32[]{:S(2)}) %collective-permute-start.6) | collective-permute-done | bytes 131104 | tf_op jit(solution)/shard_map/ppermute | solution.py:448
  113.3 1.0 level3.1
  (25 shorter events, 0.1 us)
Async XLA Ops:
  0.0 0.7 copy-start.3
  3.2 20.4 %all-to-all-start = ((s32[128,1,128]{2,1,0:T(1,128)}), s32[128,1,128]{2,1,0:T(1,128)S(1)}, u32[]{:S(2)}, u32[]{:S(2)}) async-start(s32[128,1,128]{2,1,0:T(1,128)} %bitcast.2), calls=%async_computation | async-start | bytes 131072 | tf_op jit(solution)/shard_map/all_to_all | solution.py:454
  14.3 1.5 %copy-start.2 = (f32[64,6656]{1,0:T(8,128)S(1)}, f32[64,6656]{1,0:T(8,128)}, u32[]{:S(2)}) copy-start(f32[64,6656]{1,0:T(8,128)} %wide_ref.1) | copy-start | bytes 5111812
  23.6 28.6 %copy-start.6 = (s32[4,256]{1,0:T(4,128)S(1)}, s32[4,256]{1,0:T(4,128)}, u32[]{:S(2)}) copy-start(s32[4,256]{1,0:T(4,128)} %rows_ref.3) | copy-start | bytes 12292
  23.6 28.6 %copy-start.8 = (s32[4]{0:T(128)S(1)}, s32[4]{0:T(128)}, u32[]{:S(2)}) copy-start(s32[4]{0:T(128)} %parent_ref.1) | copy-start | bytes 52
  58.3 2.8 %copy-start.5 = (s32[2,512]{1,0:T(2,128)S(1)}, s32[2,512]{1,0:T(2,128)}, u32[]{:S(2)}) copy-start(s32[2,512]{1,0:T(2,128)} %rows_ref.4) | copy-start | bytes 12292
  58.3 2.8 %copy-start.7 = (s32[2]{0:T(128)S(1)}, s32[2]{0:T(128)}, u32[]{:S(2)}) copy-start(s32[2]{0:T(128)} %parent_vmem.2) | copy-start | bytes 28
  58.3 2.7 %collective-permute-start = (bf16[2,72,256]{2,1,0:T(8,128)(2,1)S(1)}, bf16[2,72,256]{2,1,0:T(8,128)(2,1)S(1)}, u32[]{:S(2)}, u32[]{:S(2)}) collective-permute-start(bf16[2,72,256]{2,1,0:T(8,128)(2,1)S(1)} %get-tuple-element.19.after_ref), channel_id=1, source_target_pairs={{0,4},{4,0},{1,5},{5,1},{2,6},{6,2},{3,7},{7,3},{8,12},{12,8},{9,1... | collective-permute-start | bytes 221192 | tf_op jit(solution)/shard_map/ppermute | solution.py:539
  61.1 24.3 %slice-start = ((s8[4718592]{0:T(1024)(128)(4,1)}), s8[4194304]{0:T(1024)(128)(4,1)S(1)}, s32[]{:S(2)}) async-start(s8[4718592]{0:T(1024)(128)(4,1)} %bitcast.7), calls=%async_computation.4 | async-start | bytes 8388608
  61.1 24.2 %slice-start.1 = ((s8[4718592]{0:T(1024)(128)(4,1)}), s8[524288]{0:T(1024)(128)(4,1)S(1)}, s32[]{:S(2)}) async-start(s8[4718592]{0:T(1024)(128)(4,1)} %bitcast.7), calls=%async_computation.5 | async-start | bytes 1048576
  75.0 9.4 %collective-permute-start.2 = (bf16[64,1536]{1,0:T(8,128)(2,1)S(1)}, bf16[64,1536]{1,0:T(8,128)(2,1)S(1)}, u32[]{:S(2)}, u32[]{:S(2)}) collective-permute-start(bf16[64,1536]{1,0:T(8,128)(2,1)S(1)} %sum2.1.own_ref.after_ref), channel_id=1, source_target_pairs={{0,2},{1,3},{2,0},{3,1},{4,6},{5,7},{6,4},{7,5},{8,10},{9,11},{10,... | collective-permute-start | bytes 589832 | tf_op jit(solution)/shard_map/ppermute | solution.py:448
  76.3 9.1 %collective-permute-start.1 = (bf16[64,1536]{1,0:T(8,128)(2,1)S(1)}, bf16[64,1536]{1,0:T(8,128)(2,1)S(1)}, u32[]{:S(2)}, u32[]{:S(2)}) collective-permute-start(bf16[64,1536]{1,0:T(8,128)(2,1)S(1)} %sum2.1.own_ref.after_ref), channel_id=1, source_target_pairs={{0,3},{1,0},{2,1},{3,2},{4,7},{5,4},{6,5},{7,6},{8,11},{9,8},{10,9... | collective-permute-start | bytes 589832 | tf_op jit(solution)/shard_map/ppermute | solution.py:448
  78.4 8.6 %collective-permute-start.3 = (bf16[64,1536]{1,0:T(8,128)(2,1)S(1)}, bf16[64,1536]{1,0:T(8,128)(2,1)S(1)}, u32[]{:S(2)}, u32[]{:S(2)}) collective-permute-start(bf16[64,1536]{1,0:T(8,128)(2,1)S(1)} %sum2.1.own_ref.after_ref), channel_id=1, source_target_pairs={{0,1},{1,2},{2,3},{3,0},{4,5},{5,6},{6,7},{7,4},{8,9},{9,10},{10,1... | collective-permute-start | bytes 589832 | tf_op jit(solution)/shard_map/ppermute | solution.py:448
  80.4 6.5 %copy-start.1 = (bf16[4,384,768]{2,1,0:T(8,128)(2,1)S(1)}, bf16[4,384,768]{2,1,0:T(8,128)(2,1)}, u32[]{:S(2)}) copy-start(bf16[4,384,768]{2,1,0:T(8,128)(2,1)} %update_ref.1) | copy-start | bytes 7077892
  80.4 6.5 %copy-start.4 = (s32[4,768]{1,0:T(4,128)S(1)}, s32[4,768]{1,0:T(4,128)}, u32[]{:S(2)}) copy-start(s32[4,768]{1,0:T(4,128)} %rows_ref.5) | copy-start | bytes 36868
  80.4 6.5 %copy-start.9 = (s32[4]{0:T(128)S(1)}, s32[4]{0:T(128)}, u32[]{:S(2)}) copy-start(s32[4]{0:T(128)} %parent_vmem.3) | copy-start | bytes 52
  86.9 23.8 %copy-start = (bf16[2,2048,512]{2,1,0:T(8,128)(2,1)S(1)}, bf16[2,2048,512]{2,1,0:T(8,128)(2,1)}, u32[]{:S(2)}) copy-start(bf16[2,2048,512]{2,1,0:T(8,128)(2,1)} %inverse_ref.7) | copy-start | bytes 12582916
  104.0 6.7 %collective-permute-start.5 = (bf16[64,1024]{1,0:T(8,128)(2,1)S(1)}, bf16[64,1024]{1,0:T(8,128)(2,1)S(1)}, u32[]{:S(2)}, u32[]{:S(2)}) collective-permute-start(bf16[64,1024]{1,0:T(8,128)(2,1)S(1)} %sum3.1.own_ref), channel_id=1, source_target_pairs={{0,2},{1,3},{2,0},{3,1},{4,6},{5,7},{6,4},{7,5},{8,10},{9,11},{10,... | collective-permute-start | bytes 393224 | tf_op jit(solution)/shard_map/ppermute | solution.py:448
  105.0 5.7 %collective-permute-start.4 = (bf16[64,1024]{1,0:T(8,128)(2,1)S(1)}, bf16[64,1024]{1,0:T(8,128)(2,1)S(1)}, u32[]{:S(2)}, u32[]{:S(2)}) collective-permute-start(bf16[64,1024]{1,0:T(8,128)(2,1)S(1)} %sum3.1.own_ref), channel_id=1, source_target_pairs={{0,3},{1,0},{2,1},{3,2},{4,7},{5,4},{6,5},{7,6},{8,11},{9,8},{10,9... | collective-permute-start | bytes 393224 | tf_op jit(solution)/shard_map/ppermute | solution.py:448
  107.1 6.2 %collective-permute-start.6 = (bf16[64,1024]{1,0:T(8,128)(2,1)S(1)}, bf16[64,1024]{1,0:T(8,128)(2,1)S(1)}, u32[]{:S(2)}, u32[]{:S(2)}) collective-permute-start(bf16[64,1024]{1,0:T(8,128)(2,1)S(1)} %sum3.1.own_ref), channel_id=1, source_target_pairs={{0,1},{1,2},{2,3},{3,0},{4,5},{5,6},{6,7},{7,4},{8,9},{9,10},{10,1... | collective-permute-start | bytes 393224 | tf_op jit(solution)/shard_map/ppermute | solution.py:448

commit v8 on v7

--- a/solution.py
+++ b/solution.py
@@ -166,8 +166,12 @@
     lax.fori_loop(first // LANES, last // LANES, gather, 0)
 
 
-def rhs_kernel(first, last, slot_ref, both_ref, after_ref, rhs_ref, tall):
+def rhs_kernel(first, last, slot_vmem, both_ref, after_ref, rhs_ref, tall, slot_ref, sem):
     del after_ref
+    part = slice(first // LANES // 8 * 8, last // LANES)
+    load = pltpu.make_async_copy(slot_vmem.at[part], slot_ref.at[part], sem)
+    load.start()
+    load.wait()
     restore(first, last, slot_ref, both_ref, tall)
     rhs_ref[...] = tall[...].T[:RHS]
 
@@ -175,10 +179,14 @@
 def late_rhs(first, last, slot, both, after):
     return pl.pallas_call(
         functools.partial(rhs_kernel, first, last),
-        in_specs=[SMEM, VMEM, VMEM],
+        in_specs=[VMEM, VMEM, VMEM],
         out_specs=VMEM,
         out_shape=struct((RHS, last - first), f32),
-        scratch_shapes=[pltpu.VMEM((last - first, 128), f32)],
+        scratch_shapes=[
+            pltpu.VMEM((last - first, 128), f32),
+            pltpu.SMEM((BLOCKS, LANES), i32),
+            pltpu.SemaphoreType.DMA,
+        ],
         compiler_params=params(4),
         name="rhs",
     )(slot, both, after)

time: 115 us -> 114 us (level)
  transfers between devices with their start and end apart: 8 -> 8, of which waited for: 6 -> 6; matrix products, arithmetic and copies ran while one was open for 0% -> 0% of each run, Pallas kernels for 6% -> 5%
where the time goes in v8:
time: 114 us
  blocking collectives  47.1 us (41%)
  Pallas kernels  28.1 us (25%)
  waiting for transfers between devices  18.5 us (16%)
  starting transfers between devices  17.8 us (16%)
  local copies, waits for them, and re-layouts  2.25 us (2%)
    all_to_all x3, blocking collectives, exchange(): return lax.all_to_all(block, axes, split_axis=0, concat_axis=0, tiled=True)  47.1 us
    ppermute x6, waiting for transfers between devices, front_pieces(): lax.ppermute(side, 'front', [(f, (f + k) % FRONT) for f in range(FRONT)])  11.7 us
    all_to_all x1, starting transfers between devices, exchange(): return lax.all_to_all(block, axes, split_axis=0, concat_axis=0, tiled=True)  11.1 us
    pallas_call x1, Pallas kernels, per_device(): pl.pallas_call(pick_kernel, in_specs=[VMEM, VMEM], out_specs=HBM, out_sha...  7.08 us
    all_to_all x1, waiting for transfers between devices, exchange(): return lax.all_to_all(block, axes, split_axis=0, concat_axis=0, tiled=True)  6.84 us
    ppermute x6, starting transfers between devices, front_pieces(): lax.ppermute(side, 'front', [(f, (f + k) % FRONT) for f in range(FRONT)])  6.46 us
    pallas_call x1, Pallas kernels, per_device(): pl.pallas_call(leaf_kernel, in_specs=[SMEM, SMEM, VMEM, VMEM, HBM, HBM, H...  6.08 us
    pallas_call x2, Pallas kernels, late_rhs(): pl.pallas_call(functools.partial(rhs_kernel, first, last), in_specs=[VMEM...  3.83 us
  transfers between devices with their start and end apart: 8, of which 6 were waited for; matrix products, arithmetic and copies ran while one was open for 0% of the time, Pallas kernels for 5%

profile of v8, /device:TPU:0, one launch (start us, length us, event | category | flops | bytes accessed | tf_op | source)
XLA Modules:
  0.0 113.9 jit_solution(7676899007581314012)
XLA Ops:
  0.0 0.7 copy-done.3
  0.7 2.4 %rank.1 = (s32[128,128]{1,0:T(8,128)}, s32[52,128]{1,0:T(8,128)S(1)}) custom-call(s32[52,128]{1,0:T(8,128)S(1)} %bitcast.11), custom_call_target="tpu_custom_call" | custom-call | tf_op jit(solution)/shard_map/rank/pallas_call | solution.py:482
  3.2 11.1 %all-to-all-start = ((s32[128,1,128]{2,1,0:T(1,128)}), s32[128,1,128]{2,1,0:T(1,128)S(1)}, u32[]{:S(2)}, u32[]{:S(2)}) async-start(s32[128,1,128]{2,1,0:T(1,128)} %bitcast.2), calls=%async_computation | async-start | bytes 131072 | tf_op jit(solution)/shard_map/all_to_all | solution.py:462
  14.4 1.4 %copy-done.2 = f32[64,6656]{1,0:T(8,128)S(1)} copy-done((f32[64,6656]{1,0:T(8,128)S(1)}, f32[64,6656]{1,0:T(8,128)}, u32[]{:S(2)}) %copy-start.2) | copy-done | bytes 1703960
  15.8 0.9 tall.1.tall_ref
  16.7 6.8 %all-to-all-done = s32[128,1,128]{2,1,0:T(1,128)S(1)} async-done(((s32[128,1,128]{2,1,0:T(1,128)}), s32[128,1,128]{2,1,0:T(1,128)S(1)}, u32[]{:S(2)}, u32[]{:S(2)}) %all-to-all-start) | async-done | bytes 65568 | tf_op jit(solution)/shard_map/all_to_all | solution.py:462
  23.6 7.1 %pick.1 = bf16[3328,128]{1,0:T(8,128)(2,1)} custom-call(s32[128,128]{1,0:T(8,128)S(1)} %bitcast.10, f32[6656,128]{1,0:T(8,128)S(1)} %tall.1.tall_ref), custom_call_target="tpu_custom_call" | custom-call | tf_op jit(solution)/shard_map/pick/pallas_call | solution.py:499
  30.7 21.6 %all_to_all.20 = bf16[128,13,2,128]{3,2,1,0:T(2,128)(2,1)S(1)} all-to-all(bf16[128,13,2,128]{3,2,1,0:T(2,128)(2,1)} %bitcast.12), channel_id=1, replica_groups=mesh['z'=4,'x1'=2,'x0'=2,'core'=2,'front'=4] {'z','x1','x0','core','front'}, dimensions={0} | all-to-all | bytes 1703936 | tf_op jit(solution)/shard_map/all_to_all | solution.py:462
  52.2 6.1 %leaf.1 = (f32[64,6656]{1,0:T(8,128)}, bf16[2,72,256]{2,1,0:T(8,128)(2,1)S(1)}, f32[2,64,1024]{2,1,0:T(8,128)S(1)}, f32[6656,128]{1,0:T(8,128)S(1)}, bf16[2,1024...) custom-call(s32[52,128]{1,0:T(8,128)S(1)} %get-tuple-element.17.slot_ref.slot_vmem, s32[4]{0:T(128)S(1)} %copy-done.8, ...), custom_call_target="tpu_custom_call" | custom-call | tf_op jit(solution)/shard_map/leaf/pallas_call | solution.py:514
  58.3 0.0 copy-start.5
  58.3 0.2 collective-permute-start
  58.5 2.2 %rhs.2.after_ref.rhs_ref = f32[64,1536]{1,0:T(8,128)S(1)} custom-call(s32[52,128]{1,0:T(8,128)S(1)} %get-tuple-element.17.slot_ref.slot_vmem, f32[6656,128]{1,0:T(8,128)S(1)} %get-tuple-element.23.both_ref, bf16[2,72,256]{2,1,0:T(8,128)(2,1)S(1)} %get-tuple-element.19.after_ref), custom_call_target="tpu_custom_call" | custom-call | tf_op jit(solution)/shard_map/rhs/pallas_call | solution.py:180
  60.7 0.0 slice-start
  60.8 2.3 %level1.1 = (f32[64,6656]{1,0:T(8,128)}, bf16[8,2,72,128]{3,2,1,0:T(8,128)(2,1)S(1)}) custom-call(s32[2]{0:T(128)S(1)} %copy-done.7, bf16[2,72,256]{2,1,0:T(8,128)(2,1)S(1)} %collective-permute-done.got_ref, f32[2,64,1024]{2,1,0:T(8,128)S(1)} %get-tuple-element.20.rhs_ref, s32[2,512]{1,0:T(2,128)S(1)} %copy-done.5, ...), custom_call_target="tpu_custom_call", output_to_operand_aliasing={{0}: (7, {})} | custom-call | tf_op jit(solution)/shard_map/level1/pallas_call | solution.py:549
  63.0 11.1 %all_to_all.21.got_ref = bf16[8,2,72,128]{3,2,1,0:T(8,128)(2,1)S(1)} all-to-all(bf16[8,2,72,128]{3,2,1,0:T(8,128)(2,1)S(1)} %get-tuple-element.25), channel_id=1, replica_groups=mesh['z'=4,'x1'=2,'x0'=2,'core'=2,'front'=4] {'x0','front'}, dimensions={0} | all-to-all | bytes 589824 | tf_op jit(solution)/shard_map/all_to_all | solution.py:462
  74.1 0.6 sum2.1.own_ref.after_ref
  74.7 1.2 %collective-permute-start.2 = (bf16[64,1536]{1,0:T(8,128)(2,1)S(1)}, bf16[64,1536]{1,0:T(8,128)(2,1)S(1)}, u32[]{:S(2)}, u32[]{:S(2)}) collective-permute-start(bf16[64,1536]{1,0:T(8,128)(2,1)S(1)} %sum2.1.own_ref.after_ref), channel_id=1, source_target_pairs={{0,2},{1,3},{2,0},{3,1},{4,6},{5,7},{6,4},{7,5},{8,10},{9,11},{10,... | collective-permute-start | bytes 589832 | tf_op jit(solution)/shard_map/ppermute | solution.py:456
  75.9 2.1 %collective-permute-start.1 = (bf16[64,1536]{1,0:T(8,128)(2,1)S(1)}, bf16[64,1536]{1,0:T(8,128)(2,1)S(1)}, u32[]{:S(2)}, u32[]{:S(2)}) collective-permute-start(bf16[64,1536]{1,0:T(8,128)(2,1)S(1)} %sum2.1.own_ref.after_ref), channel_id=1, source_target_pairs={{0,3},{1,0},{2,1},{3,2},{4,7},{5,4},{6,5},{7,6},{8,11},{9,8},{10,9... | collective-permute-start | bytes 589832 | tf_op jit(solution)/shard_map/ppermute | solution.py:456
  78.1 1.7 %rhs.3.after_ref.rhs_ref = f32[64,1024]{1,0:T(8,128)S(1)} custom-call(s32[52,128]{1,0:T(8,128)S(1)} %get-tuple-element.17.slot_ref.slot_vmem, f32[6656,128]{1,0:T(8,128)S(1)} %get-tuple-element.23.both_ref, bf16[64,1536]{1,0:T(8,128)(2,1)S(1)} %sum2.1.own_ref.after_ref), custom_call_target="tpu_custom_call" | custom-call | tf_op jit(solution)/shard_map/rhs/pallas_call | solution.py:180
  79.8 4.4 %collective-permute-done.2.second_ref = bf16[64,1536]{1,0:T(8,128)(2,1)S(1)} collective-permute-done((bf16[64,1536]{1,0:T(8,128)(2,1)S(1)}, bf16[64,1536]{1,0:T(8,128)(2,1)S(1)}, u32[]{:S(2)}, u32[]{:S(2)}) %collective-permute-start.2) | collective-permute-done | bytes 196640 | tf_op jit(solution)/shard_map/ppermute | solution.py:456
  84.1 0.9 collective-permute-done.1.third_ref
  85.1 0.7 part.2.part_ref
  85.8 0.9 collective-permute-done.3.first_ref
  86.7 2.1 %level2.1 = (f32[64,6656]{1,0:T(8,128)}, bf16[8,3,72,128]{3,2,1,0:T(8,128)(2,1)S(1)}) custom-call(s32[4]{0:T(128)S(1)} %copy-done.9, f32[64,1536]{1,0:T(8,128)S(1)} %part.2.part_ref, bf16[64,1536]{1,0:T(8,128)(2,1)S(1)} %collective-permute-done.3.first_ref, s32[4,768]{1,0:T(4,128)S(1)} %copy-done.4, ...), custom_call_target="tpu_custom_call", output_to_operand_aliasing={{0}: (7, {})} | custom-call | tf_op jit(solution)/shard_map/level2/pallas_call | solution.py:586
  88.8 14.5 %all_to_all.22.got_ref = bf16[8,3,72,128]{3,2,1,0:T(8,128)(2,1)S(1)} all-to-all(bf16[8,3,72,128]{3,2,1,0:T(8,128)(2,1)S(1)} %get-tuple-element.27), channel_id=1, replica_groups=mesh['z'=4,'x1'=2,'x0'=2,'core'=2,'front'=4] {'x1','front'}, dimensions={0} | all-to-all | bytes 884736 | tf_op jit(solution)/shard_map/all_to_all | solution.py:462
  103.2 0.4 sum3.1.own_ref
  103.7 0.9 collective-permute-start.5
  104.6 2.2 %collective-permute-start.4 = (bf16[64,1024]{1,0:T(8,128)(2,1)S(1)}, bf16[64,1024]{1,0:T(8,128)(2,1)S(1)}, u32[]{:S(2)}, u32[]{:S(2)}) collective-permute-start(bf16[64,1024]{1,0:T(8,128)(2,1)S(1)} %sum3.1.own_ref), channel_id=1, source_target_pairs={{0,3},{1,0},{2,1},{3,2},{4,7},{5,4},{6,5},{7,6},{8,11},{9,8},{10,9... | collective-permute-start | bytes 393224 | tf_op jit(solution)/shard_map/ppermute | solution.py:456
  106.8 3.5 %collective-permute-done.5.second_ref = bf16[64,1024]{1,0:T(8,128)(2,1)S(1)} collective-permute-done((bf16[64,1024]{1,0:T(8,128)(2,1)S(1)}, bf16[64,1024]{1,0:T(8,128)(2,1)S(1)}, u32[]{:S(2)}, u32[]{:S(2)}) %collective-permute-start.5) | collective-permute-done | bytes 131104 | tf_op jit(solution)/shard_map/ppermute | solution.py:456
  110.3 0.7 part.3.part_ref
  111.0 2.0 %collective-permute-done.6.first_ref = bf16[64,1024]{1,0:T(8,128)(2,1)S(1)} collective-permute-done((bf16[64,1024]{1,0:T(8,128)(2,1)S(1)}, bf16[64,1024]{1,0:T(8,128)(2,1)S(1)}, u32[]{:S(2)}, u32[]{:S(2)}) %collective-permute-start.6) | collective-permute-done | bytes 131104 | tf_op jit(solution)/shard_map/ppermute | solution.py:456
  113.0 1.0 level3.1
  (25 shorter events, 0.1 us)
Async XLA Ops:
  0.0 0.7 copy-start.3
  3.2 20.4 %all-to-all-start = ((s32[128,1,128]{2,1,0:T(1,128)}), s32[128,1,128]{2,1,0:T(1,128)S(1)}, u32[]{:S(2)}, u32[]{:S(2)}) async-start(s32[128,1,128]{2,1,0:T(1,128)} %bitcast.2), calls=%async_computation | async-start | bytes 131072 | tf_op jit(solution)/shard_map/all_to_all | solution.py:462
  14.3 1.5 %copy-start.2 = (f32[64,6656]{1,0:T(8,128)S(1)}, f32[64,6656]{1,0:T(8,128)}, u32[]{:S(2)}) copy-start(f32[64,6656]{1,0:T(8,128)} %wide_ref.1) | copy-start | bytes 5111812
  23.6 28.6 %copy-start.6 = (s32[4,256]{1,0:T(4,128)S(1)}, s32[4,256]{1,0:T(4,128)}, u32[]{:S(2)}) copy-start(s32[4,256]{1,0:T(4,128)} %rows_ref.3) | copy-start | bytes 12292
  23.6 28.6 %copy-start.8 = (s32[4]{0:T(128)S(1)}, s32[4]{0:T(128)}, u32[]{:S(2)}) copy-start(s32[4]{0:T(128)} %parent_ref.1) | copy-start | bytes 52
  58.3 2.4 %copy-start.5 = (s32[2,512]{1,0:T(2,128)S(1)}, s32[2,512]{1,0:T(2,128)}, u32[]{:S(2)}) copy-start(s32[2,512]{1,0:T(2,128)} %rows_ref.4) | copy-start | bytes 12292
  58.3 2.4 %copy-start.7 = (s32[2]{0:T(128)S(1)}, s32[2]{0:T(128)}, u32[]{:S(2)}) copy-start(s32[2]{0:T(128)} %parent_vmem.2) | copy-start | bytes 28
  58.3 2.4 %collective-permute-start = (bf16[2,72,256]{2,1,0:T(8,128)(2,1)S(1)}, bf16[2,72,256]{2,1,0:T(8,128)(2,1)S(1)}, u32[]{:S(2)}, u32[]{:S(2)}) collective-permute-start(bf16[2,72,256]{2,1,0:T(8,128)(2,1)S(1)} %get-tuple-element.19.after_ref), channel_id=1, source_target_pairs={{0,4},{4,0},{1,5},{5,1},{2,6},{6,2},{3,7},{7,3},{8,12},{12,8},{9,1... | collective-permute-start | bytes 221192 | tf_op jit(solution)/shard_map/ppermute | solution.py:547
  60.7 24.4 %slice-start = ((s8[4718592]{0:T(1024)(128)(4,1)}), s8[4194304]{0:T(1024)(128)(4,1)S(1)}, s32[]{:S(2)}) async-start(s8[4718592]{0:T(1024)(128)(4,1)} %bitcast.7), calls=%async_computation.4 | async-start | bytes 8388608
  60.7 24.3 %slice-start.1 = ((s8[4718592]{0:T(1024)(128)(4,1)}), s8[524288]{0:T(1024)(128)(4,1)S(1)}, s32[]{:S(2)}) async-start(s8[4718592]{0:T(1024)(128)(4,1)} %bitcast.7), calls=%async_computation.5 | async-start | bytes 1048576
  74.7 9.4 %collective-permute-start.2 = (bf16[64,1536]{1,0:T(8,128)(2,1)S(1)}, bf16[64,1536]{1,0:T(8,128)(2,1)S(1)}, u32[]{:S(2)}, u32[]{:S(2)}) collective-permute-start(bf16[64,1536]{1,0:T(8,128)(2,1)S(1)} %sum2.1.own_ref.after_ref), channel_id=1, source_target_pairs={{0,2},{1,3},{2,0},{3,1},{4,6},{5,7},{6,4},{7,5},{8,10},{9,11},{10,... | collective-permute-start | bytes 589832 | tf_op jit(solution)/shard_map/ppermute | solution.py:456
  75.9 9.1 %collective-permute-start.1 = (bf16[64,1536]{1,0:T(8,128)(2,1)S(1)}, bf16[64,1536]{1,0:T(8,128)(2,1)S(1)}, u32[]{:S(2)}, u32[]{:S(2)}) collective-permute-start(bf16[64,1536]{1,0:T(8,128)(2,1)S(1)} %sum2.1.own_ref.after_ref), channel_id=1, source_target_pairs={{0,3},{1,0},{2,1},{3,2},{4,7},{5,4},{6,5},{7,6},{8,11},{9,8},{10,9... | collective-permute-start | bytes 589832 | tf_op jit(solution)/shard_map/ppermute | solution.py:456
  78.0 8.6 %collective-permute-start.3 = (bf16[64,1536]{1,0:T(8,128)(2,1)S(1)}, bf16[64,1536]{1,0:T(8,128)(2,1)S(1)}, u32[]{:S(2)}, u32[]{:S(2)}) collective-permute-start(bf16[64,1536]{1,0:T(8,128)(2,1)S(1)} %sum2.1.own_ref.after_ref), channel_id=1, source_target_pairs={{0,1},{1,2},{2,3},{3,0},{4,5},{5,6},{6,7},{7,4},{8,9},{9,10},{10,1... | collective-permute-start | bytes 589832 | tf_op jit(solution)/shard_map/ppermute | solution.py:456
  79.7 6.9 %copy-start.1 = (bf16[4,384,768]{2,1,0:T(8,128)(2,1)S(1)}, bf16[4,384,768]{2,1,0:T(8,128)(2,1)}, u32[]{:S(2)}) copy-start(bf16[4,384,768]{2,1,0:T(8,128)(2,1)} %update_ref.1) | copy-start | bytes 7077892
  79.7 6.9 %copy-start.4 = (s32[4,768]{1,0:T(4,128)S(1)}, s32[4,768]{1,0:T(4,128)}, u32[]{:S(2)}) copy-start(s32[4,768]{1,0:T(4,128)} %rows_ref.5) | copy-start | bytes 36868
  79.8 6.9 %copy-start.9 = (s32[4]{0:T(128)S(1)}, s32[4]{0:T(128)}, u32[]{:S(2)}) copy-start(s32[4]{0:T(128)} %parent_vmem.3) | copy-start | bytes 52
  86.7 23.7 %copy-start = (bf16[2,2048,512]{2,1,0:T(8,128)(2,1)S(1)}, bf16[2,2048,512]{2,1,0:T(8,128)(2,1)}, u32[]{:S(2)}) copy-start(bf16[2,2048,512]{2,1,0:T(8,128)(2,1)} %inverse_ref.7) | copy-start | bytes 12582916
  103.7 6.7 %collective-permute-start.5 = (bf16[64,1024]{1,0:T(8,128)(2,1)S(1)}, bf16[64,1024]{1,0:T(8,128)(2,1)S(1)}, u32[]{:S(2)}, u32[]{:S(2)}) collective-permute-start(bf16[64,1024]{1,0:T(8,128)(2,1)S(1)} %sum3.1.own_ref), channel_id=1, source_target_pairs={{0,2},{1,3},{2,0},{3,1},{4,6},{5,7},{6,4},{7,5},{8,10},{9,11},{10,... | collective-permute-start | bytes 393224 | tf_op jit(solution)/shard_map/ppermute | solution.py:456
  104.6 5.7 %collective-permute-start.4 = (bf16[64,1024]{1,0:T(8,128)(2,1)S(1)}, bf16[64,1024]{1,0:T(8,128)(2,1)S(1)}, u32[]{:S(2)}, u32[]{:S(2)}) collective-permute-start(bf16[64,1024]{1,0:T(8,128)(2,1)S(1)} %sum3.1.own_ref), channel_id=1, source_target_pairs={{0,3},{1,0},{2,1},{3,2},{4,7},{5,4},{6,5},{7,6},{8,11},{9,8},{10,9... | collective-permute-start | bytes 393224 | tf_op jit(solution)/shard_map/ppermute | solution.py:456
  106.8 6.2 %collective-permute-start.6 = (bf16[64,1024]{1,0:T(8,128)(2,1)S(1)}, bf16[64,1024]{1,0:T(8,128)(2,1)S(1)}, u32[]{:S(2)}, u32[]{:S(2)}) collective-permute-start(bf16[64,1024]{1,0:T(8,128)(2,1)S(1)} %sum3.1.own_ref), channel_id=1, source_target_pairs={{0,1},{1,2},{2,3},{3,0},{4,5},{5,6},{6,7},{7,4},{8,9},{9,10},{10,1... | collective-permute-start | bytes 393224 | tf_op jit(solution)/shard_map/ppermute | solution.py:456
